TPU v7x, 256 devices: a whole 4x4x8 slice. The times are simulated.
256 devices in a mesh: prow: 8 (over z), pcol: 32 (over x, y, core).
Axes of the slice: x: 4, y: 4, z: 8, core: 2. Of those that a mesh axis runs over, the one named last changes fastest.
Arguments:
- kernel: float32 [8, 8, 256, 2, 32, 256], P(None, 'prow', None, None, 'pcol'), may hold values from 0 to 1.5, as said below
- pivots: int32 [2], replicated, may hold values from 0 to 63, as said below
Outputs:
- panels: float32 [2, 8, 8, 256, 256], P(None, None, 'prow')
- trailing: float32 [8, 8, 256, 2, 32, 256], P(None, 'prow', None, None, 'pcol')
Inputs may be any that keep to these rules, and one draw needn't show every extreme that they name: `kernel`: symmetric; a positive semidefinite matrix plus 0.5 times the identity. `pivots`: two different block numbers; one of them is the newest block, 63, in either position.
All inputs are finite; a program needn't handle non-finite values.
Results may differ from a plain program's by a relative error of at most 0.0003.
Values sent between devices are 32-bit elements; how exact they have to be, the bound alone decides.
No kernel may reach another device: no remote copies, remote signals or barrier semaphores. Data moves between devices by JAX's collectives and lax.ppermute only.
A program may use at most 64 MiB of HBM per device.

v0:
```python
import jax
import jax.numpy as jnp
from jax import lax
from jax.experimental import pallas as pl
from jax.experimental.pallas import tpu as pltpu
from jax.sharding import PartitionSpec as P

BASE = 64
GROUP = 8


def split(v):
    high = v.astype(jnp.bfloat16)
    low = (v - high.astype(jnp.float32)).astype(jnp.bfloat16)
    return high, low


def dot3(a, b, dims=((1,), (0,))):
    (ah, al), (bh, bl) = a, b
    f = lambda u, v: lax.dot_general(u, v, (dims, ((), ())), preferred_element_type=jnp.float32)
    return f(ah, bh) + (f(ah, bl) + f(al, bh))


def stack(b):
    return jnp.concatenate([b[0], b[1], b[0]], axis=0)


def stacked(a, b):
    high, low = split(a)
    return jnp.dot(jnp.concatenate([high, high, low], axis=1), b, preferred_element_type=jnp.float32)


def product(a, b, dims=((1,), (0,))):
    return dot3(split(a), split(b), dims)


def factor_group(scalars):
    n = GROUP
    g = [row[:] for row in scalars]
    unit = [[None] * n for _ in range(n)]
    pivots = []
    inverses = []
    for q in range(n):
        d = g[q][q]
        inv = 1.0 / d
        pivots.append(d)
        inverses.append(inv)
        for i in range(q + 1, n):
            unit[i][q] = g[i][q] * inv
        for i in range(q + 1, n):
            for k in range(q + 1, i + 1):
                g[i][k] = g[i][k] - unit[i][q] * g[k][q]
    w = [[None] * n for _ in range(n)]
    for q in range(n):
        for i in range(q + 1, n):
            acc = unit[i][q]
            for k in range(q + 1, i):
                acc = acc + unit[i][k] * w[k][q]
            w[i][q] = -acc
    return w, pivots, inverses


def base_inverse(s):
    lanes = 2 * BASE
    row = lax.broadcasted_iota(jnp.int32, (BASE, BASE), 0)
    col = lax.broadcasted_iota(jnp.int32, (BASE, BASE), 1)
    eye = jnp.where(row == col, 1.0, 0.0).astype(jnp.float32)
    table = jnp.concatenate([s, eye], axis=1)
    groups = [table[GROUP * h : GROUP * h + GROUP, :] for h in range(BASE // GROUP)]
    shape = (GROUP, lanes)
    sub = lax.broadcasted_iota(jnp.int32, shape, 0)
    spread = lambda v: jnp.broadcast_to(v, shape)
    done = []
    for g in range(BASE // GROUP):
        p = groups[g]
        start = GROUP * g
        cols = [spread(p[:, start + q : start + q + 1]) for q in range(GROUP)]
        scalars = [[spread(cols[q][i : i + 1, :]) if i >= q else None for q in range(GROUP)] for i in range(GROUP)]
        w, pivots, inverses = factor_group(scalars)
        rows = [spread(p[q : q + 1, :]) for q in range(GROUP)]
        reduced = []
        for i in range(GROUP):
            acc = rows[i]
            for q in range(i):
                acc = acc + w[i][q] * rows[q]
            reduced.append(acc)
        for h in range(g + 1, BASE // GROUP):
            t = groups[h]
            cb = [spread(t[:, start + q : start + q + 1]) for q in range(GROUP)]
            for q in range(GROUP):
                v = cb[q]
                for k in range(q):
                    v = v + w[q][k] * cb[k]
                t = t - (v * inverses[q]) * reduced[q]
            groups[h] = t
        out = jnp.zeros(shape, jnp.float32)
        for q in range(GROUP):
            out = jnp.where(sub == q, reduced[q] * lax.rsqrt(pivots[q]), out)
        done.append(out)
    return jnp.concatenate(done, axis=0)[:, BASE:]


def pair_inverse(s):
    top = base_inverse(s[:BASE, :BASE])
    below = product(s[BASE:, :BASE], top, ((1,), (1,)))
    rest = s[BASE:, BASE:] - product(below, below, ((1,), (1,)))
    carried = product(below, top)
    bottom = base_inverse(rest)
    corner = -product(bottom, carried)
    return jnp.concatenate(
        [jnp.concatenate([top, jnp.zeros_like(top)], axis=1), jnp.concatenate([corner, bottom], axis=1)], axis=0
    )


def factor_inverse(s_ref, z_ref, m_ref):
    n = s_ref.shape[0]
    size = 2 * BASE
    row = lax.broadcasted_iota(jnp.int32, (n, n), 0)
    col = lax.broadcasted_iota(jnp.int32, (n, n), 1)
    z_ref[...] = jnp.where(row == col, 1.0, 0.0).astype(jnp.float32)

    def step(k, carry):
        here = pl.ds(pl.multiple_of(k * size, size), size)
        inverse = split(pair_inverse(s_ref[here, here]))
        us = split(dot3(inverse, split(s_ref[here, :])))
        uz = dot3(inverse, split(z_ref[here, :]))
        m_ref[here, :] = uz
        uz = split(uz)
        s_ref[...] -= dot3(us, us, ((0,), (0,)))
        z_ref[...] -= dot3(us, uz, ((0,), (0,)))
        return carry

    lax.fori_loop(0, n // size, step, 0)


AXES = ("prow", "pcol")
NB = 256
NEWEST = 63
PLANES = 8
CHUNK = 2 * NB // PLANES
HALF = CHUNK // 2
LANES = 128
VMEM = pl.BlockSpec(memory_space=pltpu.VMEM)
SMEM = pl.BlockSpec(memory_space=pltpu.SMEM)
ROW, COLUMN, ROOT, HELD, FLIPPED, FIRST, SECOND = range(7)
PARAMS = pltpu.CompilerParams(vmem_limit_bytes=48 * 1024 * 1024)


def chunk_of(info, plane):
    return plane // 2 + PLANES // 2 * ((plane + info[ROOT]) % 2)


def place_of(info, plane):
    return (chunk_of(info, plane) + PLANES // 2 * info[FLIPPED]) % PLANES


def block_column(ref, t, rows):
    return jnp.concatenate([ref[pl.ds(2 * t + j, rows, stride=4), :] for j in range(2)], axis=1)


def pick_kernel(info, piece_ref, both_ref):
    both_ref[:, :NB] = block_column(piece_ref, info[HELD], CHUNK)
    both_ref[:, NB:] = block_column(piece_ref, 1, CHUNK)


def pick(info, piece):
    return pl.pallas_call(
        pick_kernel,
        out_shape=jax.ShapeDtypeStruct((CHUNK, 2 * NB), jnp.float32),
        in_specs=[SMEM, VMEM],
        out_specs=VMEM,
        compiler_params=PARAMS,
        name="pick",
    )(info, piece)


def factor_kernel(info, own_ref, twin_ref, x_ref, w_ref, c_ref, s_ref, z_ref, m_ref):
    flip = info[FLIPPED] == 1
    core = info[COLUMN] % 2
    for slot in range(PLANES):
        base = place_of(info, (info[ROW] + 1 + slot) % PLANES) * CHUNK
        for ref, side in ((own_ref, core), (twin_ref, 1 - core)):
            v = ref[slot]
            v = jnp.where(flip, jnp.concatenate([v[:, NB:], v[:, :NB]], axis=1), v)
            s_ref[pl.ds(pl.multiple_of(base + side * HALF, HALF), HALF), :] = v
    factor_inverse(s_ref, z_ref, m_ref)
    s_ref[...] = m_ref[...].T
    for plane in range(PLANES):
        start = pl.multiple_of(place_of(info, plane) * CHUNK, CHUNK)
        z_ref[plane * CHUNK : (plane + 1) * CHUNK, :] = s_ref[pl.ds(start, CHUNK), :]
    weights = split(z_ref[...])
    w_ref[...] = stack(weights)
    weights = weights[0].T, weights[1].T
    for column in range(2):
        x = jnp.concatenate([block_column(x_ref.at[plane], column, CHUNK) for plane in range(PLANES)], axis=0)
        c_ref[:, column * NB : (column + 1) * NB] = stack(split(dot3(weights, split(x))))


def factor(info, own, twin, crossing):
    n = 2 * NB
    return pl.pallas_call(
        factor_kernel,
        out_shape=[jax.ShapeDtypeStruct((3 * n, n), jnp.bfloat16)] * 2,
        in_specs=[SMEM, VMEM, VMEM, VMEM],
        out_specs=[VMEM] * 2,
        scratch_shapes=[pltpu.VMEM((n, n), jnp.float32)] * 3,
        compiler_params=PARAMS,
        name="factor",
    )(info, own, twin, crossing)


def update_kernel(info, w_ref, c_ref, g_ref, a_ref, panels_ref, t_ref):
    group, t = pl.program_id(0), pl.program_id(1)
    block = (t * pl.num_programs(0) + group) * PLANES + info[ROW]
    columns = jnp.concatenate([block_column(g_ref.at[plane], t, CHUNK) for plane in range(PLANES)], axis=0)
    rows = stacked(columns.T, w_ref[...])
    first, second = info[FIRST], info[SECOND]
    panels_ref[0, 0] = rows[:, :NB]
    panels_ref[1, 0] = jnp.where(block != first, rows[:, NB:], 0.0)
    trail = stacked(rows, c_ref[...])
    row_kept = (block != first) & (block != second)
    for column in range(2):
        number = info[COLUMN] + 32 * column
        kept = row_kept & (number != first) & (number != second)
        for j in range(2):
            where = pl.ds(2 * column + j, NB, stride=4)
            start = column * NB + j * LANES
            t_ref[0, where, :] = jnp.where(kept, a_ref[0, where, :] - trail[:, start : start + LANES], 0.0)


def update(info, factors, gathered, flat):
    br, rows, _ = flat.shape
    groups = gathered.shape[0] // PLANES
    block = lambda k, t, info: (t * groups + k, 0, 0)
    return pl.pallas_call(
        update_kernel,
        grid_spec=pltpu.PrefetchScalarGridSpec(
            num_scalar_prefetch=1,
            grid=(groups, br // groups),
            in_specs=[VMEM] * 2
            + [
                pl.BlockSpec((PLANES, 4 * CHUNK, LANES), lambda k, t, info: (k, 0, 0)),
                pl.BlockSpec((1, rows, LANES), block),
            ],
            out_specs=[
                pl.BlockSpec((2, 1, NB, NB), lambda k, t, info: (0, t * groups + k, 0, 0)),
                pl.BlockSpec((1, rows, LANES), block),
            ],
        ),
        out_shape=[
            jax.ShapeDtypeStruct((2, br, NB, NB), jnp.float32),
            jax.ShapeDtypeStruct(flat.shape, jnp.float32),
        ],
        compiler_params=PARAMS,
        name="update",
    )(info, *factors, gathered, flat)


def shards(kernel, pivots):
    height, width = lax.axis_size("prow"), lax.axis_size("pcol")
    assert (height, width) == (PLANES, 32)
    br, bc = kernel.shape[0], kernel.shape[3]
    assert bc == 2
    flat = kernel.reshape(br, NB * bc * NB // LANES, LANES)
    r = lax.axis_index("prow")
    c = lax.axis_index("pcol")
    flipped = pivots[0] == NEWEST
    other = jnp.where(flipped, pivots[1], pivots[0])
    block_row, root_row = other >> 3, other & 7
    root_t, root_col = other >> 5, other & 31
    info = jnp.stack([r, c, root_row, root_t, flipped.astype(jnp.int32), pivots[0], pivots[1]])
    device = lambda row, column: row * width + column
    everyone = [(row, column) for row in range(height) for column in range(width)]
    send = lambda value, to: lax.ppermute(value, AXES, [(device(a, b), device(*to(a, b))) for a, b in everyone])
    up = lambda value, d: send(value, lambda a, b: ((a + d) % height, b))
    core_twin = lambda value: send(value, lambda a, b: (a, b ^ 1))

    piece_rows = 4 * CHUNK
    part = lambda rows, q: rows[q * piece_rows : (q + 1) * piece_rows]
    line = lambda start, end: [(device(start, k), device(end, k)) for k in range(width)]

    def scatter_from(root):
        parity, quarter = root % 2, root // 2
        away = 1 - parity

        def run(others, newest):
            arrived = []
            for q in range(4):
                plane = 2 * q + away
                if plane != height - 1:
                    arrived.append((plane, lax.ppermute(part(newest, q), AXES, line(height - 1, plane))))
                if q != quarter:
                    plane = 2 * q + parity
                    pairs = line(root, plane)
                    if quarter < 3:
                        pairs = line(2 * quarter, 2 * q) + line(2 * quarter + 1, 2 * q + 1)
                    arrived.append((plane, lax.ppermute(part(others, q), AXES, pairs)))
            arrived.append((root, part(others, quarter)))
            if away == 1:
                arrived.append((height - 1, part(newest, 3)))
            piece = arrived[0][1]
            for plane, value in arrived[1:]:
                piece = jnp.where(r == plane, value, piece)
            return piece

        return run

    others = lax.dynamic_slice(flat, (block_row, 0, 0), (1,) + flat.shape[1:])[0]
    piece = lax.switch(root_row, [scatter_from(root) for root in range(height)], others, flat[NEWEST // height])
    both = pick(info, piece)

    crossing = lax.all_gather(piece, "prow", axis=0, tiled=False)
    moved = send(piece, lambda a, b: (b % height, (b // height) * height + a))

    core, ypos, xpos = c & 1, (c >> 1) & 3, c >> 3
    rcore, ry, rx = root_col & 1, (root_col >> 1) & 3, root_col >> 3
    side = lax.broadcasted_iota(jnp.int32, (CHUNK, 2 * NB), 1) < NB
    both = jnp.where(jnp.where(side, core == rcore, core == 1), both, core_twin(both))
    mine = lax.dynamic_slice_in_dim(both, core * HALF, HALF, 0)
    side = side[:HALF]

    def spread(value, position, goal, last, shift):
        source = jnp.where(side, (position - goal) & 3, (position - last) & 3)
        out = value
        for d in range(1, 4):
            out = jnp.where(source == d, send(value, lambda a, b: (a, shift(b, d))), out)
        return out

    mine = spread(mine, xpos, rx, 3, lambda b, d: (b + 8 * d) % 32)
    moved, mine = lax.optimization_barrier((moved, mine))
    gathered = lax.all_gather(moved, "pcol", axis=0, tiled=False)
    mine = spread(mine, ypos, ry, 3, lambda b, d: (b // 8) * 8 + (b + 2 * d) % 8)
    ring = jnp.stack([up(mine, d) for d in range(height - 1, 0, -1)] + [mine])
    factors = factor(info, ring, core_twin(ring), crossing)
    panels, trailing = update(info, factors, gathered, flat)
    return panels.reshape(2, br, 1, NB, NB), trailing.reshape(kernel.shape)


def solution(mesh):
    in_specs = (P(None, "prow", None, None, "pcol", None), P())
    out_specs = (P(None, None, "prow", None, None), P(None, "prow", None, None, "pcol", None))
    return jax.shard_map(shards, mesh=mesh, in_specs=in_specs, out_specs=out_specs, check_vma=False)
```

profile of v0, /device:TPU:1, one launch (start us, length us, event | category | flops | bytes accessed | tf_op | source)
XLA Modules:
  0.0 152.8 jit_solution(6530990474620993040)
XLA Ops:
  7.2 1.3 fusion.17
  10.3 1.4 slice.222
  11.8 1.1 dynamic-slice_bitcast_fusion
  12.9 22.4 %conditional.1 = (f32[256,128]{1,0:T(8,128)S(1)}) conditional(s32[]{:T(128)} %clamp.3, (s32[]{:T(128)}, f32[1024,128]{1,0:T(8,128)S(1)}, f32[1024,128]{1,0:T(8,128)S(1)}) %tuple.89, (s32[]{:T(128)}, f32[1024,128]{1,0:T(8,128)S(1)}, f32[1024,128]{1,0:T(8,128)S(1)}) %tuple.93, (s32[]{:T(128)}, ...), branch_computations={%region_0.1_spmd, %region_1.2_spmd, %region_2.3_spmd, %region_3.4_... | conditional | flops 229383 | bytes 6685030 | solution.py:309
  12.9 0.7 collective-permute-start.5
  13.6 0.7 collective-permute-start.4
  14.3 0.7 collective-permute-start.2
  15.0 5.7 %collective-permute-start.3 = (f32[256,128]{1,0:T(8,128)S(1)}, f32[256,128]{1,0:T(8,128)S(1)}, u32[]{:S(2)}, u32[]{:S(2)}) collective-permute-start(f32[256,128]{1,0:T(8,128)S(1)} %get-tuple-element.100), channel_id=1, source_target_pairs={{0,64},{1,65},{2,66},{3,67},{4,68},{5,69},{6,70},{7,71},{8,72},{9,... | collective-permute-start | bytes 393224 | tf_op jit(solution)/shard_map/cond/branch_0_fun/ppermute | solution.py:297
  20.7 4.6 %collective-permute-start.1 = (f32[256,128]{1,0:T(8,128)S(1)}, f32[256,128]{1,0:T(8,128)S(1)}, u32[]{:S(2)}, u32[]{:S(2)}) collective-permute-start(f32[256,128]{1,0:T(8,128)S(1)} %get-tuple-element.101), channel_id=1, source_target_pairs={{0,128},{1,129},{2,130},{3,131},{4,132},{5,133},{6,134},{7,135},{8... | collective-permute-start | bytes 393224 | tf_op jit(solution)/shard_map/cond/branch_0_fun/ppermute | solution.py:297
  25.3 1.3 collective-permute-start
  26.7 2.1 %collective-permute-done.1 = f32[256,128]{1,0:T(8,128)S(1)} collective-permute-done((f32[256,128]{1,0:T(8,128)S(1)}, f32[256,128]{1,0:T(8,128)S(1)}, u32[]{:S(2)}, u32[]{:S(2)}) %collective-permute-start.1) | collective-permute-done | bytes 131104 | tf_op jit(solution)/shard_map/cond/branch_0_fun/ppermute | solution.py:297
  28.8 6.4 %collective-permute-done = f32[256,128]{1,0:T(8,128)S(1)} collective-permute-done((f32[256,128]{1,0:T(8,128)S(1)}, f32[256,128]{1,0:T(8,128)S(1)}, u32[]{:S(2)}, u32[]{:S(2)}) %collective-permute-start) | collective-permute-done | bytes 131104 | tf_op jit(solution)/shard_map/cond/branch_0_fun/ppermute | solution.py:297
  35.3 0.6 copy-done.5
  35.9 0.0 all-gather.7.cloned.1.call-start
  36.0 1.9 %collective-permute-start.52 = (f32[256,128]{1,0:T(8,128)}, f32[256,128]{1,0:T(8,128)S(1)}, u32[]{:S(2)}, u32[]{:S(2)}) collective-permute-start(f32[256,128]{1,0:T(8,128)} %copy-done.5), channel_id=1, source_target_pairs={{0,0},{1,32},{2,64},{3,96},{4,128},{5,160},{6,192},{7,224},{8,8},{... | collective-permute-start | bytes 393224 | tf_op jit(solution)/shard_map/ppermute | solution.py:274
  37.9 0.1 stack.54.info
  38.0 0.9 pick.1
  39.0 0.2 collective-permute-start.53
  39.2 1.2 collective-permute-done.53
  40.4 1.3 collective-permute-start.56
  41.7 2.5 %collective-permute-start.55 = (f32[32,512]{1,0:T(8,128)S(1)}, f32[32,512]{1,0:T(8,128)S(1)}, u32[]{:S(2)}, u32[]{:S(2)}) collective-permute-start(f32[32,512]{1,0:T(8,128)S(1)} %dynamic-slice_select_fusion), channel_id=1, source_target_pairs={{0,16},{1,17},{2,18},{3,19},{4,20},{5,21},{6,22},{7,23},{8,24},{9,... | collective-permute-start | bytes 196616 | tf_op jit(solution)/shard_map/ppermute | solution.py:274
  44.2 1.2 collective-permute-start.54
  45.3 2.3 %collective-permute-done.55 = f32[32,512]{1,0:T(8,128)S(1)} collective-permute-done((f32[32,512]{1,0:T(8,128)S(1)}, f32[32,512]{1,0:T(8,128)S(1)}, u32[]{:S(2)}, u32[]{:S(2)}) %collective-permute-start.55) | collective-permute-done | bytes 65568 | tf_op jit(solution)/shard_map/ppermute | solution.py:274
  47.7 0.6 copy-done.6
  48.4 2.4 %collective-permute-start.59 = (f32[32,512]{1,0:T(8,128)S(1)}, f32[32,512]{1,0:T(8,128)S(1)}, u32[]{:S(2)}, u32[]{:S(2)}) collective-permute-start(f32[32,512]{1,0:T(8,128)S(1)} %select_select_fusion.9), channel_id=1, source_target_pairs={{0,2},{1,3},{2,4},{3,5},{4,6},{5,7},{6,0},{7,1},{8,10},{9,11},{10,... | collective-permute-start | bytes 196616 | tf_op jit(solution)/shard_map/ppermute | solution.py:274
  50.8 6.0 %collective-permute-start.58 = (f32[32,512]{1,0:T(8,128)S(1)}, f32[32,512]{1,0:T(8,128)S(1)}, u32[]{:S(2)}, u32[]{:S(2)}) collective-permute-start(f32[32,512]{1,0:T(8,128)S(1)} %select_select_fusion.9), channel_id=1, source_target_pairs={{0,4},{1,5},{2,6},{3,7},{4,0},{5,1},{6,2},{7,3},{8,12},{9,13},{10,... | collective-permute-start | bytes 196616 | tf_op jit(solution)/shard_map/ppermute | solution.py:274
  56.8 0.6 collective-permute-start.57
  57.4 1.9 %collective-permute-done.58 = f32[32,512]{1,0:T(8,128)S(1)} collective-permute-done((f32[32,512]{1,0:T(8,128)S(1)}, f32[32,512]{1,0:T(8,128)S(1)}, u32[]{:S(2)}, u32[]{:S(2)}) %collective-permute-start.58) | collective-permute-done | bytes 65568 | tf_op jit(solution)/shard_map/ppermute | solution.py:274
  59.2 1.5 collective-permute-done.57
  60.7 0.1 collective-permute-start.60
  60.8 1.5 collective-permute-start.66
  62.3 3.0 %collective-permute-start.65 = (f32[32,512]{1,0:T(8,128)S(1)}, f32[32,512]{1,0:T(8,128)S(1)}, u32[]{:S(2)}, u32[]{:S(2)}) collective-permute-start(f32[32,512]{1,0:T(8,128)S(1)} %select_select_fusion.8), channel_id=1, source_target_pairs={{0,64},{1,65},{2,66},{3,67},{4,68},{5,69},{6,70},{7,71},{8,72},{9,... | collective-permute-start | bytes 196616 | tf_op jit(solution)/shard_map/ppermute | solution.py:274
  65.3 1.0 collective-permute-start.64
  66.3 3.4 %collective-permute-start.63 = (f32[32,512]{1,0:T(8,128)S(1)}, f32[32,512]{1,0:T(8,128)S(1)}, u32[]{:S(2)}, u32[]{:S(2)}) collective-permute-start(f32[32,512]{1,0:T(8,128)S(1)} %select_select_fusion.8), channel_id=1, source_target_pairs={{0,128},{1,129},{2,130},{3,131},{4,132},{5,133},{6,134},{7,135},{8... | collective-permute-start | bytes 196616 | tf_op jit(solution)/shard_map/ppermute | solution.py:274
  69.7 0.6 collective-permute-start.61
  70.3 5.9 %collective-permute-done.61 = f32[32,512]{1,0:T(8,128)S(1)} collective-permute-done((f32[32,512]{1,0:T(8,128)S(1)}, f32[32,512]{1,0:T(8,128)S(1)}, u32[]{:S(2)}, u32[]{:S(2)}) %collective-permute-start.61) | collective-permute-done | bytes 65568 | tf_op jit(solution)/shard_map/ppermute | solution.py:274
  76.3 0.6 collective-permute-start.62
  76.8 4.5 %collective-permute-done.62 = f32[32,512]{1,0:T(8,128)S(1)} collective-permute-done((f32[32,512]{1,0:T(8,128)S(1)}, f32[32,512]{1,0:T(8,128)S(1)}, u32[]{:S(2)}, u32[]{:S(2)}) %collective-permute-start.62) | collective-permute-done | bytes 65568 | tf_op jit(solution)/shard_map/ppermute | solution.py:274
  81.5 6.5 %collective-permute-start.67 = (f32[8,32,512]{2,1,0:T(8,128)S(1)}, f32[8,32,512]{2,1,0:T(8,128)S(1)}, u32[]{:S(2)}, u32[]{:S(2)}) collective-permute-start(f32[8,32,512]{2,1,0:T(8,128)S(1)} %bitcast_dynamic-update-slice_fusion.own_ref), channel_id=1, source_target_pairs={{0,1},{1,0},{2,3},{3,2},{4,5},{5,4},{6,7},{7,6},{8,9},{9,8},{10,11... | collective-permute-start | bytes 1572872 | tf_op jit(solution)/shard_map/ppermute | solution.py:274
  88.0 0.8 copy-done.1
  88.8 0.7 collective-permute-done.67.twin_ref
  89.5 0.8 copy-done.3
  90.3 1.2 copy-done
  91.6 1.0 copy-done.2
  92.6 1.1 copy-done.4
  93.7 28.0 %factor.1 = (bf16[1536,512]{1,0:T(8,128)(2,1)S(1)}, bf16[1536,512]{1,0:T(8,128)(2,1)S(1)}) custom-call(s32[7]{0:T(128)S(1)} %stack.54.info, f32[8,32,512]{2,1,0:T(8,128)S(1)} %copy-done.2, f32[8,32,512]{2,1,0:T(8,128)S(1)} %copy-done.4, f32[8,256,128]{2,1,0:T(8,128)S(1)} %bitcast.33), custom_call_target="tpu_custom_call" | custom-call | tf_op jit(solution)/shard_map/factor/pallas_call | solution.py:201
  121.7 10.6 %all-gather.7.cloned.1.call-done = f32[8192,128]{1,0:T(8,128)} async-done(((f32[256,128]{1,0:T(8,128)}), f32[8192,128]{1,0:T(8,128)}) %all-gather.7.cloned.1.call-update) | async-done | bytes 4194320 | tf_op jit(solution)/shard_map/all_gather | solution.py:331
  132.3 13.7 %update.1 = (f32[2,8,256,256]{3,2,1,0:T(8,128)}, f32[8,1024,128]{2,1,0:T(8,128)}) custom-call(s32[7]{0:T(128)S(1)} %stack.54.info, bf16[1536,512]{1,0:T(8,128)(2,1)S(1)} %get-tuple-element.90.w_ref, bf16[1536,512]{1,0:T(8,128)(2,1)S(1)} %get-tuple-element.91.c_ref, f32[32,256,128]{2,1,0:T(8,128)} %bitcast.44, f32[8,1024,128]{2,1,0:T(8,128)} %bitcast.43), custom_call_target="tpu_custom_call" | custom-call | tf_op jit(solution)/shard_map/update/pallas_call | solution.py:235
  (45 shorter events, 0.4 us)
Async XLA Ops:
  7.2 83.2 %all-gather.5.cloned.1.call-start = ((), (), s32[]{:S(2)}) async-start(), calls=%async_computation | async-start | bytes 1179648 | tf_op jit(solution)/shard_map/all_gather | solution.py:312
  12.8 25.1 %copy-start.7 = (s32[2]{0:T(128)S(1)}, s32[2]{0:T(128)}, u32[]{:S(2)}) copy-start(s32[2]{0:T(128)} %param.11) | copy-start | bytes 28
  12.9 12.4 %collective-permute-start.5 = (f32[256,128]{1,0:T(8,128)S(1)}, f32[256,128]{1,0:T(8,128)S(1)}, u32[]{:S(2)}, u32[]{:S(2)}) collective-permute-start(f32[256,128]{1,0:T(8,128)S(1)} %get-tuple-element.97), channel_id=1, source_target_pairs={{224,32},{225,33},{226,34},{227,35},{228,36},{229,37},{230,38},{23... | collective-permute-start | bytes 393224 | tf_op jit(solution)/shard_map/cond/branch_0_fun/ppermute | solution.py:291
  13.6 13.1 %collective-permute-start.4 = (f32[256,128]{1,0:T(8,128)S(1)}, f32[256,128]{1,0:T(8,128)S(1)}, u32[]{:S(2)}, u32[]{:S(2)}) collective-permute-start(f32[256,128]{1,0:T(8,128)S(1)} %get-tuple-element.98), channel_id=1, source_target_pairs={{224,96},{225,97},{226,98},{227,99},{228,100},{229,101},{230,102},... | collective-permute-start | bytes 393224 | tf_op jit(solution)/shard_map/cond/branch_0_fun/ppermute | solution.py:291
  14.3 12.4 %collective-permute-start.2 = (f32[256,128]{1,0:T(8,128)S(1)}, f32[256,128]{1,0:T(8,128)S(1)}, u32[]{:S(2)}, u32[]{:S(2)}) collective-permute-start(f32[256,128]{1,0:T(8,128)S(1)} %get-tuple-element.99), channel_id=1, source_target_pairs={{224,160},{225,161},{226,162},{227,163},{228,164},{229,165},{230,1... | collective-permute-start | bytes 393224 | tf_op jit(solution)/shard_map/cond/branch_0_fun/ppermute | solution.py:291
  15.0 11.7 %collective-permute-start.3 = (f32[256,128]{1,0:T(8,128)S(1)}, f32[256,128]{1,0:T(8,128)S(1)}, u32[]{:S(2)}, u32[]{:S(2)}) collective-permute-start(f32[256,128]{1,0:T(8,128)S(1)} %get-tuple-element.100), channel_id=1, source_target_pairs={{0,64},{1,65},{2,66},{3,67},{4,68},{5,69},{6,70},{7,71},{8,72},{9,... | collective-permute-start | bytes 393224 | tf_op jit(solution)/shard_map/cond/branch_0_fun/ppermute | solution.py:297
  20.7 8.1 %collective-permute-start.1 = (f32[256,128]{1,0:T(8,128)S(1)}, f32[256,128]{1,0:T(8,128)S(1)}, u32[]{:S(2)}, u32[]{:S(2)}) collective-permute-start(f32[256,128]{1,0:T(8,128)S(1)} %get-tuple-element.101), channel_id=1, source_target_pairs={{0,128},{1,129},{2,130},{3,131},{4,132},{5,133},{6,134},{7,135},{8... | collective-permute-start | bytes 393224 | tf_op jit(solution)/shard_map/cond/branch_0_fun/ppermute | solution.py:297
  25.3 9.9 %collective-permute-start = (f32[256,128]{1,0:T(8,128)S(1)}, f32[256,128]{1,0:T(8,128)S(1)}, u32[]{:S(2)}, u32[]{:S(2)}) collective-permute-start(f32[256,128]{1,0:T(8,128)S(1)} %get-tuple-element.102), channel_id=1, source_target_pairs={{0,192},{1,193},{2,194},{3,195},{4,196},{5,197},{6,198},{7,199},{8... | collective-permute-start | bytes 393224 | tf_op jit(solution)/shard_map/cond/branch_0_fun/ppermute | solution.py:297
  35.3 0.6 copy-start.5
  35.9 96.3 %all-gather.7.cloned.1.call-start = ((), (), s32[]{:S(2)}) async-start(), calls=%async_computation.1 | async-start | bytes 4325376 | tf_op jit(solution)/shard_map/all_gather | solution.py:331
  36.0 11.7 %collective-permute-start.52 = (f32[256,128]{1,0:T(8,128)}, f32[256,128]{1,0:T(8,128)S(1)}, u32[]{:S(2)}, u32[]{:S(2)}) collective-permute-start(f32[256,128]{1,0:T(8,128)} %copy-done.5), channel_id=1, source_target_pairs={{0,0},{1,32},{2,64},{3,96},{4,128},{5,160},{6,192},{7,224},{8,8},{... | collective-permute-start | bytes 393224 | tf_op jit(solution)/shard_map/ppermute | solution.py:274
  39.0 1.4 collective-permute-start.53
  40.4 4.9 %collective-permute-start.56 = (f32[32,512]{1,0:T(8,128)S(1)}, f32[32,512]{1,0:T(8,128)S(1)}, u32[]{:S(2)}, u32[]{:S(2)}) collective-permute-start(f32[32,512]{1,0:T(8,128)S(1)} %dynamic-slice_select_fusion), channel_id=1, source_target_pairs={{0,8},{1,9},{2,10},{3,11},{4,12},{5,13},{6,14},{7,15},{8,16},{9,17... | collective-permute-start | bytes 196616 | tf_op jit(solution)/shard_map/ppermute | solution.py:274
  41.7 5.9 %collective-permute-start.55 = (f32[32,512]{1,0:T(8,128)S(1)}, f32[32,512]{1,0:T(8,128)S(1)}, u32[]{:S(2)}, u32[]{:S(2)}) collective-permute-start(f32[32,512]{1,0:T(8,128)S(1)} %dynamic-slice_select_fusion), channel_id=1, source_target_pairs={{0,16},{1,17},{2,18},{3,19},{4,20},{5,21},{6,22},{7,23},{8,24},{9,... | collective-permute-start | bytes 196616 | tf_op jit(solution)/shard_map/ppermute | solution.py:274
  44.2 3.5 %collective-permute-start.54 = (f32[32,512]{1,0:T(8,128)S(1)}, f32[32,512]{1,0:T(8,128)S(1)}, u32[]{:S(2)}, u32[]{:S(2)}) collective-permute-start(f32[32,512]{1,0:T(8,128)S(1)} %dynamic-slice_select_fusion), channel_id=1, source_target_pairs={{0,24},{1,25},{2,26},{3,27},{4,28},{5,29},{6,30},{7,31},{8,0},{9,1... | collective-permute-start | bytes 196616 | tf_op jit(solution)/shard_map/ppermute | solution.py:274
  47.7 0.7 copy-start.6
  48.4 9.0 %collective-permute-start.59 = (f32[32,512]{1,0:T(8,128)S(1)}, f32[32,512]{1,0:T(8,128)S(1)}, u32[]{:S(2)}, u32[]{:S(2)}) collective-permute-start(f32[32,512]{1,0:T(8,128)S(1)} %select_select_fusion.9), channel_id=1, source_target_pairs={{0,2},{1,3},{2,4},{3,5},{4,6},{5,7},{6,0},{7,1},{8,10},{9,11},{10,... | collective-permute-start | bytes 196616 | tf_op jit(solution)/shard_map/ppermute | solution.py:274
  50.8 8.4 %collective-permute-start.58 = (f32[32,512]{1,0:T(8,128)S(1)}, f32[32,512]{1,0:T(8,128)S(1)}, u32[]{:S(2)}, u32[]{:S(2)}) collective-permute-start(f32[32,512]{1,0:T(8,128)S(1)} %select_select_fusion.9), channel_id=1, source_target_pairs={{0,4},{1,5},{2,6},{3,7},{4,0},{5,1},{6,2},{7,3},{8,12},{9,13},{10,... | collective-permute-start | bytes 196616 | tf_op jit(solution)/shard_map/ppermute | solution.py:274
  56.8 3.9 %collective-permute-start.57 = (f32[32,512]{1,0:T(8,128)S(1)}, f32[32,512]{1,0:T(8,128)S(1)}, u32[]{:S(2)}, u32[]{:S(2)}) collective-permute-start(f32[32,512]{1,0:T(8,128)S(1)} %select_select_fusion.9), channel_id=1, source_target_pairs={{0,6},{1,7},{2,0},{3,1},{4,2},{5,3},{6,4},{7,5},{8,14},{9,15},{10,... | collective-permute-start | bytes 196616 | tf_op jit(solution)/shard_map/ppermute | solution.py:274
  60.7 9.0 %collective-permute-start.60 = (f32[32,512]{1,0:T(8,128)S(1)}, f32[32,512]{1,0:T(8,128)S(1)}, u32[]{:S(2)}, u32[]{:S(2)}) collective-permute-start(f32[32,512]{1,0:T(8,128)S(1)} %select_select_fusion.8), channel_id=1, source_target_pairs={{0,224},{1,225},{2,226},{3,227},{4,228},{5,229},{6,230},{7,231},{8... | collective-permute-start | bytes 196616 | tf_op jit(solution)/shard_map/ppermute | solution.py:274
  60.8 20.6 %collective-permute-start.66 = (f32[32,512]{1,0:T(8,128)S(1)}, f32[32,512]{1,0:T(8,128)S(1)}, u32[]{:S(2)}, u32[]{:S(2)}) collective-permute-start(f32[32,512]{1,0:T(8,128)S(1)} %select_select_fusion.8), channel_id=1, source_target_pairs={{0,32},{1,33},{2,34},{3,35},{4,36},{5,37},{6,38},{7,39},{8,40},{9,... | collective-permute-start | bytes 196616 | tf_op jit(solution)/shard_map/ppermute | solution.py:274
  62.3 19.1 %collective-permute-start.65 = (f32[32,512]{1,0:T(8,128)S(1)}, f32[32,512]{1,0:T(8,128)S(1)}, u32[]{:S(2)}, u32[]{:S(2)}) collective-permute-start(f32[32,512]{1,0:T(8,128)S(1)} %select_select_fusion.8), channel_id=1, source_target_pairs={{0,64},{1,65},{2,66},{3,67},{4,68},{5,69},{6,70},{7,71},{8,72},{9,... | collective-permute-start | bytes 196616 | tf_op jit(solution)/shard_map/ppermute | solution.py:274
  65.3 16.1 %collective-permute-start.64 = (f32[32,512]{1,0:T(8,128)S(1)}, f32[32,512]{1,0:T(8,128)S(1)}, u32[]{:S(2)}, u32[]{:S(2)}) collective-permute-start(f32[32,512]{1,0:T(8,128)S(1)} %select_select_fusion.8), channel_id=1, source_target_pairs={{0,96},{1,97},{2,98},{3,99},{4,100},{5,101},{6,102},{7,103},{8,104... | collective-permute-start | bytes 196616 | tf_op jit(solution)/shard_map/ppermute | solution.py:274
  66.3 15.1 %collective-permute-start.63 = (f32[32,512]{1,0:T(8,128)S(1)}, f32[32,512]{1,0:T(8,128)S(1)}, u32[]{:S(2)}, u32[]{:S(2)}) collective-permute-start(f32[32,512]{1,0:T(8,128)S(1)} %select_select_fusion.8), channel_id=1, source_target_pairs={{0,128},{1,129},{2,130},{3,131},{4,132},{5,133},{6,134},{7,135},{8... | collective-permute-start | bytes 196616 | tf_op jit(solution)/shard_map/ppermute | solution.py:274
  69.7 6.5 %collective-permute-start.61 = (f32[32,512]{1,0:T(8,128)S(1)}, f32[32,512]{1,0:T(8,128)S(1)}, u32[]{:S(2)}, u32[]{:S(2)}) collective-permute-start(f32[32,512]{1,0:T(8,128)S(1)} %select_select_fusion.8), channel_id=1, source_target_pairs={{0,192},{1,193},{2,194},{3,195},{4,196},{5,197},{6,198},{7,199},{8... | collective-permute-start | bytes 196616 | tf_op jit(solution)/shard_map/ppermute | solution.py:274
  76.3 5.1 %collective-permute-start.62 = (f32[32,512]{1,0:T(8,128)S(1)}, f32[32,512]{1,0:T(8,128)S(1)}, u32[]{:S(2)}, u32[]{:S(2)}) collective-permute-start(f32[32,512]{1,0:T(8,128)S(1)} %select_select_fusion.8), channel_id=1, source_target_pairs={{0,160},{1,161},{2,162},{3,163},{4,164},{5,165},{6,166},{7,167},{8... | collective-permute-start | bytes 196616 | tf_op jit(solution)/shard_map/ppermute | solution.py:274
  81.5 8.0 %collective-permute-start.67 = (f32[8,32,512]{2,1,0:T(8,128)S(1)}, f32[8,32,512]{2,1,0:T(8,128)S(1)}, u32[]{:S(2)}, u32[]{:S(2)}) collective-permute-start(f32[8,32,512]{2,1,0:T(8,128)S(1)} %bitcast_dynamic-update-slice_fusion.own_ref), channel_id=1, source_target_pairs={{0,1},{1,0},{2,3},{3,2},{4,5},{5,4},{6,7},{7,6},{8,9},{9,8},{10,11... | collective-permute-start | bytes 1572872 | tf_op jit(solution)/shard_map/ppermute | solution.py:274
  88.0 0.8 copy-start.1
  89.5 0.8 copy-start.3
  90.3 1.2 copy-start
  91.6 1.0 copy-start.2
  92.6 1.1 copy-start.4
Sparse Core Ops, SparseCore 0:
  36.1 35.4 all-gather.4
  74.1 58.0 all-gather.6
where the time goes:
time: 152 us; the launch traced here: 153 us
  starting transfers between devices  46.3 us (30%)
  Pallas kernels  42.6 us (28%)
  waiting for transfers between devices  37.3 us (25%)
  between operations  16.1 us (11%)
  local copies, waits for them, and re-layouts  10.2 us (7%)
    ppermute x16, starting transfers between devices, shards(): lax.ppermute(value, AXES, [(device(a, b), device(*to(a, b))) for a, b in...  32.6 us
    pallas_call x1, Pallas kernels, factor(): pl.pallas_call(factor_kernel, out_shape=[jax.ShapeDtypeStruct((3 * n, n),...  28 us
    ppermute x16, waiting for transfers between devices, shards(): lax.ppermute(value, AXES, [(device(a, b), device(*to(a, b))) for a, b in...  18.1 us
    pallas_call x1, Pallas kernels, update(): pl.pallas_call(update_kernel, grid_spec=pltpu.PrefetchScalarGridSpec(num_...  13.7 us
    ppermute x3, starting transfers between devices, run(): arrived.append((plane, lax.ppermute(part(others, q), AXES, pairs)))  11.6 us
    all_gather x1, waiting for transfers between devices, shards(): gathered = lax.all_gather(moved, 'pcol', axis=0, tiled=False)  10.6 us
    ppermute x3, waiting for transfers between devices, run(): arrived.append((plane, lax.ppermute(part(others, q), AXES, pairs)))  8.53 us
    unnamed x23, local copies, waits for them, and re-layouts  6.25 us
  transfers between devices with their start and end apart: 24, of which 10 were waited for; matrix products, arithmetic and copies ran while one was open for 0% of the time, Pallas kernels for 19%

commit v1 on v0

--- a/solution.py
+++ b/solution.py
@@ -38,18 +38,26 @@
     n = GROUP
     g = [row[:] for row in scalars]
     unit = [[None] * n for _ in range(n)]
-    pivots = []
-    inverses = []
-    for q in range(n):
-        d = g[q][q]
-        inv = 1.0 / d
-        pivots.append(d)
-        inverses.append(inv)
-        for i in range(q + 1, n):
-            unit[i][q] = g[i][q] * inv
-        for i in range(q + 1, n):
-            for k in range(q + 1, i + 1):
-                g[i][k] = g[i][k] - unit[i][q] * g[k][q]
+    pivots, inverses = [], []
+    for q in range(0, n, 2):
+        a, b, d = g[q][q], g[q + 1][q], g[q + 1][q + 1]
+        det = a * d - b * b
+        over = 1.0 / det
+        inv = 1.0 / a
+        step = b * inv
+        below = d - step * b
+        pivots += [a, below]
+        inverses += [inv, a * over]
+        unit[q + 1][q] = step
+        for i in range(q + 2, n):
+            x, y = g[i][q], g[i][q + 1]
+            unit[i][q] = x * inv
+            unit[i][q + 1] = (y * a - x * b) * over
+        for i in range(q + 2, n):
+            x, y = g[i][q], g[i][q + 1]
+            u, v = (x * d - y * b) * over, unit[i][q + 1]
+            for k in range(q + 2, i + 1):
+                g[i][k] = g[i][k] - (u * g[k][q] + v * g[k][q + 1])
     w = [[None] * n for _ in range(n)]
     for q in range(n):
         for i in range(q + 1, n):
@@ -143,6 +151,7 @@
 VMEM = pl.BlockSpec(memory_space=pltpu.VMEM)
 SMEM = pl.BlockSpec(memory_space=pltpu.SMEM)
 ROW, COLUMN, ROOT, HELD, FLIPPED, FIRST, SECOND = range(7)
+MASKS = (0, 4, 2, 6, 1, 5, 3, 7)
 PARAMS = pltpu.CompilerParams(vmem_limit_bytes=48 * 1024 * 1024)
 
 
@@ -174,39 +183,59 @@
     )(info, piece)
 
 
-def factor_kernel(info, own_ref, twin_ref, x_ref, w_ref, c_ref, s_ref, z_ref, m_ref):
+def factor_kernel(info, own_ref, twin_ref, m_ref, s_ref, z_ref):
     flip = info[FLIPPED] == 1
     core = info[COLUMN] % 2
     for slot in range(PLANES):
-        base = place_of(info, (info[ROW] + 1 + slot) % PLANES) * CHUNK
+        base = place_of(info, info[ROW] ^ MASKS[slot]) * CHUNK
         for ref, side in ((own_ref, core), (twin_ref, 1 - core)):
             v = ref[slot]
             v = jnp.where(flip, jnp.concatenate([v[:, NB:], v[:, :NB]], axis=1), v)
             s_ref[pl.ds(pl.multiple_of(base + side * HALF, HALF), HALF), :] = v
     factor_inverse(s_ref, z_ref, m_ref)
-    s_ref[...] = m_ref[...].T
-    for plane in range(PLANES):
-        start = pl.multiple_of(place_of(info, plane) * CHUNK, CHUNK)
-        z_ref[plane * CHUNK : (plane + 1) * CHUNK, :] = s_ref[pl.ds(start, CHUNK), :]
-    weights = split(z_ref[...])
-    w_ref[...] = stack(weights)
-    weights = weights[0].T, weights[1].T
-    for column in range(2):
-        x = jnp.concatenate([block_column(x_ref.at[plane], column, CHUNK) for plane in range(PLANES)], axis=0)
-        c_ref[:, column * NB : (column + 1) * NB] = stack(split(dot3(weights, split(x))))
-
-
-def factor(info, own, twin, crossing):
+
+
+def factor(info, own, twin):
     n = 2 * NB
     return pl.pallas_call(
         factor_kernel,
+        out_shape=jax.ShapeDtypeStruct((n, n), jnp.float32),
+        in_specs=[SMEM, VMEM, VMEM],
+        out_specs=VMEM,
+        scratch_shapes=[pltpu.VMEM((n, n), jnp.float32)] * 2,
+        compiler_params=PARAMS,
+        cost_estimate=pl.CostEstimate(flops=10**9, transcendentals=0, bytes_accessed=9 * 10**7),
+        name="factor",
+    )(info, own, twin)
+
+
+def cross_kernel(info, m_ref, near_ref, far_ref, w_ref, c_ref, t_ref, x_ref):
+    t_ref[...] = m_ref[...].T
+    for plane in range(PLANES):
+        start = pl.multiple_of(place_of(info, plane) * CHUNK, CHUNK)
+        x_ref[plane * CHUNK : (plane + 1) * CHUNK, :] = t_ref[pl.ds(start, CHUNK), :]
+    weights = split(x_ref[...])
+    w_ref[...] = stack(weights)
+    weights = weights[0].T, weights[1].T
+    for slot in range(PLANES):
+        ref = (near_ref, far_ref)[slot // 4].at[slot % 4]
+        start = pl.multiple_of((info[ROW] ^ MASKS[slot]) * CHUNK, CHUNK)
+        for column in range(2):
+            x_ref[pl.ds(start, CHUNK), column * NB : (column + 1) * NB] = block_column(ref, column, CHUNK)
+    c_ref[...] = stack(split(dot3(weights, split(x_ref[...]))))
+
+
+def cross(info, inverse, near, far):
+    n = 2 * NB
+    return pl.pallas_call(
+        cross_kernel,
         out_shape=[jax.ShapeDtypeStruct((3 * n, n), jnp.bfloat16)] * 2,
-        in_specs=[SMEM, VMEM, VMEM, VMEM],
+        in_specs=[SMEM] + [VMEM] * 3,
         out_specs=[VMEM] * 2,
-        scratch_shapes=[pltpu.VMEM((n, n), jnp.float32)] * 3,
+        scratch_shapes=[pltpu.VMEM((n, n), jnp.float32)] * 2,
         compiler_params=PARAMS,
-        name="factor",
-    )(info, own, twin, crossing)
+        name="cross",
+    )(info, inverse, near, far)
 
 
 def update_kernel(info, w_ref, c_ref, g_ref, a_ref, panels_ref, t_ref):
@@ -272,7 +301,8 @@
     device = lambda row, column: row * width + column
     everyone = [(row, column) for row in range(height) for column in range(width)]
     send = lambda value, to: lax.ppermute(value, AXES, [(device(a, b), device(*to(a, b))) for a, b in everyone])
-    up = lambda value, d: send(value, lambda a, b: ((a + d) % height, b))
+    double = lambda value, mask: jnp.concatenate([value, send(value, lambda a, b: (a ^ mask, b))], axis=0)
+    tie = lambda *values: lax.optimization_barrier(values)
     core_twin = lambda value: send(value, lambda a, b: (a, b ^ 1))
 
     piece_rows = 4 * CHUNK
@@ -306,11 +336,13 @@
         return run
 
     others = lax.dynamic_slice(flat, (block_row, 0, 0), (1,) + flat.shape[1:])[0]
-    piece = lax.switch(root_row, [scatter_from(root) for root in range(height)], others, flat[NEWEST // height])
+    rows = tie(others, flat[NEWEST // height])
+    piece = lax.switch(root_row, [scatter_from(root) for root in range(height)], *rows)
     both = pick(info, piece)
 
-    crossing = lax.all_gather(piece, "prow", axis=0, tiled=False)
     moved = send(piece, lambda a, b: (b % height, (b // height) * height + a))
+
+    crossing = double(piece[None], 4)
 
     core, ypos, xpos = c & 1, (c >> 1) & 3, c >> 3
     rcore, ry, rx = root_col & 1, (root_col >> 1) & 3, root_col >> 3
@@ -327,11 +359,14 @@
         return out
 
     mine = spread(mine, xpos, rx, 3, lambda b, d: (b + 8 * d) % 32)
-    moved, mine = lax.optimization_barrier((moved, mine))
+    moved, crossing, mine = tie(moved, crossing, mine)
     gathered = lax.all_gather(moved, "pcol", axis=0, tiled=False)
+    crossing = double(crossing, 2)
     mine = spread(mine, ypos, ry, 3, lambda b, d: (b // 8) * 8 + (b + 2 * d) % 8)
-    ring = jnp.stack([up(mine, d) for d in range(height - 1, 0, -1)] + [mine])
-    factors = factor(info, ring, core_twin(ring), crossing)
+    crossing, mine = tie(crossing, mine)
+    beyond = send(crossing, lambda a, b: (a ^ 1, b))
+    ring = double(double(double(mine[None], 4), 2), 1)
+    factors = cross(info, factor(info, ring, core_twin(ring)), crossing, beyond)
     panels, trailing = update(info, factors, gathered, flat)
     return panels.reshape(2, br, 1, NB, NB), trailing.reshape(kernel.shape)
 

time: 152 us -> 149 us (0.980)
  waiting for transfers between devices: 37.3 us -> 44.3 us
  starting transfers between devices: 46.3 us -> 41 us
  local copies, waits for them, and re-layouts: 10.2 us -> 5.51 us
    ppermute x16 -> x15, waiting for transfers between devices: 18.1 us -> 35.9 us  [shards(): lax.ppermute(value, AXES, [(device(a, b), device(*to(a, b))) for a, b in...]
    all_gather x1, waiting for transfers between devices: 10.6 us -> 0.02 us  [shards(): gathered = lax.all_gather(moved, 'pcol', axis=0, tiled=False)]
    ppermute x3, starting transfers between devices: 11.6 us -> 2.62 us  [run(): arrived.append((plane, lax.ppermute(part(others, q), AXES, pairs)))]
    ppermute x3, waiting for transfers between devices: 8.53 us -> 2.14 us  [run(): arrived.append((plane, lax.ppermute(part(others, q), AXES, pairs)))]
    ppermute x3 -> x4, waiting for transfers between devices: 0.01 us -> 6.24 us  [run(): lax.ppermute(part(newest, q), AXES, line(height - 1, plane))]
    unnamed x23 -> x4, local copies, waits for them, and re-layouts: 6.25 us -> 0.66 us
    ppermute x16 -> x15, starting transfers between devices: 32.6 us -> 35.1 us  [shards(): lax.ppermute(value, AXES, [(device(a, b), device(*to(a, b))) for a, b in...]
    ppermute x3 -> x4, starting transfers between devices: 2.01 us -> 3.3 us  [run(): lax.ppermute(part(newest, q), AXES, line(height - 1, plane))]
  transfers between devices with their start and end apart: 24 -> 23, of which waited for: 10 -> 11; matrix products, arithmetic and copies ran while one was open for 0% -> 0% of each run, Pallas kernels for 19% -> 19%
where the time goes in v1:
time: 149 us
  waiting for transfers between devices  44.3 us (30%)
  Pallas kernels  41.4 us (28%)
  starting transfers between devices  41 us (28%)
  between operations  16.1 us (11%)
  local copies, waits for them, and re-layouts  5.51 us (4%)
    ppermute x15, waiting for transfers between devices, shards(): lax.ppermute(value, AXES, [(device(a, b), device(*to(a, b))) for a, b in...  35.9 us
    ppermute x15, starting transfers between devices, shards(): lax.ppermute(value, AXES, [(device(a, b), device(*to(a, b))) for a, b in...  35.1 us
    pallas_call x1, Pallas kernels, factor(): pl.pallas_call(factor_kernel, out_shape=jax.ShapeDtypeStruct((n, n), jnp....  24.9 us
    pallas_call x1, Pallas kernels, update(): pl.pallas_call(update_kernel, grid_spec=pltpu.PrefetchScalarGridSpec(num_...  13.7 us
    ppermute x4, waiting for transfers between devices, run(): lax.ppermute(part(newest, q), AXES, line(height - 1, plane))  6.24 us
    ppermute x4, starting transfers between devices, run(): lax.ppermute(part(newest, q), AXES, line(height - 1, plane))  3.3 us
  transfers between devices with their start and end apart: 23, of which 11 were waited for; matrix products, arithmetic and copies ran while one was open for 0% of the time, Pallas kernels for 19%

profile of v1, /device:TPU:1, one launch (start us, length us, event | category | flops | bytes accessed | tf_op | source)
XLA Modules:
  0.0 149.5 jit_solution(14083497442699453429)
XLA Ops:
  7.2 0.0 all-gather.3.cloned.1.call-start
  7.2 1.3 fusion.17
  10.4 1.4 slice.221
  11.8 1.1 dynamic-slice_bitcast_fusion
  12.9 0.0 copy-start.1
  12.9 16.1 %conditional.1 = (f32[256,128]{1,0:T(8,128)}, f32[256,128]{1,0:T(8,128)S(1)}) conditional(s32[]{:T(128)} %clamp.3, (s32[]{:T(128)}, f32[1024,128]{1,0:T(8,128)S(1)}, f32[1024,128]{1,0:T(8,128)S(1)}) %tuple.150, (s32[]{:T(128)}, f32[1024,128]{1,0:T(8,128)S(1)}, f32[1024,128]{1,0:T(8,128)S(1)}) %tuple.154, (s32[]{:T(128)}, ...), branch_computations={%region_0.1_spmd, %region_1.2_spmd, %region_2.3_spmd, %region_3.4_... | conditional | flops 229383 | bytes 6947182 | solution.py:340
  13.0 1.3 collective-permute-start.25
  14.3 0.7 collective-permute-start.23
  15.0 0.7 collective-permute-start.22
  15.7 0.7 collective-permute-start.20
  16.4 1.3 collective-permute-start.24
  17.7 6.2 %collective-permute-done.25 = f32[256,128]{1,0:T(8,128)S(1)} collective-permute-done((f32[256,128]{1,0:T(8,128)S(1)}, f32[256,128]{1,0:T(8,128)S(1)}, u32[]{:S(2)}, u32[]{:S(2)}) %collective-permute-start.25) | collective-permute-done | bytes 131104 | tf_op jit(solution)/shard_map/cond/branch_3_fun/ppermute | solution.py:321
  23.9 0.7 collective-permute-start.21
  24.6 0.7 collective-permute-start.19
  25.3 2.1 %collective-permute-done.24 = f32[256,128]{1,0:T(8,128)S(1)} collective-permute-done((f32[256,128]{1,0:T(8,128)S(1)}, f32[256,128]{1,0:T(8,128)S(1)}, u32[]{:S(2)}, u32[]{:S(2)}) %collective-permute-start.24) | collective-permute-done | bytes 131104 | tf_op jit(solution)/shard_map/cond/branch_3_fun/ppermute | solution.py:327
  27.5 0.7 select_select_fusion.3
  28.2 0.9 copy.13
  29.1 1.9 %collective-permute-start.52 = (f32[256,128]{1,0:T(8,128)S(1)}, f32[256,128]{1,0:T(8,128)S(1)}, u32[]{:S(2)}, u32[]{:S(2)}) collective-permute-start(f32[256,128]{1,0:T(8,128)S(1)} %get-tuple-element.109.piece_ref), channel_id=1, source_target_pairs={{0,0},{1,32},{2,64},{3,96},{4,128},{5,160},{6,192},{7,224},{8,8},{... | collective-permute-start | bytes 393224 | tf_op jit(solution)/shard_map/ppermute | solution.py:303
  31.0 0.1 stack.27.info
  31.1 0.6 pick.1
  31.7 0.1 collective-permute-start.54
  31.8 9.5 %collective-permute-start.53 = (f32[1,256,128]{2,1,0:T(8,128)S(1)}, f32[1,256,128]{2,1,0:T(8,128)S(1)}, u32[]{:S(2)}, u32[]{:S(2)}) collective-permute-start(f32[1,256,128]{2,1,0:T(8,128)S(1)} %bitcast.29), channel_id=1, source_target_pairs={{0,128},{1,129},{2,130},{3,131},{4,132},{5,133},{6,134},{7,135},{8... | collective-permute-start | bytes 393224 | tf_op jit(solution)/shard_map/ppermute | solution.py:303
  41.4 1.3 collective-permute-start.57
  42.7 2.5 %collective-permute-start.56 = (f32[32,512]{1,0:T(8,128)S(1)}, f32[32,512]{1,0:T(8,128)S(1)}, u32[]{:S(2)}, u32[]{:S(2)}) collective-permute-start(f32[32,512]{1,0:T(8,128)S(1)} %dynamic-slice_select_fusion), channel_id=1, source_target_pairs={{0,16},{1,17},{2,18},{3,19},{4,20},{5,21},{6,22},{7,23},{8,24},{9,... | collective-permute-start | bytes 196616 | tf_op jit(solution)/shard_map/ppermute | solution.py:303
  45.1 1.2 collective-permute-start.55
  46.3 1.8 %collective-permute-done.56 = f32[32,512]{1,0:T(8,128)S(1)} collective-permute-done((f32[32,512]{1,0:T(8,128)S(1)}, f32[32,512]{1,0:T(8,128)S(1)}, u32[]{:S(2)}, u32[]{:S(2)}) %collective-permute-start.56) | collective-permute-done | bytes 65568 | tf_op jit(solution)/shard_map/ppermute | solution.py:303
  48.1 0.5 collective-permute-done.55
  48.6 0.6 copy-done
  49.2 0.0 all-gather.3.cloned.1.call-update
  49.3 4.1 %collective-permute-start.61 = (f32[32,512]{1,0:T(8,128)S(1)}, f32[32,512]{1,0:T(8,128)S(1)}, u32[]{:S(2)}, u32[]{:S(2)}) collective-permute-start(f32[32,512]{1,0:T(8,128)S(1)} %select_select_fusion.9), channel_id=1, source_target_pairs={{0,2},{1,3},{2,4},{3,5},{4,6},{5,7},{6,0},{7,1},{8,10},{9,11},{10,... | collective-permute-start | bytes 196616 | tf_op jit(solution)/shard_map/ppermute | solution.py:303
  53.4 7.7 %collective-permute-start.60 = (f32[32,512]{1,0:T(8,128)S(1)}, f32[32,512]{1,0:T(8,128)S(1)}, u32[]{:S(2)}, u32[]{:S(2)}) collective-permute-start(f32[32,512]{1,0:T(8,128)S(1)} %select_select_fusion.9), channel_id=1, source_target_pairs={{0,4},{1,5},{2,6},{3,7},{4,0},{5,1},{6,2},{7,3},{8,12},{9,13},{10,... | collective-permute-start | bytes 196616 | tf_op jit(solution)/shard_map/ppermute | solution.py:303
  61.1 1.3 collective-permute-start.58
  62.4 2.4 %collective-permute-done.60 = f32[32,512]{1,0:T(8,128)S(1)} collective-permute-done((f32[32,512]{1,0:T(8,128)S(1)}, f32[32,512]{1,0:T(8,128)S(1)}, u32[]{:S(2)}, u32[]{:S(2)}) %collective-permute-start.60) | collective-permute-done | bytes 65568 | tf_op jit(solution)/shard_map/ppermute | solution.py:303
  64.8 0.1 collective-permute-done.59
  65.0 10.8 %collective-permute-done.58 = f32[2,256,128]{2,1,0:T(8,128)S(1)} collective-permute-done((f32[2,256,128]{2,1,0:T(8,128)S(1)}, f32[2,256,128]{2,1,0:T(8,128)S(1)}, u32[]{:S(2)}, u32[]{:S(2)}) %collective-permute-start.58) | collective-permute-done | bytes 262176 | tf_op jit(solution)/shard_map/ppermute | solution.py:303
  75.8 2.8 %collective-permute-start.62 = (f32[1,32,512]{2,1,0:T(8,128)S(1)}, f32[1,32,512]{2,1,0:T(8,128)S(1)}, u32[]{:S(2)}, u32[]{:S(2)}) collective-permute-start(f32[1,32,512]{2,1,0:T(8,128)S(1)} %bitcast.31), channel_id=1, source_target_pairs={{0,128},{1,129},{2,130},{3,131},{4,132},{5,133},{6,134},{7,135},{8... | collective-permute-start | bytes 196616 | tf_op jit(solution)/shard_map/ppermute | solution.py:303
  78.6 4.5 %collective-permute-done.62 = f32[1,32,512]{2,1,0:T(8,128)S(1)} collective-permute-done((f32[1,32,512]{2,1,0:T(8,128)S(1)}, f32[1,32,512]{2,1,0:T(8,128)S(1)}, u32[]{:S(2)}, u32[]{:S(2)}) %collective-permute-start.62) | collective-permute-done | bytes 65568 | tf_op jit(solution)/shard_map/ppermute | solution.py:303
  83.1 0.1 collective-permute-start.63
  83.2 8.0 %collective-permute-done.63 = f32[2,32,512]{2,1,0:T(8,128)S(1)} collective-permute-done((f32[2,32,512]{2,1,0:T(8,128)S(1)}, f32[2,32,512]{2,1,0:T(8,128)S(1)}, u32[]{:S(2)}, u32[]{:S(2)}) %collective-permute-start.63) | collective-permute-done | bytes 131104 | tf_op jit(solution)/shard_map/ppermute | solution.py:303
  91.2 0.1 collective-permute-start.64
  91.3 6.3 %collective-permute-done.64 = f32[4,32,512]{2,1,0:T(8,128)S(1)} collective-permute-done((f32[4,32,512]{2,1,0:T(8,128)S(1)}, f32[4,32,512]{2,1,0:T(8,128)S(1)}, u32[]{:S(2)}, u32[]{:S(2)}) %collective-permute-start.64) | collective-permute-done | bytes 262176 | tf_op jit(solution)/shard_map/ppermute | solution.py:303
  97.7 2.5 %collective-permute-start.65 = (f32[8,32,512]{2,1,0:T(8,128)S(1)}, f32[8,32,512]{2,1,0:T(8,128)S(1)}, u32[]{:S(2)}, u32[]{:S(2)}) collective-permute-start(f32[8,32,512]{2,1,0:T(8,128)S(1)} %pad_maximum_fusion.1.own_ref), channel_id=1, source_target_pairs={{0,1},{1,0},{2,3},{3,2},{4,5},{5,4},{6,7},{7,6},{8,9},{9,8},{10,11... | collective-permute-start | bytes 1572872 | tf_op jit(solution)/shard_map/ppermute | solution.py:303
  100.2 0.0 collective-permute-start.66
  100.2 1.5 %collective-permute-done.65.twin_ref = f32[8,32,512]{2,1,0:T(8,128)S(1)} collective-permute-done((f32[8,32,512]{2,1,0:T(8,128)S(1)}, f32[8,32,512]{2,1,0:T(8,128)S(1)}, u32[]{:S(2)}, u32[]{:S(2)}) %collective-permute-start.65) | collective-permute-done | bytes 524320 | tf_op jit(solution)/shard_map/ppermute | solution.py:303
  101.7 24.9 %factor.1.m_ref = f32[512,512]{1,0:T(8,128)S(1)} custom-call(s32[7]{0:T(128)S(1)} %stack.27.info, f32[8,32,512]{2,1,0:T(8,128)S(1)} %pad_maximum_fusion.1.own_ref, f32[8,32,512]{2,1,0:T(8,128)S(1)} %collective-permute-done.65.twin_ref), custom_call_target="tpu_custom_call" | custom-call | flops 1000000000 | bytes 90000000 | tf_op jit(solution)/shard_map/factor/pallas_call | solution.py:200
  126.6 2.2 %cross.1 = (bf16[1536,512]{1,0:T(8,128)(2,1)S(1)}, bf16[1536,512]{1,0:T(8,128)(2,1)S(1)}) custom-call(s32[7]{0:T(128)S(1)} %stack.27.info, f32[512,512]{1,0:T(8,128)S(1)} %factor.1.m_ref, f32[4,256,128]{2,1,0:T(8,128)S(1)} %pad_maximum_fusion.near_ref, f32[4,256,128]{2,1,0:T(8,128)S(1)} %collective-permute-done.66.far_ref), custom_call_target="tpu_custom_call" | custom-call | tf_op jit(solution)/shard_map/cross/pallas_call | solution.py:230
  128.9 0.0 all-gather.3.cloned.1.call-done
  128.9 13.7 %update.1 = (f32[2,8,256,256]{3,2,1,0:T(8,128)}, f32[8,1024,128]{2,1,0:T(8,128)}) custom-call(s32[7]{0:T(128)S(1)} %stack.27.info, bf16[1536,512]{1,0:T(8,128)(2,1)S(1)} %get-tuple-element.100.w_ref, bf16[1536,512]{1,0:T(8,128)(2,1)S(1)} %get-tuple-element.101.c_ref, f32[32,256,128]{2,1,0:T(8,128)} %bitcast.28, f32[8,1024,128]{2,1,0:T(8,128)} %bitcast.27), custom_call_target="tpu_custom_call" | custom-call | tf_op jit(solution)/shard_map/update/pallas_call | solution.py:264
  (29 shorter events, 0.3 us)
Async XLA Ops:
  7.2 121.7 %all-gather.3.cloned.1.call-start = ((), (), s32[]{:S(2)}) async-start(), calls=%async_computation | async-start | bytes 4325376 | tf_op jit(solution)/shard_map/all_gather | solution.py:363
  12.9 18.1 %copy-start.1 = (s32[2]{0:T(128)S(1)}, s32[2]{0:T(128)}, u32[]{:S(2)}) copy-start(s32[2]{0:T(128)} %param.11) | copy-start | bytes 28
  13.0 10.9 %collective-permute-start.25 = (f32[256,128]{1,0:T(8,128)S(1)}, f32[256,128]{1,0:T(8,128)S(1)}, u32[]{:S(2)}, u32[]{:S(2)}) collective-permute-start(f32[256,128]{1,0:T(8,128)S(1)} %get-tuple-element.129), channel_id=1, source_target_pairs={{224,0},{225,1},{226,2},{227,3},{228,4},{229,5},{230,6},{231,7},{2... | collective-permute-start | bytes 393224 | tf_op jit(solution)/shard_map/cond/branch_3_fun/ppermute | solution.py:321
  14.3 10.3 %collective-permute-start.23 = (f32[256,128]{1,0:T(8,128)S(1)}, f32[256,128]{1,0:T(8,128)S(1)}, u32[]{:S(2)}, u32[]{:S(2)}) collective-permute-start(f32[256,128]{1,0:T(8,128)S(1)} %get-tuple-element.130), channel_id=1, source_target_pairs={{224,64},{225,65},{226,66},{227,67},{228,68},{229,69},{230,70},{23... | collective-permute-start | bytes 393224 | tf_op jit(solution)/shard_map/cond/branch_3_fun/ppermute | solution.py:321
  15.0 10.3 %collective-permute-start.22 = (f32[256,128]{1,0:T(8,128)S(1)}, f32[256,128]{1,0:T(8,128)S(1)}, u32[]{:S(2)}, u32[]{:S(2)}) collective-permute-start(f32[256,128]{1,0:T(8,128)S(1)} %get-tuple-element.131), channel_id=1, source_target_pairs={{224,128},{225,129},{226,130},{227,131},{228,132},{229,133},{230,1... | collective-permute-start | bytes 393224 | tf_op jit(solution)/shard_map/cond/branch_3_fun/ppermute | solution.py:321
  15.7 9.6 %collective-permute-start.20 = (f32[256,128]{1,0:T(8,128)S(1)}, f32[256,128]{1,0:T(8,128)S(1)}, u32[]{:S(2)}, u32[]{:S(2)}) collective-permute-start(f32[256,128]{1,0:T(8,128)S(1)} %get-tuple-element.132), channel_id=1, source_target_pairs={{224,192},{225,193},{226,194},{227,195},{228,196},{229,197},{230,1... | collective-permute-start | bytes 393224 | tf_op jit(solution)/shard_map/cond/branch_3_fun/ppermute | solution.py:321
  16.4 11.1 %collective-permute-start.24 = (f32[256,128]{1,0:T(8,128)S(1)}, f32[256,128]{1,0:T(8,128)S(1)}, u32[]{:S(2)}, u32[]{:S(2)}) collective-permute-start(f32[256,128]{1,0:T(8,128)S(1)} %get-tuple-element.133), channel_id=1, source_target_pairs={{64,0},{65,1},{66,2},{67,3},{68,4},{69,5},{70,6},{71,7},{72,8},{73... | collective-permute-start | bytes 393224 | tf_op jit(solution)/shard_map/cond/branch_3_fun/ppermute | solution.py:327
  23.9 3.5 %collective-permute-start.21 = (f32[256,128]{1,0:T(8,128)S(1)}, f32[256,128]{1,0:T(8,128)S(1)}, u32[]{:S(2)}, u32[]{:S(2)}) collective-permute-start(f32[256,128]{1,0:T(8,128)S(1)} %get-tuple-element.134), channel_id=1, source_target_pairs={{64,128},{65,129},{66,130},{67,131},{68,132},{69,133},{70,134},{71... | collective-permute-start | bytes 393224 | tf_op jit(solution)/shard_map/cond/branch_3_fun/ppermute | solution.py:327
  24.6 2.9 %collective-permute-start.19 = (f32[256,128]{1,0:T(8,128)S(1)}, f32[256,128]{1,0:T(8,128)S(1)}, u32[]{:S(2)}, u32[]{:S(2)}) collective-permute-start(f32[256,128]{1,0:T(8,128)S(1)} %get-tuple-element.135), channel_id=1, source_target_pairs={{64,192},{65,193},{66,194},{67,195},{68,196},{69,197},{70,198},{71... | collective-permute-start | bytes 393224 | tf_op jit(solution)/shard_map/cond/branch_3_fun/ppermute | solution.py:327
  29.1 19.5 %collective-permute-start.52 = (f32[256,128]{1,0:T(8,128)S(1)}, f32[256,128]{1,0:T(8,128)S(1)}, u32[]{:S(2)}, u32[]{:S(2)}) collective-permute-start(f32[256,128]{1,0:T(8,128)S(1)} %get-tuple-element.109.piece_ref), channel_id=1, source_target_pairs={{0,0},{1,32},{2,64},{3,96},{4,128},{5,160},{6,192},{7,224},{8,8},{... | collective-permute-start | bytes 393224 | tf_op jit(solution)/shard_map/ppermute | solution.py:303
  31.7 9.7 %collective-permute-start.54 = (f32[64,512]{1,0:T(8,128)S(1)}, f32[64,512]{1,0:T(8,128)S(1)}, u32[]{:S(2)}, u32[]{:S(2)}) collective-permute-start(f32[64,512]{1,0:T(8,128)S(1)} %pick.1), channel_id=1, source_target_pairs={{0,1},{1,0},{2,3},{3,2},{4,5},{5,4},{6,7},{7,6},{8,9},{9,8},{10,11... | collective-permute-start | bytes 393224 | tf_op jit(solution)/shard_map/ppermute | solution.py:303
  31.8 14.5 %collective-permute-start.53 = (f32[1,256,128]{2,1,0:T(8,128)S(1)}, f32[1,256,128]{2,1,0:T(8,128)S(1)}, u32[]{:S(2)}, u32[]{:S(2)}) collective-permute-start(f32[1,256,128]{2,1,0:T(8,128)S(1)} %bitcast.29), channel_id=1, source_target_pairs={{0,128},{1,129},{2,130},{3,131},{4,132},{5,133},{6,134},{7,135},{8... | collective-permute-start | bytes 393224 | tf_op jit(solution)/shard_map/ppermute | solution.py:303
  41.4 4.9 %collective-permute-start.57 = (f32[32,512]{1,0:T(8,128)S(1)}, f32[32,512]{1,0:T(8,128)S(1)}, u32[]{:S(2)}, u32[]{:S(2)}) collective-permute-start(f32[32,512]{1,0:T(8,128)S(1)} %dynamic-slice_select_fusion), channel_id=1, source_target_pairs={{0,8},{1,9},{2,10},{3,11},{4,12},{5,13},{6,14},{7,15},{8,16},{9,17... | collective-permute-start | bytes 196616 | tf_op jit(solution)/shard_map/ppermute | solution.py:303
  42.7 5.4 %collective-permute-start.56 = (f32[32,512]{1,0:T(8,128)S(1)}, f32[32,512]{1,0:T(8,128)S(1)}, u32[]{:S(2)}, u32[]{:S(2)}) collective-permute-start(f32[32,512]{1,0:T(8,128)S(1)} %dynamic-slice_select_fusion), channel_id=1, source_target_pairs={{0,16},{1,17},{2,18},{3,19},{4,20},{5,21},{6,22},{7,23},{8,24},{9,... | collective-permute-start | bytes 196616 | tf_op jit(solution)/shard_map/ppermute | solution.py:303
  45.1 3.4 %collective-permute-start.55 = (f32[32,512]{1,0:T(8,128)S(1)}, f32[32,512]{1,0:T(8,128)S(1)}, u32[]{:S(2)}, u32[]{:S(2)}) collective-permute-start(f32[32,512]{1,0:T(8,128)S(1)} %dynamic-slice_select_fusion), channel_id=1, source_target_pairs={{0,24},{1,25},{2,26},{3,27},{4,28},{5,29},{6,30},{7,31},{8,0},{9,1... | collective-permute-start | bytes 196616 | tf_op jit(solution)/shard_map/ppermute | solution.py:303
  48.6 0.7 copy-start
  49.3 13.1 %collective-permute-start.61 = (f32[32,512]{1,0:T(8,128)S(1)}, f32[32,512]{1,0:T(8,128)S(1)}, u32[]{:S(2)}, u32[]{:S(2)}) collective-permute-start(f32[32,512]{1,0:T(8,128)S(1)} %select_select_fusion.9), channel_id=1, source_target_pairs={{0,2},{1,3},{2,4},{3,5},{4,6},{5,7},{6,0},{7,1},{8,10},{9,11},{10,... | collective-permute-start | bytes 196616 | tf_op jit(solution)/shard_map/ppermute | solution.py:303
  53.4 11.4 %collective-permute-start.60 = (f32[32,512]{1,0:T(8,128)S(1)}, f32[32,512]{1,0:T(8,128)S(1)}, u32[]{:S(2)}, u32[]{:S(2)}) collective-permute-start(f32[32,512]{1,0:T(8,128)S(1)} %select_select_fusion.9), channel_id=1, source_target_pairs={{0,4},{1,5},{2,6},{3,7},{4,0},{5,1},{6,2},{7,3},{8,12},{9,13},{10,... | collective-permute-start | bytes 196616 | tf_op jit(solution)/shard_map/ppermute | solution.py:303
  61.1 3.8 %collective-permute-start.59 = (f32[32,512]{1,0:T(8,128)S(1)}, f32[32,512]{1,0:T(8,128)S(1)}, u32[]{:S(2)}, u32[]{:S(2)}) collective-permute-start(f32[32,512]{1,0:T(8,128)S(1)} %select_select_fusion.9), channel_id=1, source_target_pairs={{0,6},{1,7},{2,0},{3,1},{4,2},{5,3},{6,4},{7,5},{8,14},{9,15},{10,... | collective-permute-start | bytes 196616 | tf_op jit(solution)/shard_map/ppermute | solution.py:303
  61.1 14.7 %collective-permute-start.58 = (f32[2,256,128]{2,1,0:T(8,128)S(1)}, f32[2,256,128]{2,1,0:T(8,128)S(1)}, u32[]{:S(2)}, u32[]{:S(2)}) collective-permute-start(f32[2,256,128]{2,1,0:T(8,128)S(1)} %pad_maximum_fusion.2), channel_id=1, source_target_pairs={{0,64},{1,65},{2,66},{3,67},{4,68},{5,69},{6,70},{7,71},{8,72},{9,... | collective-permute-start | bytes 786440 | tf_op jit(solution)/shard_map/ppermute | solution.py:303
  75.8 7.3 %collective-permute-start.62 = (f32[1,32,512]{2,1,0:T(8,128)S(1)}, f32[1,32,512]{2,1,0:T(8,128)S(1)}, u32[]{:S(2)}, u32[]{:S(2)}) collective-permute-start(f32[1,32,512]{2,1,0:T(8,128)S(1)} %bitcast.31), channel_id=1, source_target_pairs={{0,128},{1,129},{2,130},{3,131},{4,132},{5,133},{6,134},{7,135},{8... | collective-permute-start | bytes 196616 | tf_op jit(solution)/shard_map/ppermute | solution.py:303
  83.1 8.1 %collective-permute-start.63 = (f32[2,32,512]{2,1,0:T(8,128)S(1)}, f32[2,32,512]{2,1,0:T(8,128)S(1)}, u32[]{:S(2)}, u32[]{:S(2)}) collective-permute-start(f32[2,32,512]{2,1,0:T(8,128)S(1)} %pad_maximum_fusion.4), channel_id=1, source_target_pairs={{0,64},{1,65},{2,66},{3,67},{4,68},{5,69},{6,70},{7,71},{8,72},{9,... | collective-permute-start | bytes 393224 | tf_op jit(solution)/shard_map/ppermute | solution.py:303
  91.2 6.4 %collective-permute-start.64 = (f32[4,32,512]{2,1,0:T(8,128)S(1)}, f32[4,32,512]{2,1,0:T(8,128)S(1)}, u32[]{:S(2)}, u32[]{:S(2)}) collective-permute-start(f32[4,32,512]{2,1,0:T(8,128)S(1)} %pad_maximum_fusion.3), channel_id=1, source_target_pairs={{0,32},{1,33},{2,34},{3,35},{4,36},{5,37},{6,38},{7,39},{8,40},{9,... | collective-permute-start | bytes 786440 | tf_op jit(solution)/shard_map/ppermute | solution.py:303
  97.7 4.1 %collective-permute-start.65 = (f32[8,32,512]{2,1,0:T(8,128)S(1)}, f32[8,32,512]{2,1,0:T(8,128)S(1)}, u32[]{:S(2)}, u32[]{:S(2)}) collective-permute-start(f32[8,32,512]{2,1,0:T(8,128)S(1)} %pad_maximum_fusion.1.own_ref), channel_id=1, source_target_pairs={{0,1},{1,0},{2,3},{3,2},{4,5},{5,4},{6,7},{7,6},{8,9},{9,8},{10,11... | collective-permute-start | bytes 1572872 | tf_op jit(solution)/shard_map/ppermute | solution.py:303
  100.2 26.4 %collective-permute-start.66 = (f32[4,256,128]{2,1,0:T(8,128)S(1)}, f32[4,256,128]{2,1,0:T(8,128)S(1)}, u32[]{:S(2)}, u32[]{:S(2)}) collective-permute-start(f32[4,256,128]{2,1,0:T(8,128)S(1)} %pad_maximum_fusion.near_ref), channel_id=1, source_target_pairs={{0,32},{1,33},{2,34},{3,35},{4,36},{5,37},{6,38},{7,39},{8,40},{9,... | collective-permute-start | bytes 1572872 | tf_op jit(solution)/shard_map/ppermute | solution.py:303
Sparse Core Ops, SparseCore 0:
  49.4 57.6 all-gather.2

commit v2 on v1

--- a/solution.py
+++ b/solution.py
@@ -239,50 +239,51 @@
 
 
 def update_kernel(info, w_ref, c_ref, g_ref, a_ref, panels_ref, t_ref):
-    group, t = pl.program_id(0), pl.program_id(1)
-    block = (t * pl.num_programs(0) + group) * PLANES + info[ROW]
-    columns = jnp.concatenate([block_column(g_ref.at[plane], t, CHUNK) for plane in range(PLANES)], axis=0)
-    rows = stacked(columns.T, w_ref[...])
+    group = pl.program_id(0)
     first, second = info[FIRST], info[SECOND]
-    panels_ref[0, 0] = rows[:, :NB]
-    panels_ref[1, 0] = jnp.where(block != first, rows[:, NB:], 0.0)
-    trail = stacked(rows, c_ref[...])
-    row_kept = (block != first) & (block != second)
-    for column in range(2):
-        number = info[COLUMN] + 32 * column
-        kept = row_kept & (number != first) & (number != second)
-        for j in range(2):
-            where = pl.ds(2 * column + j, NB, stride=4)
-            start = column * NB + j * LANES
-            t_ref[0, where, :] = jnp.where(kept, a_ref[0, where, :] - trail[:, start : start + LANES], 0.0)
+    for t in range(2):
+        block = (t * pl.num_programs(0) + group) * PLANES + info[ROW]
+        columns = jnp.concatenate([block_column(g_ref.at[plane], t, CHUNK) for plane in range(PLANES)], axis=0)
+        rows = stacked(columns.T, w_ref[...])
+        row_kept = (block != first) & (block != second)
+        panels_ref[0, t, 0] = rows[:, :NB]
+        panels_ref[1, t, 0] = jnp.where(block != first, rows[:, NB:], 0.0)
+        trail = stacked(rows, c_ref[...])
+        for column in range(2):
+            number = info[COLUMN] + 32 * column
+            kept = row_kept & (number != first) & (number != second)
+            for j in range(2):
+                where = pl.ds(2 * column + j, NB, stride=4)
+                start = column * NB + j * LANES
+                t_ref[t, 0, where, :] = jnp.where(kept, a_ref[t, 0, where, :] - trail[:, start : start + LANES], 0.0)
 
 
 def update(info, factors, gathered, flat):
     br, rows, _ = flat.shape
     groups = gathered.shape[0] // PLANES
-    block = lambda k, t, info: (t * groups + k, 0, 0)
+    block = lambda k, info: (0, k, 0, 0)
     return pl.pallas_call(
         update_kernel,
         grid_spec=pltpu.PrefetchScalarGridSpec(
             num_scalar_prefetch=1,
-            grid=(groups, br // groups),
+            grid=(groups,),
             in_specs=[VMEM] * 2
             + [
-                pl.BlockSpec((PLANES, 4 * CHUNK, LANES), lambda k, t, info: (k, 0, 0)),
-                pl.BlockSpec((1, rows, LANES), block),
+                pl.BlockSpec((PLANES, 4 * CHUNK, LANES), lambda k, info: (k, 0, 0)),
+                pl.BlockSpec((2, 1, rows, LANES), block),
             ],
             out_specs=[
-                pl.BlockSpec((2, 1, NB, NB), lambda k, t, info: (0, t * groups + k, 0, 0)),
-                pl.BlockSpec((1, rows, LANES), block),
+                pl.BlockSpec((2, 2, 1, NB, NB), lambda k, info: (0, 0, k, 0, 0)),
+                pl.BlockSpec((2, 1, rows, LANES), block),
             ],
         ),
         out_shape=[
-            jax.ShapeDtypeStruct((2, br, NB, NB), jnp.float32),
-            jax.ShapeDtypeStruct(flat.shape, jnp.float32),
+            jax.ShapeDtypeStruct((2, 2, groups, NB, NB), jnp.float32),
+            jax.ShapeDtypeStruct((2, groups) + flat.shape[1:], jnp.float32),
         ],
         compiler_params=PARAMS,
         name="update",
-    )(info, *factors, gathered, flat)
+    )(info, *factors, gathered, flat.reshape((2, groups) + flat.shape[1:]))
 
 
 def shards(kernel, pivots):
@@ -322,7 +323,7 @@
                 if q != quarter:
                     plane = 2 * q + parity
                     pairs = line(root, plane)
-                    if quarter < 3:
+                    if quarter in (1, 2):
                         pairs = line(2 * quarter, 2 * q) + line(2 * quarter + 1, 2 * q + 1)
                     arrived.append((plane, lax.ppermute(part(others, q), AXES, pairs)))
             arrived.append((root, part(others, quarter)))
@@ -363,9 +364,10 @@
     gathered = lax.all_gather(moved, "pcol", axis=0, tiled=False)
     crossing = double(crossing, 2)
     mine = spread(mine, ypos, ry, 3, lambda b, d: (b // 8) * 8 + (b + 2 * d) % 8)
-    crossing, mine = tie(crossing, mine)
+    ring = double(double(mine[None], 4), 2)
+    crossing, ring = tie(crossing, ring)
     beyond = send(crossing, lambda a, b: (a ^ 1, b))
-    ring = double(double(double(mine[None], 4), 2), 1)
+    ring = double(ring, 1)
     factors = cross(info, factor(info, ring, core_twin(ring)), crossing, beyond)
     panels, trailing = update(info, factors, gathered, flat)
     return panels.reshape(2, br, 1, NB, NB), trailing.reshape(kernel.shape)

time: 149 us -> 145 us (0.973)
  waiting for transfers between devices: 44.3 us -> 34.1 us
  starting transfers between devices: 41 us -> 48.2 us
  Pallas kernels: 41.4 us -> 39.5 us
    ppermute x15, waiting for transfers between devices: 35.9 us -> 25.4 us  [shards(): lax.ppermute(value, AXES, [(device(a, b), device(*to(a, b))) for a, b in...]
    ppermute x15, starting transfers between devices: 35.1 us -> 43.5 us  [shards(): lax.ppermute(value, AXES, [(device(a, b), device(*to(a, b))) for a, b in...]
    ppermute x3, waiting for transfers between devices: 2.14 us -> 8.68 us  [run(): arrived.append((plane, lax.ppermute(part(others, q), AXES, pairs)))]
    ppermute x4 -> x3, waiting for transfers between devices: 6.24 us -> 0.01 us  [run(): lax.ppermute(part(newest, q), AXES, line(height - 1, plane))]
    pallas_call x1, Pallas kernels: 13.7 us -> 11.8 us  [update(): pl.pallas_call(update_kernel, grid_spec=pltpu.PrefetchScalarGridSpec(num_...]
    ppermute x4 -> x3, starting transfers between devices: 3.3 us -> 2.01 us  [run(): lax.ppermute(part(newest, q), AXES, line(height - 1, plane))]
  transfers between devices with their start and end apart: 23 -> 22, of which waited for: 11 -> 7; matrix products, arithmetic and copies ran while one was open for 0% -> 0% of each run, Pallas kernels for 19% -> 19%
where the time goes in v2:
time: 145 us; the launch traced here: 144 us
  starting transfers between devices  48.2 us (33%)
  Pallas kernels  39.5 us (27%)
  waiting for transfers between devices  34.1 us (24%)
  between operations  16.2 us (11%)
  local copies, waits for them, and re-layouts  5.54 us (4%)
    ppermute x15, starting transfers between devices, shards(): lax.ppermute(value, AXES, [(device(a, b), device(*to(a, b))) for a, b in...  43.5 us
    ppermute x15, waiting for transfers between devices, shards(): lax.ppermute(value, AXES, [(device(a, b), device(*to(a, b))) for a, b in...  25.4 us
    pallas_call x1, Pallas kernels, factor(): pl.pallas_call(factor_kernel, out_shape=jax.ShapeDtypeStruct((n, n), jnp....  24.9 us
    pallas_call x1, Pallas kernels, update(): pl.pallas_call(update_kernel, grid_spec=pltpu.PrefetchScalarGridSpec(num_...  11.8 us
    ppermute x3, waiting for transfers between devices, run(): arrived.append((plane, lax.ppermute(part(others, q), AXES, pairs)))  8.68 us
  transfers between devices with their start and end apart: 22, of which 7 were waited for; matrix products, arithmetic and copies ran while one was open for 0% of the time, Pallas kernels for 19%

profile of v2, /device:TPU:1, one launch (start us, length us, event | category | flops | bytes accessed | tf_op | source)
XLA Modules:
  0.0 144.5 jit_solution(414479413460621157)
XLA Ops:
  7.2 0.0 all-gather.3.cloned.1.call-start
  7.2 1.3 fusion.17
  10.4 1.4 slice.221
  11.8 1.1 dynamic-slice_bitcast_fusion
  12.9 0.0 copy-start.1
  12.9 15.1 %conditional.1 = (f32[256,128]{1,0:T(8,128)}, f32[256,128]{1,0:T(8,128)S(1)}) conditional(s32[]{:T(128)} %clamp.3, (s32[]{:T(128)}, f32[1024,128]{1,0:T(8,128)S(1)}, f32[1024,128]{1,0:T(8,128)S(1)}) %tuple.150, (s32[]{:T(128)}, f32[1024,128]{1,0:T(8,128)S(1)}, f32[1024,128]{1,0:T(8,128)S(1)}) %tuple.154, (s32[]{:T(128)}, ...), branch_computations={%region_0.1_spmd, %region_1.2_spmd, %region_2.3_spmd, %region_3.4_... | conditional | flops 229383 | bytes 6947182 | solution.py:341
  13.0 0.7 collective-permute-start.31
  13.7 0.7 collective-permute-start.29
  14.4 0.7 collective-permute-start.27
  15.1 1.3 collective-permute-start.30
  16.4 0.7 collective-permute-start.28
  17.0 0.0 collective-permute-done.31
  17.1 0.7 collective-permute-start.26
  17.8 0.0 collective-permute-done.29
  17.8 0.0 collective-permute-done.27
  17.8 8.7 %collective-permute-done.30 = f32[256,128]{1,0:T(8,128)S(1)} collective-permute-done((f32[256,128]{1,0:T(8,128)S(1)}, f32[256,128]{1,0:T(8,128)S(1)}, u32[]{:S(2)}, u32[]{:S(2)}) %collective-permute-start.30) | collective-permute-done | bytes 131104 | tf_op jit(solution)/shard_map/cond/branch_4_fun/ppermute | solution.py:328
  26.4 0.7 select_select_fusion.4
  27.2 0.9 copy.15
  28.1 8.9 %collective-permute-start.52 = (f32[256,128]{1,0:T(8,128)S(1)}, f32[256,128]{1,0:T(8,128)S(1)}, u32[]{:S(2)}, u32[]{:S(2)}) collective-permute-start(f32[256,128]{1,0:T(8,128)S(1)} %get-tuple-element.109.piece_ref), channel_id=1, source_target_pairs={{0,0},{1,32},{2,64},{3,96},{4,128},{5,160},{6,192},{7,224},{8,8},{... | collective-permute-start | bytes 393224 | tf_op jit(solution)/shard_map/ppermute | solution.py:304
  37.0 0.1 stack.27.info
  37.1 0.6 pick.1
  37.7 0.1 collective-permute-start.54
  37.8 6.9 %collective-permute-start.53 = (f32[1,256,128]{2,1,0:T(8,128)S(1)}, f32[1,256,128]{2,1,0:T(8,128)S(1)}, u32[]{:S(2)}, u32[]{:S(2)}) collective-permute-start(f32[1,256,128]{2,1,0:T(8,128)S(1)} %bitcast.31), channel_id=1, source_target_pairs={{0,128},{1,129},{2,130},{3,131},{4,132},{5,133},{6,134},{7,135},{8... | collective-permute-start | bytes 393224 | tf_op jit(solution)/shard_map/ppermute | solution.py:304
  44.7 1.3 collective-permute-start.57
  46.0 2.5 %collective-permute-start.56 = (f32[32,512]{1,0:T(8,128)S(1)}, f32[32,512]{1,0:T(8,128)S(1)}, u32[]{:S(2)}, u32[]{:S(2)}) collective-permute-start(f32[32,512]{1,0:T(8,128)S(1)} %dynamic-slice_select_fusion), channel_id=1, source_target_pairs={{0,16},{1,17},{2,18},{3,19},{4,20},{5,21},{6,22},{7,23},{8,24},{9,... | collective-permute-start | bytes 196616 | tf_op jit(solution)/shard_map/ppermute | solution.py:304
  48.5 1.2 collective-permute-start.55
  49.7 1.4 collective-permute-done.56
  51.1 1.1 collective-permute-done.55
  52.2 0.0 copy-start
  52.2 0.6 copy-done
  52.8 0.0 all-gather.3.cloned.1.call-update
  52.9 3.6 %collective-permute-start.61 = (f32[32,512]{1,0:T(8,128)S(1)}, f32[32,512]{1,0:T(8,128)S(1)}, u32[]{:S(2)}, u32[]{:S(2)}) collective-permute-start(f32[32,512]{1,0:T(8,128)S(1)} %select_select_fusion.8), channel_id=1, source_target_pairs={{0,2},{1,3},{2,4},{3,5},{4,6},{5,7},{6,0},{7,1},{8,10},{9,11},{10,... | collective-permute-start | bytes 196616 | tf_op jit(solution)/shard_map/ppermute | solution.py:304
  56.5 1.7 %collective-permute-start.60 = (f32[32,512]{1,0:T(8,128)S(1)}, f32[32,512]{1,0:T(8,128)S(1)}, u32[]{:S(2)}, u32[]{:S(2)}) collective-permute-start(f32[32,512]{1,0:T(8,128)S(1)} %select_select_fusion.8), channel_id=1, source_target_pairs={{0,4},{1,5},{2,6},{3,7},{4,0},{5,1},{6,2},{7,3},{8,12},{9,13},{10,... | collective-permute-start | bytes 196616 | tf_op jit(solution)/shard_map/ppermute | solution.py:304
  58.2 0.8 collective-permute-start.59
  59.0 2.5 %collective-permute-done.60 = f32[32,512]{1,0:T(8,128)S(1)} collective-permute-done((f32[32,512]{1,0:T(8,128)S(1)}, f32[32,512]{1,0:T(8,128)S(1)}, u32[]{:S(2)}, u32[]{:S(2)}) %collective-permute-start.60) | collective-permute-done | bytes 65568 | tf_op jit(solution)/shard_map/ppermute | solution.py:304
  61.5 3.4 %collective-permute-start.62 = (f32[1,32,512]{2,1,0:T(8,128)S(1)}, f32[1,32,512]{2,1,0:T(8,128)S(1)}, u32[]{:S(2)}, u32[]{:S(2)}) collective-permute-start(f32[1,32,512]{2,1,0:T(8,128)S(1)} %select_bitcast_fusion), channel_id=1, source_target_pairs={{0,128},{1,129},{2,130},{3,131},{4,132},{5,133},{6,134},{7,135},{8... | collective-permute-start | bytes 196616 | tf_op jit(solution)/shard_map/ppermute | solution.py:304
  64.9 3.9 %collective-permute-start.58 = (f32[2,256,128]{2,1,0:T(8,128)S(1)}, f32[2,256,128]{2,1,0:T(8,128)S(1)}, u32[]{:S(2)}, u32[]{:S(2)}) collective-permute-start(f32[2,256,128]{2,1,0:T(8,128)S(1)} %pad_maximum_fusion.1), channel_id=1, source_target_pairs={{0,64},{1,65},{2,66},{3,67},{4,68},{5,69},{6,70},{7,71},{8,72},{9,... | collective-permute-start | bytes 786440 | tf_op jit(solution)/shard_map/ppermute | solution.py:304
  68.8 7.8 %collective-permute-start.63 = (f32[2,32,512]{2,1,0:T(8,128)S(1)}, f32[2,32,512]{2,1,0:T(8,128)S(1)}, u32[]{:S(2)}, u32[]{:S(2)}) collective-permute-start(f32[2,32,512]{2,1,0:T(8,128)S(1)} %pad_maximum_fusion.3), channel_id=1, source_target_pairs={{0,64},{1,65},{2,66},{3,67},{4,68},{5,69},{6,70},{7,71},{8,72},{9,... | collective-permute-start | bytes 393224 | tf_op jit(solution)/shard_map/ppermute | solution.py:304
  76.6 11.4 %collective-permute-done.63 = f32[2,32,512]{2,1,0:T(8,128)S(1)} collective-permute-done((f32[2,32,512]{2,1,0:T(8,128)S(1)}, f32[2,32,512]{2,1,0:T(8,128)S(1)}, u32[]{:S(2)}, u32[]{:S(2)}) %collective-permute-start.63) | collective-permute-done | bytes 131104 | tf_op jit(solution)/shard_map/ppermute | solution.py:304
  88.2 0.1 collective-permute-start.64
  88.3 7.4 %collective-permute-done.64 = f32[4,32,512]{2,1,0:T(8,128)S(1)} collective-permute-done((f32[4,32,512]{2,1,0:T(8,128)S(1)}, f32[4,32,512]{2,1,0:T(8,128)S(1)}, u32[]{:S(2)}, u32[]{:S(2)}) %collective-permute-start.64) | collective-permute-done | bytes 262176 | tf_op jit(solution)/shard_map/ppermute | solution.py:304
  95.8 1.3 collective-permute-start.65
  97.1 0.0 collective-permute-start.66
  97.1 1.5 %collective-permute-done.65.twin_ref = f32[8,32,512]{2,1,0:T(8,128)S(1)} collective-permute-done((f32[8,32,512]{2,1,0:T(8,128)S(1)}, f32[8,32,512]{2,1,0:T(8,128)S(1)}, u32[]{:S(2)}, u32[]{:S(2)}) %collective-permute-start.65) | collective-permute-done | bytes 524320 | tf_op jit(solution)/shard_map/ppermute | solution.py:304
  98.6 24.9 %factor.1.m_ref = f32[512,512]{1,0:T(8,128)S(1)} custom-call(s32[7]{0:T(128)S(1)} %stack.27.info, f32[8,32,512]{2,1,0:T(8,128)S(1)} %constant_dynamic-update-slice_fusion.own_ref, f32[8,32,512]{2,1,0:T(8,128)S(1)} %collective-permute-done.65.twin_ref), custom_call_target="tpu_custom_call" | custom-call | flops 1000000000 | bytes 90000000 | tf_op jit(solution)/shard_map/factor/pallas_call | solution.py:200
  123.5 2.2 %cross.1 = (bf16[1536,512]{1,0:T(8,128)(2,1)S(1)}, bf16[1536,512]{1,0:T(8,128)(2,1)S(1)}) custom-call(s32[7]{0:T(128)S(1)} %stack.27.info, f32[512,512]{1,0:T(8,128)S(1)} %factor.1.m_ref, f32[4,256,128]{2,1,0:T(8,128)S(1)} %pad_maximum_fusion.near_ref, f32[4,256,128]{2,1,0:T(8,128)S(1)} %collective-permute-done.66.far_ref), custom_call_target="tpu_custom_call" | custom-call | tf_op jit(solution)/shard_map/cross/pallas_call | solution.py:230
  125.7 0.0 all-gather.3.cloned.1.call-done
  125.8 11.8 %update.1 = (f32[2,2,4,256,256]{4,3,2,1,0:T(8,128)}, f32[2,4,1024,128]{3,2,1,0:T(8,128)}) custom-call(s32[7]{0:T(128)S(1)} %stack.27.info, bf16[1536,512]{1,0:T(8,128)(2,1)S(1)} %get-tuple-element.100.w_ref, bf16[1536,512]{1,0:T(8,128)(2,1)S(1)} %get-tuple-element.101.c_ref, f32[32,256,128]{2,1,0:T(8,128)} %bitcast.30, f32[2,4,1024,128]{3,2,1,0:T(8,128)} %bitcast.29), custom_call_target="tpu_custom_call" | custom-call | tf_op jit(solution)/shard_map/update/pallas_call | solution.py:265
  (28 shorter events, 0.3 us)
Async XLA Ops:
  7.2 118.6 %all-gather.3.cloned.1.call-start = ((), (), s32[]{:S(2)}) async-start(), calls=%async_computation | async-start | bytes 4325376 | tf_op jit(solution)/shard_map/all_gather | solution.py:364
  12.9 24.1 %copy-start.1 = (s32[2]{0:T(128)S(1)}, s32[2]{0:T(128)}, u32[]{:S(2)}) copy-start(s32[2]{0:T(128)} %param.11) | copy-start | bytes 28
  13.0 4.0 %collective-permute-start.31 = (f32[256,128]{1,0:T(8,128)S(1)}, f32[256,128]{1,0:T(8,128)S(1)}, u32[]{:S(2)}, u32[]{:S(2)}) collective-permute-start(f32[256,128]{1,0:T(8,128)S(1)} %get-tuple-element.136), channel_id=1, source_target_pairs={{224,32},{225,33},{226,34},{227,35},{228,36},{229,37},{230,38},{23... | collective-permute-start | bytes 393224 | tf_op jit(solution)/shard_map/cond/branch_4_fun/ppermute | solution.py:322
  13.7 4.1 %collective-permute-start.29 = (f32[256,128]{1,0:T(8,128)S(1)}, f32[256,128]{1,0:T(8,128)S(1)}, u32[]{:S(2)}, u32[]{:S(2)}) collective-permute-start(f32[256,128]{1,0:T(8,128)S(1)} %get-tuple-element.137), channel_id=1, source_target_pairs={{224,96},{225,97},{226,98},{227,99},{228,100},{229,101},{230,102},... | collective-permute-start | bytes 393224 | tf_op jit(solution)/shard_map/cond/branch_4_fun/ppermute | solution.py:322
  14.4 3.4 %collective-permute-start.27 = (f32[256,128]{1,0:T(8,128)S(1)}, f32[256,128]{1,0:T(8,128)S(1)}, u32[]{:S(2)}, u32[]{:S(2)}) collective-permute-start(f32[256,128]{1,0:T(8,128)S(1)} %get-tuple-element.138), channel_id=1, source_target_pairs={{224,160},{225,161},{226,162},{227,163},{228,164},{229,165},{230,1... | collective-permute-start | bytes 393224 | tf_op jit(solution)/shard_map/cond/branch_4_fun/ppermute | solution.py:322
  15.1 11.4 %collective-permute-start.30 = (f32[256,128]{1,0:T(8,128)S(1)}, f32[256,128]{1,0:T(8,128)S(1)}, u32[]{:S(2)}, u32[]{:S(2)}) collective-permute-start(f32[256,128]{1,0:T(8,128)S(1)} %get-tuple-element.139), channel_id=1, source_target_pairs={{128,0},{129,1},{130,2},{131,3},{132,4},{133,5},{134,6},{135,7},{1... | collective-permute-start | bytes 393224 | tf_op jit(solution)/shard_map/cond/branch_4_fun/ppermute | solution.py:328
  16.4 10.1 %collective-permute-start.28 = (f32[256,128]{1,0:T(8,128)S(1)}, f32[256,128]{1,0:T(8,128)S(1)}, u32[]{:S(2)}, u32[]{:S(2)}) collective-permute-start(f32[256,128]{1,0:T(8,128)S(1)} %get-tuple-element.140), channel_id=1, source_target_pairs={{128,64},{129,65},{130,66},{131,67},{132,68},{133,69},{134,70},{13... | collective-permute-start | bytes 393224 | tf_op jit(solution)/shard_map/cond/branch_4_fun/ppermute | solution.py:328
  17.1 9.4 %collective-permute-start.26 = (f32[256,128]{1,0:T(8,128)S(1)}, f32[256,128]{1,0:T(8,128)S(1)}, u32[]{:S(2)}, u32[]{:S(2)}) collective-permute-start(f32[256,128]{1,0:T(8,128)S(1)} %get-tuple-element.141), channel_id=1, source_target_pairs={{128,192},{129,193},{130,194},{131,195},{132,196},{133,197},{134,1... | collective-permute-start | bytes 393224 | tf_op jit(solution)/shard_map/cond/branch_4_fun/ppermute | solution.py:328
  28.1 24.1 %collective-permute-start.52 = (f32[256,128]{1,0:T(8,128)S(1)}, f32[256,128]{1,0:T(8,128)S(1)}, u32[]{:S(2)}, u32[]{:S(2)}) collective-permute-start(f32[256,128]{1,0:T(8,128)S(1)} %get-tuple-element.109.piece_ref), channel_id=1, source_target_pairs={{0,0},{1,32},{2,64},{3,96},{4,128},{5,160},{6,192},{7,224},{8,8},{... | collective-permute-start | bytes 393224 | tf_op jit(solution)/shard_map/ppermute | solution.py:304
  37.7 7.0 %collective-permute-start.54 = (f32[64,512]{1,0:T(8,128)S(1)}, f32[64,512]{1,0:T(8,128)S(1)}, u32[]{:S(2)}, u32[]{:S(2)}) collective-permute-start(f32[64,512]{1,0:T(8,128)S(1)} %pick.1), channel_id=1, source_target_pairs={{0,1},{1,0},{2,3},{3,2},{4,5},{5,4},{6,7},{7,6},{8,9},{9,8},{10,11... | collective-permute-start | bytes 393224 | tf_op jit(solution)/shard_map/ppermute | solution.py:304
  37.8 11.9 %collective-permute-start.53 = (f32[1,256,128]{2,1,0:T(8,128)S(1)}, f32[1,256,128]{2,1,0:T(8,128)S(1)}, u32[]{:S(2)}, u32[]{:S(2)}) collective-permute-start(f32[1,256,128]{2,1,0:T(8,128)S(1)} %bitcast.31), channel_id=1, source_target_pairs={{0,128},{1,129},{2,130},{3,131},{4,132},{5,133},{6,134},{7,135},{8... | collective-permute-start | bytes 393224 | tf_op jit(solution)/shard_map/ppermute | solution.py:304
  44.7 4.9 %collective-permute-start.57 = (f32[32,512]{1,0:T(8,128)S(1)}, f32[32,512]{1,0:T(8,128)S(1)}, u32[]{:S(2)}, u32[]{:S(2)}) collective-permute-start(f32[32,512]{1,0:T(8,128)S(1)} %dynamic-slice_select_fusion), channel_id=1, source_target_pairs={{0,8},{1,9},{2,10},{3,11},{4,12},{5,13},{6,14},{7,15},{8,16},{9,17... | collective-permute-start | bytes 196616 | tf_op jit(solution)/shard_map/ppermute | solution.py:304
  46.0 5.0 %collective-permute-start.56 = (f32[32,512]{1,0:T(8,128)S(1)}, f32[32,512]{1,0:T(8,128)S(1)}, u32[]{:S(2)}, u32[]{:S(2)}) collective-permute-start(f32[32,512]{1,0:T(8,128)S(1)} %dynamic-slice_select_fusion), channel_id=1, source_target_pairs={{0,16},{1,17},{2,18},{3,19},{4,20},{5,21},{6,22},{7,23},{8,24},{9,... | collective-permute-start | bytes 196616 | tf_op jit(solution)/shard_map/ppermute | solution.py:304
  48.5 3.7 %collective-permute-start.55 = (f32[32,512]{1,0:T(8,128)S(1)}, f32[32,512]{1,0:T(8,128)S(1)}, u32[]{:S(2)}, u32[]{:S(2)}) collective-permute-start(f32[32,512]{1,0:T(8,128)S(1)} %dynamic-slice_select_fusion), channel_id=1, source_target_pairs={{0,24},{1,25},{2,26},{3,27},{4,28},{5,29},{6,30},{7,31},{8,0},{9,1... | collective-permute-start | bytes 196616 | tf_op jit(solution)/shard_map/ppermute | solution.py:304
  52.2 0.7 copy-start
  52.9 6.2 %collective-permute-start.61 = (f32[32,512]{1,0:T(8,128)S(1)}, f32[32,512]{1,0:T(8,128)S(1)}, u32[]{:S(2)}, u32[]{:S(2)}) collective-permute-start(f32[32,512]{1,0:T(8,128)S(1)} %select_select_fusion.8), channel_id=1, source_target_pairs={{0,2},{1,3},{2,4},{3,5},{4,6},{5,7},{6,0},{7,1},{8,10},{9,11},{10,... | collective-permute-start | bytes 196616 | tf_op jit(solution)/shard_map/ppermute | solution.py:304
  56.5 5.0 %collective-permute-start.60 = (f32[32,512]{1,0:T(8,128)S(1)}, f32[32,512]{1,0:T(8,128)S(1)}, u32[]{:S(2)}, u32[]{:S(2)}) collective-permute-start(f32[32,512]{1,0:T(8,128)S(1)} %select_select_fusion.8), channel_id=1, source_target_pairs={{0,4},{1,5},{2,6},{3,7},{4,0},{5,1},{6,2},{7,3},{8,12},{9,13},{10,... | collective-permute-start | bytes 196616 | tf_op jit(solution)/shard_map/ppermute | solution.py:304
  58.2 3.3 %collective-permute-start.59 = (f32[32,512]{1,0:T(8,128)S(1)}, f32[32,512]{1,0:T(8,128)S(1)}, u32[]{:S(2)}, u32[]{:S(2)}) collective-permute-start(f32[32,512]{1,0:T(8,128)S(1)} %select_select_fusion.8), channel_id=1, source_target_pairs={{0,6},{1,7},{2,0},{3,1},{4,2},{5,3},{6,4},{7,5},{8,14},{9,15},{10,... | collective-permute-start | bytes 196616 | tf_op jit(solution)/shard_map/ppermute | solution.py:304
  61.5 7.2 %collective-permute-start.62 = (f32[1,32,512]{2,1,0:T(8,128)S(1)}, f32[1,32,512]{2,1,0:T(8,128)S(1)}, u32[]{:S(2)}, u32[]{:S(2)}) collective-permute-start(f32[1,32,512]{2,1,0:T(8,128)S(1)} %select_bitcast_fusion), channel_id=1, source_target_pairs={{0,128},{1,129},{2,130},{3,131},{4,132},{5,133},{6,134},{7,135},{8... | collective-permute-start | bytes 196616 | tf_op jit(solution)/shard_map/ppermute | solution.py:304
  64.9 23.2 %collective-permute-start.58 = (f32[2,256,128]{2,1,0:T(8,128)S(1)}, f32[2,256,128]{2,1,0:T(8,128)S(1)}, u32[]{:S(2)}, u32[]{:S(2)}) collective-permute-start(f32[2,256,128]{2,1,0:T(8,128)S(1)} %pad_maximum_fusion.1), channel_id=1, source_target_pairs={{0,64},{1,65},{2,66},{3,67},{4,68},{5,69},{6,70},{7,71},{8,72},{9,... | collective-permute-start | bytes 786440 | tf_op jit(solution)/shard_map/ppermute | solution.py:304
  68.8 19.3 %collective-permute-start.63 = (f32[2,32,512]{2,1,0:T(8,128)S(1)}, f32[2,32,512]{2,1,0:T(8,128)S(1)}, u32[]{:S(2)}, u32[]{:S(2)}) collective-permute-start(f32[2,32,512]{2,1,0:T(8,128)S(1)} %pad_maximum_fusion.3), channel_id=1, source_target_pairs={{0,64},{1,65},{2,66},{3,67},{4,68},{5,69},{6,70},{7,71},{8,72},{9,... | collective-permute-start | bytes 393224 | tf_op jit(solution)/shard_map/ppermute | solution.py:304
  88.2 7.6 %collective-permute-start.64 = (f32[4,32,512]{2,1,0:T(8,128)S(1)}, f32[4,32,512]{2,1,0:T(8,128)S(1)}, u32[]{:S(2)}, u32[]{:S(2)}) collective-permute-start(f32[4,32,512]{2,1,0:T(8,128)S(1)} %pad_maximum_fusion.2), channel_id=1, source_target_pairs={{0,32},{1,33},{2,34},{3,35},{4,36},{5,37},{6,38},{7,39},{8,40},{9,... | collective-permute-start | bytes 786440 | tf_op jit(solution)/shard_map/ppermute | solution.py:304
  95.8 2.9 %collective-permute-start.65 = (f32[8,32,512]{2,1,0:T(8,128)S(1)}, f32[8,32,512]{2,1,0:T(8,128)S(1)}, u32[]{:S(2)}, u32[]{:S(2)}) collective-permute-start(f32[8,32,512]{2,1,0:T(8,128)S(1)} %constant_dynamic-update-slice_fusion.own_ref), channel_id=1, source_target_pairs={{0,1},{1,0},{2,3},{3,2},{4,5},{5,4},{6,7},{7,6},{8,9},{9,8},{10,11... | collective-permute-start | bytes 1572872 | tf_op jit(solution)/shard_map/ppermute | solution.py:304
  97.1 26.4 %collective-permute-start.66 = (f32[4,256,128]{2,1,0:T(8,128)S(1)}, f32[4,256,128]{2,1,0:T(8,128)S(1)}, u32[]{:S(2)}, u32[]{:S(2)}) collective-permute-start(f32[4,256,128]{2,1,0:T(8,128)S(1)} %pad_maximum_fusion.near_ref), channel_id=1, source_target_pairs={{0,32},{1,33},{2,34},{3,35},{4,36},{5,37},{6,38},{7,39},{8,40},{9,... | collective-permute-start | bytes 1572872 | tf_op jit(solution)/shard_map/ppermute | solution.py:304
Sparse Core Ops, SparseCore 0:
  53.0 53.6 all-gather.2

commit v3 on v2

--- a/solution.py
+++ b/solution.py
@@ -183,7 +183,7 @@
     )(info, piece)
 
 
-def factor_kernel(info, own_ref, twin_ref, m_ref, s_ref, z_ref):
+def first_kernel(info, own_ref, twin_ref, m_ref, w_ref, rest_ref, d_ref, s_ref, z_ref):
     flip = info[FLIPPED] == 1
     core = info[COLUMN] % 2
     for slot in range(PLANES):
@@ -191,51 +191,75 @@
         for ref, side in ((own_ref, core), (twin_ref, 1 - core)):
             v = ref[slot]
             v = jnp.where(flip, jnp.concatenate([v[:, NB:], v[:, :NB]], axis=1), v)
-            s_ref[pl.ds(pl.multiple_of(base + side * HALF, HALF), HALF), :] = v
+            d_ref[pl.ds(pl.multiple_of(base + side * HALF, HALF), HALF), :] = v
+    s_ref[...] = d_ref[:NB, :NB]
     factor_inverse(s_ref, z_ref, m_ref)
-
-
-def factor(info, own, twin):
-    n = 2 * NB
+    inverse = split(m_ref[...])
+    below = split(dot3(split(d_ref[NB:, :NB]), inverse, ((1,), (1,))))
+    rest_ref[...] = d_ref[NB:, NB:] - dot3(below, below, ((1,), (1,)))
+    w_ref[...] = dot3(below, inverse)
+
+
+def second_kernel(w_ref, rest_ref, m_ref, corner_ref, s_ref, z_ref):
+    s_ref[...] = rest_ref[...]
+    factor_inverse(s_ref, z_ref, m_ref)
+    corner_ref[...] = -product(m_ref[...], w_ref[...])
+
+
+def stage(kernel, name, inputs, outputs, scratch):
+    square = lambda: jax.ShapeDtypeStruct((NB, NB), jnp.float32)
     return pl.pallas_call(
-        factor_kernel,
-        out_shape=jax.ShapeDtypeStruct((n, n), jnp.float32),
-        in_specs=[SMEM, VMEM, VMEM],
-        out_specs=VMEM,
-        scratch_shapes=[pltpu.VMEM((n, n), jnp.float32)] * 2,
+        kernel,
+        out_shape=[square() for _ in range(outputs)],
+        in_specs=inputs,
+        out_specs=[VMEM] * outputs,
+        scratch_shapes=scratch + [pltpu.VMEM((NB, NB), jnp.float32)] * 2,
         compiler_params=PARAMS,
-        cost_estimate=pl.CostEstimate(flops=10**9, transcendentals=0, bytes_accessed=9 * 10**7),
-        name="factor",
-    )(info, own, twin)
-
-
-def cross_kernel(info, m_ref, near_ref, far_ref, w_ref, c_ref, t_ref, x_ref):
-    t_ref[...] = m_ref[...].T
+        cost_estimate=pl.CostEstimate(flops=10**8, transcendentals=0, bytes_accessed=4 * 10**7),
+        name=name,
+    )
+
+
+def first_factor(info, own, twin):
+    whole = [pltpu.VMEM((2 * NB, 2 * NB), jnp.float32)]
+    return stage(first_kernel, "first", [SMEM, VMEM, VMEM], 3, whole)(info, own, twin)
+
+
+def second_factor(carried, rest):
+    return stage(second_kernel, "second", [VMEM, VMEM], 2, [])(carried, rest)
+
+
+def cross_kernel(info, first_ref, second_ref, corner_ref, near_ref, far_ref, w_ref, c_ref, t_ref, x_ref):
+    t_ref[:NB, :NB] = first_ref[...].T
+    t_ref[:NB, NB:] = corner_ref[...].T
+    t_ref[NB:, :NB] = jnp.zeros((NB, NB), jnp.float32)
+    t_ref[NB:, NB:] = second_ref[...].T
     for plane in range(PLANES):
         start = pl.multiple_of(place_of(info, plane) * CHUNK, CHUNK)
         x_ref[plane * CHUNK : (plane + 1) * CHUNK, :] = t_ref[pl.ds(start, CHUNK), :]
     weights = split(x_ref[...])
     w_ref[...] = stack(weights)
-    weights = weights[0].T, weights[1].T
+    high, low = weights[0].T, weights[1].T
     for slot in range(PLANES):
         ref = (near_ref, far_ref)[slot // 4].at[slot % 4]
         start = pl.multiple_of((info[ROW] ^ MASKS[slot]) * CHUNK, CHUNK)
         for column in range(2):
             x_ref[pl.ds(start, CHUNK), column * NB : (column + 1) * NB] = block_column(ref, column, CHUNK)
-    c_ref[...] = stack(split(dot3(weights, split(x_ref[...]))))
-
-
-def cross(info, inverse, near, far):
+    rows = jnp.concatenate([high, high, low], axis=1)
+    c_ref[...] = stack(split(jnp.dot(rows, stack(split(x_ref[...])), preferred_element_type=jnp.float32)))
+
+
+def cross(info, first, second, corner, near, far):
     n = 2 * NB
     return pl.pallas_call(
         cross_kernel,
         out_shape=[jax.ShapeDtypeStruct((3 * n, n), jnp.bfloat16)] * 2,
-        in_specs=[SMEM] + [VMEM] * 3,
+        in_specs=[SMEM] + [VMEM] * 5,
         out_specs=[VMEM] * 2,
         scratch_shapes=[pltpu.VMEM((n, n), jnp.float32)] * 2,
         compiler_params=PARAMS,
         name="cross",
-    )(info, inverse, near, far)
+    )(info, first, second, corner, near, far)
 
 
 def update_kernel(info, w_ref, c_ref, g_ref, a_ref, panels_ref, t_ref):
@@ -353,22 +377,25 @@
     side = side[:HALF]
 
     def spread(value, position, goal, last, shift):
-        source = jnp.where(side, (position - goal) & 3, (position - last) & 3)
+        source = jnp.where(side, position ^ goal, position ^ last)
         out = value
         for d in range(1, 4):
-            out = jnp.where(source == d, send(value, lambda a, b: (a, shift(b, d))), out)
+            out = jnp.where(source == d, send(value, lambda a, b: (a, b ^ (d << shift))), out)
         return out
 
-    mine = spread(mine, xpos, rx, 3, lambda b, d: (b + 8 * d) % 32)
+    mine = spread(mine, xpos, rx, 3, 3)
     moved, crossing, mine = tie(moved, crossing, mine)
     gathered = lax.all_gather(moved, "pcol", axis=0, tiled=False)
-    crossing = double(crossing, 2)
-    mine = spread(mine, ypos, ry, 3, lambda b, d: (b // 8) * 8 + (b + 2 * d) % 8)
-    ring = double(double(mine[None], 4), 2)
+    mine = spread(mine, ypos, ry, 3, 1)
+    ring = double(double(double(mine[None], 4), 2), 1)
     crossing, ring = tie(crossing, ring)
+    facing = send(crossing, lambda a, b: (a ^ 2, b))
+    first, carried, rest = first_factor(info, ring, core_twin(ring))
+    crossing, facing, carried, rest = tie(crossing, facing, carried, rest)
+    crossing = jnp.concatenate([crossing, facing], axis=0)
     beyond = send(crossing, lambda a, b: (a ^ 1, b))
-    ring = double(ring, 1)
-    factors = cross(info, factor(info, ring, core_twin(ring)), crossing, beyond)
+    second, corner = second_factor(carried, rest)
+    factors = cross(info, first, second, corner, crossing, beyond)
     panels, trailing = update(info, factors, gathered, flat)
     return panels.reshape(2, br, 1, NB, NB), trailing.reshape(kernel.shape)
 

time: 145 us -> 137 us (0.945); the launches traced: 144 us -> 139 us
  starting transfers between devices: 48.2 us -> 44.2 us
  Pallas kernels: 39.5 us -> 37.9 us
    ppermute x3, waiting for transfers between devices: 8.68 us -> 0.01 us  [run(): arrived.append((plane, lax.ppermute(part(others, q), AXES, pairs)))]
    ppermute x3 -> x4, waiting for transfers between devices: 0.01 us -> 6.87 us  [run(): lax.ppermute(part(newest, q), AXES, line(height - 1, plane))]
    ppermute x15, starting transfers between devices: 43.5 us -> 38.9 us  [shards(): lax.ppermute(value, AXES, [(device(a, b), device(*to(a, b))) for a, b in...]
    ppermute x15, waiting for transfers between devices: 25.4 us -> 27.3 us  [shards(): lax.ppermute(value, AXES, [(device(a, b), device(*to(a, b))) for a, b in...]
    pallas_call x1 -> x2, Pallas kernels: 24.9 us -> 23.3 us  [the longest x1 12.2 us: first_factor(): stage(first_kernel, 'first', [SMEM, VMEM, VMEM], 3, whole)(info, own, twin)]
    ppermute x3 -> x4, starting transfers between devices: 2.01 us -> 3.3 us  [run(): lax.ppermute(part(newest, q), AXES, line(height - 1, plane))]
  transfers between devices with their start and end apart: 22 -> 23, of which waited for: 7 -> 9; matrix products, arithmetic and copies ran while one was open for 0% -> 0% of each run, Pallas kernels for 19% -> 19%
where the time goes in v3:
time: 137 us; the launch traced here: 139 us
  starting transfers between devices  44.2 us (32%)
  Pallas kernels  37.9 us (28%)
  waiting for transfers between devices  34.2 us (25%)
  between operations  16.2 us (12%)
  local copies, waits for them, and re-layouts  5.55 us (4%)
    ppermute x15, starting transfers between devices, shards(): lax.ppermute(value, AXES, [(device(a, b), device(*to(a, b))) for a, b in...  38.9 us
    ppermute x15, waiting for transfers between devices, shards(): lax.ppermute(value, AXES, [(device(a, b), device(*to(a, b))) for a, b in...  27.3 us
    pallas_call x1, Pallas kernels, first_factor(): stage(first_kernel, 'first', [SMEM, VMEM, VMEM], 3, whole)(info, own, twin)  12.2 us
    pallas_call x1, Pallas kernels, update(): pl.pallas_call(update_kernel, grid_spec=pltpu.PrefetchScalarGridSpec(num_...  11.8 us
    pallas_call x1, Pallas kernels, second_factor(): return stage(second_kernel, 'second', [VMEM, VMEM], 2, [])(carried, rest)  11.1 us
    ppermute x4, waiting for transfers between devices, run(): lax.ppermute(part(newest, q), AXES, line(height - 1, plane))  6.87 us
    ppermute x4, starting transfers between devices, run(): lax.ppermute(part(newest, q), AXES, line(height - 1, plane))  3.3 us
  transfers between devices with their start and end apart: 23, of which 9 were waited for; matrix products, arithmetic and copies ran while one was open for 0% of the time, Pallas kernels for 19%

profile of v3, /device:TPU:1, one launch (start us, length us, event | category | flops | bytes accessed | tf_op | source)
XLA Modules:
  0.0 139.1 jit_solution(2536162503351258444)
XLA Ops:
  7.2 0.0 all-gather.3.cloned.1.call-start
  7.2 1.3 fusion.17
  10.5 1.4 %slice.221 = f32[1,1,256,2,1,256]{5,4,3,2,1,0:T(1,128)S(1)} slice(f32[8,1,256,2,1,256]{5,4,3,2,1,0:T(1,128)} %param.10), slice={[7:8], [0:1], [0:256], [0:2], [0:1], [0:256]} | slice | bytes 1048576 | tf_op jit(solution)/shard_map/slice | solution.py:364
  11.9 1.1 dynamic-slice_bitcast_fusion
  13.0 0.0 copy-start.1
  13.0 14.0 %conditional.1 = (f32[256,128]{1,0:T(8,128)}, f32[256,128]{1,0:T(8,128)S(1)}) conditional(s32[]{:T(128)} %clamp.3, (s32[]{:T(128)}, f32[1024,128]{1,0:T(8,128)S(1)}, f32[1024,128]{1,0:T(8,128)S(1)}) %tuple.152, (s32[]{:T(128)}, f32[1024,128]{1,0:T(8,128)S(1)}, f32[1024,128]{1,0:T(8,128)S(1)}) %tuple.156, (s32[]{:T(128)}, ...), branch_computations={%region_0.1_spmd, %region_1.2_spmd, %region_2.3_spmd, %region_3.4_... | conditional | flops 229383 | bytes 6947182 | solution.py:365
  13.0 1.3 collective-permute-start.12
  14.3 0.7 collective-permute-start.11
  15.0 0.7 collective-permute-start.9
  15.7 0.7 collective-permute-start.7
  16.4 0.7 collective-permute-start.10
  17.1 6.9 %collective-permute-done.12 = f32[256,128]{1,0:T(8,128)S(1)} collective-permute-done((f32[256,128]{1,0:T(8,128)S(1)}, f32[256,128]{1,0:T(8,128)S(1)}, u32[]{:S(2)}, u32[]{:S(2)}) %collective-permute-start.12) | collective-permute-done | bytes 131104 | tf_op jit(solution)/shard_map/cond/branch_1_fun/ppermute | solution.py:346
  23.9 0.7 collective-permute-start.8
  24.6 0.7 collective-permute-start.6
  25.4 0.7 select_select_fusion.1
  26.1 0.9 copy.9
  27.0 10.3 %collective-permute-start.52 = (f32[256,128]{1,0:T(8,128)S(1)}, f32[256,128]{1,0:T(8,128)S(1)}, u32[]{:S(2)}, u32[]{:S(2)}) collective-permute-start(f32[256,128]{1,0:T(8,128)S(1)} %get-tuple-element.127.piece_ref), channel_id=1, source_target_pairs={{0,0},{1,32},{2,64},{3,96},{4,128},{5,160},{6,192},{7,224},{8,8},{... | collective-permute-start | bytes 393224 | tf_op jit(solution)/shard_map/ppermute | solution.py:328
  37.3 0.1 stack.27.info
  37.4 0.6 pick.1
  38.0 0.1 collective-permute-start.54
  38.1 6.9 %collective-permute-start.53 = (f32[1,256,128]{2,1,0:T(8,128)S(1)}, f32[1,256,128]{2,1,0:T(8,128)S(1)}, u32[]{:S(2)}, u32[]{:S(2)}) collective-permute-start(f32[1,256,128]{2,1,0:T(8,128)S(1)} %bitcast.31), channel_id=1, source_target_pairs={{0,128},{1,129},{2,130},{3,131},{4,132},{5,133},{6,134},{7,135},{8... | collective-permute-start | bytes 393224 | tf_op jit(solution)/shard_map/ppermute | solution.py:328
  45.0 1.3 collective-permute-start.57
  46.3 2.5 %collective-permute-start.56 = (f32[32,512]{1,0:T(8,128)S(1)}, f32[32,512]{1,0:T(8,128)S(1)}, u32[]{:S(2)}, u32[]{:S(2)}) collective-permute-start(f32[32,512]{1,0:T(8,128)S(1)} %dynamic-slice_select_fusion), channel_id=1, source_target_pairs={{0,16},{1,17},{2,18},{3,19},{4,20},{5,21},{6,22},{7,23},{8,24},{9,... | collective-permute-start | bytes 196616 | tf_op jit(solution)/shard_map/ppermute | solution.py:328
  48.8 0.2 collective-permute-start.55
  49.0 2.4 %collective-permute-done.56 = f32[32,512]{1,0:T(8,128)S(1)} collective-permute-done((f32[32,512]{1,0:T(8,128)S(1)}, f32[32,512]{1,0:T(8,128)S(1)}, u32[]{:S(2)}, u32[]{:S(2)}) %collective-permute-start.56) | collective-permute-done | bytes 65568 | tf_op jit(solution)/shard_map/ppermute | solution.py:328
  51.4 1.9 %collective-permute-done.55 = f32[32,512]{1,0:T(8,128)S(1)} collective-permute-done((f32[32,512]{1,0:T(8,128)S(1)}, f32[32,512]{1,0:T(8,128)S(1)}, u32[]{:S(2)}, u32[]{:S(2)}) %collective-permute-start.55) | collective-permute-done | bytes 65568 | tf_op jit(solution)/shard_map/ppermute | solution.py:328
  53.3 0.0 copy-start
  53.3 0.6 copy-done
  53.9 0.0 all-gather.3.cloned.1.call-update
  54.0 0.1 collective-permute-start.60
  54.1 4.6 %collective-permute-start.59 = (f32[32,512]{1,0:T(8,128)S(1)}, f32[32,512]{1,0:T(8,128)S(1)}, u32[]{:S(2)}, u32[]{:S(2)}) collective-permute-start(f32[32,512]{1,0:T(8,128)S(1)} %select_select_fusion.8), channel_id=1, source_target_pairs={{0,4},{1,5},{2,6},{3,7},{4,0},{5,1},{6,2},{7,3},{8,12},{9,13},{10,... | collective-permute-start | bytes 196616 | tf_op jit(solution)/shard_map/ppermute | solution.py:328
  58.7 2.3 %collective-permute-done.59 = f32[32,512]{1,0:T(8,128)S(1)} collective-permute-done((f32[32,512]{1,0:T(8,128)S(1)}, f32[32,512]{1,0:T(8,128)S(1)}, u32[]{:S(2)}, u32[]{:S(2)}) %collective-permute-start.59) | collective-permute-done | bytes 65568 | tf_op jit(solution)/shard_map/ppermute | solution.py:328
  61.0 2.2 %collective-permute-done.58 = f32[32,512]{1,0:T(8,128)S(1)} collective-permute-done((f32[32,512]{1,0:T(8,128)S(1)}, f32[32,512]{1,0:T(8,128)S(1)}, u32[]{:S(2)}, u32[]{:S(2)}) %collective-permute-start.58) | collective-permute-done | bytes 65568 | tf_op jit(solution)/shard_map/ppermute | solution.py:328
  63.2 1.1 collective-permute-start.61
  64.3 6.1 %collective-permute-done.61 = f32[1,32,512]{2,1,0:T(8,128)S(1)} collective-permute-done((f32[1,32,512]{2,1,0:T(8,128)S(1)}, f32[1,32,512]{2,1,0:T(8,128)S(1)}, u32[]{:S(2)}, u32[]{:S(2)}) %collective-permute-start.61) | collective-permute-done | bytes 65568 | tf_op jit(solution)/shard_map/ppermute | solution.py:328
  70.4 2.7 %collective-permute-start.62 = (f32[2,32,512]{2,1,0:T(8,128)S(1)}, f32[2,32,512]{2,1,0:T(8,128)S(1)}, u32[]{:S(2)}, u32[]{:S(2)}) collective-permute-start(f32[2,32,512]{2,1,0:T(8,128)S(1)} %pad_maximum_fusion.3), channel_id=1, source_target_pairs={{0,64},{1,65},{2,66},{3,67},{4,68},{5,69},{6,70},{7,71},{8,72},{9,... | collective-permute-start | bytes 393224 | tf_op jit(solution)/shard_map/ppermute | solution.py:328
  73.2 5.2 %collective-permute-done.62 = f32[2,32,512]{2,1,0:T(8,128)S(1)} collective-permute-done((f32[2,32,512]{2,1,0:T(8,128)S(1)}, f32[2,32,512]{2,1,0:T(8,128)S(1)}, u32[]{:S(2)}, u32[]{:S(2)}) %collective-permute-start.62) | collective-permute-done | bytes 131104 | tf_op jit(solution)/shard_map/ppermute | solution.py:328
  78.4 0.3 collective-permute-start.63
  78.7 5.2 %collective-permute-done.63 = f32[4,32,512]{2,1,0:T(8,128)S(1)} collective-permute-done((f32[4,32,512]{2,1,0:T(8,128)S(1)}, f32[4,32,512]{2,1,0:T(8,128)S(1)}, u32[]{:S(2)}, u32[]{:S(2)}) %collective-permute-start.63) | collective-permute-done | bytes 262176 | tf_op jit(solution)/shard_map/ppermute | solution.py:328
  83.9 5.4 %collective-permute-start.64 = (f32[8,32,512]{2,1,0:T(8,128)S(1)}, f32[8,32,512]{2,1,0:T(8,128)S(1)}, u32[]{:S(2)}, u32[]{:S(2)}) collective-permute-start(f32[8,32,512]{2,1,0:T(8,128)S(1)} %pad_maximum_fusion.own_ref), channel_id=1, source_target_pairs={{0,1},{1,0},{2,3},{3,2},{4,5},{5,4},{6,7},{7,6},{8,9},{9,8},{10,11... | collective-permute-start | bytes 1572872 | tf_op jit(solution)/shard_map/ppermute | solution.py:328
  89.3 3.1 %collective-permute-start.65 = (f32[2,256,128]{2,1,0:T(8,128)S(1)}, f32[2,256,128]{2,1,0:T(8,128)S(1)}, u32[]{:S(2)}, u32[]{:S(2)}) collective-permute-start(f32[2,256,128]{2,1,0:T(8,128)S(1)} %pad_maximum_fusion.1), channel_id=1, source_target_pairs={{0,64},{1,65},{2,66},{3,67},{4,68},{5,69},{6,70},{7,71},{8,72},{9,... | collective-permute-start | bytes 786440 | tf_op jit(solution)/shard_map/ppermute | solution.py:328
  92.4 12.2 %first.1 = (f32[256,256]{1,0:T(8,128)S(1)}, f32[256,256]{1,0:T(8,128)S(1)}, f32[256,256]{1,0:T(8,128)S(1)}) custom-call(s32[7]{0:T(128)S(1)} %stack.27.info, f32[8,32,512]{2,1,0:T(8,128)S(1)} %pad_maximum_fusion.own_ref, f32[8,32,512]{2,1,0:T(8,128)S(1)} %collective-permute-done.64.twin_ref), custom_call_target="tpu_custom_call" | custom-call | flops 100000000 | bytes 40000000 | tf_op jit(solution)/shard_map/first/pallas_call | solution.py:225
  104.7 0.3 collective-permute-start.66
  105.0 11.1 %second.1 = (f32[256,256]{1,0:T(8,128)S(1)}, f32[256,256]{1,0:T(8,128)S(1)}) custom-call(f32[256,256]{1,0:T(8,128)S(1)} %get-tuple-element.112.w_ref, f32[256,256]{1,0:T(8,128)S(1)} %get-tuple-element.113.rest_ref), custom_call_target="tpu_custom_call" | custom-call | flops 100000000 | bytes 40000000 | tf_op jit(solution)/shard_map/second/pallas_call | solution.py:229
  116.1 2.0 %collective-permute-done.66.far_ref = f32[4,256,128]{2,1,0:T(8,128)S(1)} collective-permute-done((f32[4,256,128]{2,1,0:T(8,128)S(1)}, f32[4,256,128]{2,1,0:T(8,128)S(1)}, u32[]{:S(2)}, u32[]{:S(2)}) %collective-permute-start.66) | collective-permute-done | bytes 524320 | tf_op jit(solution)/shard_map/ppermute | solution.py:328
  118.2 2.2 %cross.1 = (bf16[1536,512]{1,0:T(8,128)(2,1)S(1)}, bf16[1536,512]{1,0:T(8,128)(2,1)S(1)}) custom-call(s32[7]{0:T(128)S(1)} %stack.27.info, f32[256,256]{1,0:T(8,128)S(1)} %get-tuple-element.108.first_ref, f32[256,256]{1,0:T(8,128)S(1)} %get-tuple-element.114.second_ref, f32[256,256]{1,0:T(8,128)S(1)} %get-tuple-element.115.corner_ref, ...), custom_call_target="tpu_custom_call" | custom-call | tf_op jit(solution)/shard_map/cross/pallas_call | solution.py:254
  120.4 0.0 all-gather.3.cloned.1.call-done
  120.4 11.8 %update.1 = (f32[2,2,4,256,256]{4,3,2,1,0:T(8,128)}, f32[2,4,1024,128]{3,2,1,0:T(8,128)}) custom-call(s32[7]{0:T(128)S(1)} %stack.27.info, bf16[1536,512]{1,0:T(8,128)(2,1)S(1)} %get-tuple-element.118.w_ref, bf16[1536,512]{1,0:T(8,128)(2,1)S(1)} %get-tuple-element.119.c_ref, f32[32,256,128]{2,1,0:T(8,128)} %bitcast.30, f32[2,4,1024,128]{3,2,1,0:T(8,128)} %bitcast.29), custom_call_target="tpu_custom_call" | custom-call | tf_op jit(solution)/shard_map/update/pallas_call | solution.py:289
  (31 shorter events, 0.3 us)
Async XLA Ops:
  7.2 113.2 %all-gather.3.cloned.1.call-start = ((), (), s32[]{:S(2)}) async-start(), calls=%async_computation | async-start | bytes 4325376 | tf_op jit(solution)/shard_map/all_gather | solution.py:388
  13.0 24.3 %copy-start.1 = (s32[2]{0:T(128)S(1)}, s32[2]{0:T(128)}, u32[]{:S(2)}) copy-start(s32[2]{0:T(128)} %param.11) | copy-start | bytes 28
  13.0 10.9 %collective-permute-start.12 = (f32[256,128]{1,0:T(8,128)S(1)}, f32[256,128]{1,0:T(8,128)S(1)}, u32[]{:S(2)}, u32[]{:S(2)}) collective-permute-start(f32[256,128]{1,0:T(8,128)S(1)} %get-tuple-element.134), channel_id=1, source_target_pairs={{224,0},{225,1},{226,2},{227,3},{228,4},{229,5},{230,6},{231,7},{2... | collective-permute-start | bytes 393224 | tf_op jit(solution)/shard_map/cond/branch_1_fun/ppermute | solution.py:346
  14.3 10.3 %collective-permute-start.11 = (f32[256,128]{1,0:T(8,128)S(1)}, f32[256,128]{1,0:T(8,128)S(1)}, u32[]{:S(2)}, u32[]{:S(2)}) collective-permute-start(f32[256,128]{1,0:T(8,128)S(1)} %get-tuple-element.135), channel_id=1, source_target_pairs={{224,64},{225,65},{226,66},{227,67},{228,68},{229,69},{230,70},{23... | collective-permute-start | bytes 393224 | tf_op jit(solution)/shard_map/cond/branch_1_fun/ppermute | solution.py:346
  15.0 10.3 %collective-permute-start.9 = (f32[256,128]{1,0:T(8,128)S(1)}, f32[256,128]{1,0:T(8,128)S(1)}, u32[]{:S(2)}, u32[]{:S(2)}) collective-permute-start(f32[256,128]{1,0:T(8,128)S(1)} %get-tuple-element.136), channel_id=1, source_target_pairs={{224,128},{225,129},{226,130},{227,131},{228,132},{229,133},{230,1... | collective-permute-start | bytes 393224 | tf_op jit(solution)/shard_map/cond/branch_1_fun/ppermute | solution.py:346
  15.7 9.6 %collective-permute-start.7 = (f32[256,128]{1,0:T(8,128)S(1)}, f32[256,128]{1,0:T(8,128)S(1)}, u32[]{:S(2)}, u32[]{:S(2)}) collective-permute-start(f32[256,128]{1,0:T(8,128)S(1)} %get-tuple-element.137), channel_id=1, source_target_pairs={{224,192},{225,193},{226,194},{227,195},{228,196},{229,197},{230,1... | collective-permute-start | bytes 393224 | tf_op jit(solution)/shard_map/cond/branch_1_fun/ppermute | solution.py:346
  16.4 8.9 %collective-permute-start.10 = (f32[256,128]{1,0:T(8,128)S(1)}, f32[256,128]{1,0:T(8,128)S(1)}, u32[]{:S(2)}, u32[]{:S(2)}) collective-permute-start(f32[256,128]{1,0:T(8,128)S(1)} %get-tuple-element.138), channel_id=1, source_target_pairs={{32,96},{33,97},{34,98},{35,99},{36,100},{37,101},{38,102},{39,103... | collective-permute-start | bytes 393224 | tf_op jit(solution)/shard_map/cond/branch_1_fun/ppermute | solution.py:352
  23.9 1.4 %collective-permute-start.8 = (f32[256,128]{1,0:T(8,128)S(1)}, f32[256,128]{1,0:T(8,128)S(1)}, u32[]{:S(2)}, u32[]{:S(2)}) collective-permute-start(f32[256,128]{1,0:T(8,128)S(1)} %get-tuple-element.139), channel_id=1, source_target_pairs={{32,160},{33,161},{34,162},{35,163},{36,164},{37,165},{38,166},{39... | collective-permute-start | bytes 393224 | tf_op jit(solution)/shard_map/cond/branch_1_fun/ppermute | solution.py:352
  24.6 0.7 collective-permute-start.6
  27.0 26.3 %collective-permute-start.52 = (f32[256,128]{1,0:T(8,128)S(1)}, f32[256,128]{1,0:T(8,128)S(1)}, u32[]{:S(2)}, u32[]{:S(2)}) collective-permute-start(f32[256,128]{1,0:T(8,128)S(1)} %get-tuple-element.127.piece_ref), channel_id=1, source_target_pairs={{0,0},{1,32},{2,64},{3,96},{4,128},{5,160},{6,192},{7,224},{8,8},{... | collective-permute-start | bytes 393224 | tf_op jit(solution)/shard_map/ppermute | solution.py:328
  38.0 7.0 %collective-permute-start.54 = (f32[64,512]{1,0:T(8,128)S(1)}, f32[64,512]{1,0:T(8,128)S(1)}, u32[]{:S(2)}, u32[]{:S(2)}) collective-permute-start(f32[64,512]{1,0:T(8,128)S(1)} %pick.1), channel_id=1, source_target_pairs={{0,1},{1,0},{2,3},{3,2},{4,5},{5,4},{6,7},{7,6},{8,9},{9,8},{10,11... | collective-permute-start | bytes 393224 | tf_op jit(solution)/shard_map/ppermute | solution.py:328
  38.1 10.9 %collective-permute-start.53 = (f32[1,256,128]{2,1,0:T(8,128)S(1)}, f32[1,256,128]{2,1,0:T(8,128)S(1)}, u32[]{:S(2)}, u32[]{:S(2)}) collective-permute-start(f32[1,256,128]{2,1,0:T(8,128)S(1)} %bitcast.31), channel_id=1, source_target_pairs={{0,128},{1,129},{2,130},{3,131},{4,132},{5,133},{6,134},{7,135},{8... | collective-permute-start | bytes 393224 | tf_op jit(solution)/shard_map/ppermute | solution.py:328
  45.0 4.0 %collective-permute-start.57 = (f32[32,512]{1,0:T(8,128)S(1)}, f32[32,512]{1,0:T(8,128)S(1)}, u32[]{:S(2)}, u32[]{:S(2)}) collective-permute-start(f32[32,512]{1,0:T(8,128)S(1)} %dynamic-slice_select_fusion), channel_id=1, source_target_pairs={{0,8},{1,9},{2,10},{3,11},{4,12},{5,13},{6,14},{7,15},{8,0},{9,1},... | collective-permute-start | bytes 196616 | tf_op jit(solution)/shard_map/ppermute | solution.py:328
  46.3 5.0 %collective-permute-start.56 = (f32[32,512]{1,0:T(8,128)S(1)}, f32[32,512]{1,0:T(8,128)S(1)}, u32[]{:S(2)}, u32[]{:S(2)}) collective-permute-start(f32[32,512]{1,0:T(8,128)S(1)} %dynamic-slice_select_fusion), channel_id=1, source_target_pairs={{0,16},{1,17},{2,18},{3,19},{4,20},{5,21},{6,22},{7,23},{8,24},{9,... | collective-permute-start | bytes 196616 | tf_op jit(solution)/shard_map/ppermute | solution.py:328
  48.8 4.5 %collective-permute-start.55 = (f32[32,512]{1,0:T(8,128)S(1)}, f32[32,512]{1,0:T(8,128)S(1)}, u32[]{:S(2)}, u32[]{:S(2)}) collective-permute-start(f32[32,512]{1,0:T(8,128)S(1)} %dynamic-slice_select_fusion), channel_id=1, source_target_pairs={{0,24},{1,25},{2,26},{3,27},{4,28},{5,29},{6,30},{7,31},{8,16},{9,... | collective-permute-start | bytes 196616 | tf_op jit(solution)/shard_map/ppermute | solution.py:328
  53.3 0.7 copy-start
  54.0 4.7 %collective-permute-start.60 = (f32[32,512]{1,0:T(8,128)S(1)}, f32[32,512]{1,0:T(8,128)S(1)}, u32[]{:S(2)}, u32[]{:S(2)}) collective-permute-start(f32[32,512]{1,0:T(8,128)S(1)} %select_select_fusion.8), channel_id=1, source_target_pairs={{0,2},{1,3},{2,0},{3,1},{4,6},{5,7},{6,4},{7,5},{8,10},{9,11},{10,... | collective-permute-start | bytes 196616 | tf_op jit(solution)/shard_map/ppermute | solution.py:328
  54.1 6.9 %collective-permute-start.59 = (f32[32,512]{1,0:T(8,128)S(1)}, f32[32,512]{1,0:T(8,128)S(1)}, u32[]{:S(2)}, u32[]{:S(2)}) collective-permute-start(f32[32,512]{1,0:T(8,128)S(1)} %select_select_fusion.8), channel_id=1, source_target_pairs={{0,4},{1,5},{2,6},{3,7},{4,0},{5,1},{6,2},{7,3},{8,12},{9,13},{10,... | collective-permute-start | bytes 196616 | tf_op jit(solution)/shard_map/ppermute | solution.py:328
  58.7 4.5 %collective-permute-start.58 = (f32[32,512]{1,0:T(8,128)S(1)}, f32[32,512]{1,0:T(8,128)S(1)}, u32[]{:S(2)}, u32[]{:S(2)}) collective-permute-start(f32[32,512]{1,0:T(8,128)S(1)} %select_select_fusion.8), channel_id=1, source_target_pairs={{0,6},{1,7},{2,4},{3,5},{4,2},{5,3},{6,0},{7,1},{8,14},{9,15},{10,... | collective-permute-start | bytes 196616 | tf_op jit(solution)/shard_map/ppermute | solution.py:328
  63.2 7.2 %collective-permute-start.61 = (f32[1,32,512]{2,1,0:T(8,128)S(1)}, f32[1,32,512]{2,1,0:T(8,128)S(1)}, u32[]{:S(2)}, u32[]{:S(2)}) collective-permute-start(f32[1,32,512]{2,1,0:T(8,128)S(1)} %select_bitcast_fusion), channel_id=1, source_target_pairs={{0,128},{1,129},{2,130},{3,131},{4,132},{5,133},{6,134},{7,135},{8... | collective-permute-start | bytes 196616 | tf_op jit(solution)/shard_map/ppermute | solution.py:328
  70.4 7.9 %collective-permute-start.62 = (f32[2,32,512]{2,1,0:T(8,128)S(1)}, f32[2,32,512]{2,1,0:T(8,128)S(1)}, u32[]{:S(2)}, u32[]{:S(2)}) collective-permute-start(f32[2,32,512]{2,1,0:T(8,128)S(1)} %pad_maximum_fusion.3), channel_id=1, source_target_pairs={{0,64},{1,65},{2,66},{3,67},{4,68},{5,69},{6,70},{7,71},{8,72},{9,... | collective-permute-start | bytes 393224 | tf_op jit(solution)/shard_map/ppermute | solution.py:328
  78.4 5.5 %collective-permute-start.63 = (f32[4,32,512]{2,1,0:T(8,128)S(1)}, f32[4,32,512]{2,1,0:T(8,128)S(1)}, u32[]{:S(2)}, u32[]{:S(2)}) collective-permute-start(f32[4,32,512]{2,1,0:T(8,128)S(1)} %pad_maximum_fusion.2), channel_id=1, source_target_pairs={{0,32},{1,33},{2,34},{3,35},{4,36},{5,37},{6,38},{7,39},{8,40},{9,... | collective-permute-start | bytes 786440 | tf_op jit(solution)/shard_map/ppermute | solution.py:328
  83.9 8.5 %collective-permute-start.64 = (f32[8,32,512]{2,1,0:T(8,128)S(1)}, f32[8,32,512]{2,1,0:T(8,128)S(1)}, u32[]{:S(2)}, u32[]{:S(2)}) collective-permute-start(f32[8,32,512]{2,1,0:T(8,128)S(1)} %pad_maximum_fusion.own_ref), channel_id=1, source_target_pairs={{0,1},{1,0},{2,3},{3,2},{4,5},{5,4},{6,7},{7,6},{8,9},{9,8},{10,11... | collective-permute-start | bytes 1572872 | tf_op jit(solution)/shard_map/ppermute | solution.py:328
  89.3 15.3 %collective-permute-start.65 = (f32[2,256,128]{2,1,0:T(8,128)S(1)}, f32[2,256,128]{2,1,0:T(8,128)S(1)}, u32[]{:S(2)}, u32[]{:S(2)}) collective-permute-start(f32[2,256,128]{2,1,0:T(8,128)S(1)} %pad_maximum_fusion.1), channel_id=1, source_target_pairs={{0,64},{1,65},{2,66},{3,67},{4,68},{5,69},{6,70},{7,71},{8,72},{9,... | collective-permute-start | bytes 786440 | tf_op jit(solution)/shard_map/ppermute | solution.py:328
  104.7 13.5 %collective-permute-start.66 = (f32[4,256,128]{2,1,0:T(8,128)S(1)}, f32[4,256,128]{2,1,0:T(8,128)S(1)}, u32[]{:S(2)}, u32[]{:S(2)}) collective-permute-start(f32[4,256,128]{2,1,0:T(8,128)S(1)} %constant_dynamic-update-slice_fusion.near_ref), channel_id=1, source_target_pairs={{0,32},{1,33},{2,34},{3,35},{4,36},{5,37},{6,38},{7,39},{8,40},{9,... | collective-permute-start | bytes 1572872 | tf_op jit(solution)/shard_map/ppermute | solution.py:328
Sparse Core Ops, SparseCore 0:
  54.1 50.5 all-gather.2

commit v4 on v3

--- a/solution.py
+++ b/solution.py
@@ -384,9 +384,9 @@
         return out
 
     mine = spread(mine, xpos, rx, 3, 3)
-    moved, crossing, mine = tie(moved, crossing, mine)
+    mine = spread(mine, ypos, ry, 3, 1)
+    moved, mine = tie(moved, mine)
     gathered = lax.all_gather(moved, "pcol", axis=0, tiled=False)
-    mine = spread(mine, ypos, ry, 3, 1)
     ring = double(double(double(mine[None], 4), 2), 1)
     crossing, ring = tie(crossing, ring)
     facing = send(crossing, lambda a, b: (a ^ 2, b))

time: 137 us -> 138 us (level); the launches traced: 139 us -> 138 us
  waiting for transfers between devices: 34.2 us -> 26.6 us
  starting transfers between devices: 44.2 us -> 50.3 us
    ppermute x3, starting transfers between devices: 2 us -> 11.6 us  [run(): arrived.append((plane, lax.ppermute(part(others, q), AXES, pairs)))]
    ppermute x4 -> x3, waiting for transfers between devices: 6.87 us -> 0.01 us  [run(): lax.ppermute(part(newest, q), AXES, line(height - 1, plane))]
    ppermute x15, waiting for transfers between devices: 27.3 us -> 24.4 us  [shards(): lax.ppermute(value, AXES, [(device(a, b), device(*to(a, b))) for a, b in...]
    ppermute x15, starting transfers between devices: 38.9 us -> 36.7 us  [shards(): lax.ppermute(value, AXES, [(device(a, b), device(*to(a, b))) for a, b in...]
    ppermute x3, waiting for transfers between devices: 0.01 us -> 2.1 us  [run(): arrived.append((plane, lax.ppermute(part(others, q), AXES, pairs)))]
    ppermute x4 -> x3, starting transfers between devices: 3.3 us -> 2.01 us  [run(): lax.ppermute(part(newest, q), AXES, line(height - 1, plane))]
  transfers between devices with their start and end apart: 23 -> 22, of which waited for: 9 -> 11; matrix products, arithmetic and copies ran while one was open for 0% -> 0% of each run, Pallas kernels for 19% -> 19%
where the time goes in v4:
time: 138 us
  starting transfers between devices  50.3 us (36%)
  Pallas kernels  37.9 us (27%)
  waiting for transfers between devices  26.6 us (19%)
  between operations  16.2 us (12%)
  local copies, waits for them, and re-layouts  5.54 us (4%)
    ppermute x15, starting transfers between devices, shards(): lax.ppermute(value, AXES, [(device(a, b), device(*to(a, b))) for a, b in...  36.7 us
    ppermute x15, waiting for transfers between devices, shards(): lax.ppermute(value, AXES, [(device(a, b), device(*to(a, b))) for a, b in...  24.4 us
    pallas_call x1, Pallas kernels, first_factor(): stage(first_kernel, 'first', [SMEM, VMEM, VMEM], 3, whole)(info, own, twin)  12.2 us
    pallas_call x1, Pallas kernels, update(): pl.pallas_call(update_kernel, grid_spec=pltpu.PrefetchScalarGridSpec(num_...  11.8 us
    ppermute x3, starting transfers between devices, run(): arrived.append((plane, lax.ppermute(part(others, q), AXES, pairs)))  11.6 us
    pallas_call x1, Pallas kernels, second_factor(): return stage(second_kernel, 'second', [VMEM, VMEM], 2, [])(carried, rest)  11.1 us
  transfers between devices with their start and end apart: 22, of which 11 were waited for; matrix products, arithmetic and copies ran while one was open for 0% of the time, Pallas kernels for 19%

profile of v4, /device:TPU:1, one launch (start us, length us, event | category | flops | bytes accessed | tf_op | source)
XLA Modules:
  0.0 137.6 jit_solution(13916132981278794066)
XLA Ops:
  7.2 0.0 all-gather.3.cloned.1.call-start
  7.2 1.3 fusion.17
  10.5 1.4 %slice.221 = f32[1,1,256,2,1,256]{5,4,3,2,1,0:T(1,128)S(1)} slice(f32[8,1,256,2,1,256]{5,4,3,2,1,0:T(1,128)} %param.10), slice={[7:8], [0:1], [0:256], [0:2], [0:1], [0:256]} | slice | bytes 1048576 | tf_op jit(solution)/shard_map/slice | solution.py:364
  11.9 1.1 dynamic-slice_bitcast_fusion
  13.0 17.5 %conditional.1 = (f32[256,128]{1,0:T(8,128)}, f32[256,128]{1,0:T(8,128)S(1)}) conditional(s32[]{:T(128)} %clamp.3, (s32[]{:T(128)}, f32[1024,128]{1,0:T(8,128)S(1)}, f32[1024,128]{1,0:T(8,128)S(1)}) %tuple.152, (s32[]{:T(128)}, f32[1024,128]{1,0:T(8,128)S(1)}, f32[1024,128]{1,0:T(8,128)S(1)}) %tuple.156, (s32[]{:T(128)}, ...), branch_computations={%region_0.1_spmd, %region_1.2_spmd, %region_2.3_spmd, %region_3.4_... | conditional | flops 229383 | bytes 6947182 | solution.py:365
  13.0 0.7 collective-permute-start.5
  13.7 0.7 collective-permute-start.4
  14.4 0.7 collective-permute-start.2
  15.1 5.7 %collective-permute-start.3 = (f32[256,128]{1,0:T(8,128)S(1)}, f32[256,128]{1,0:T(8,128)S(1)}, u32[]{:S(2)}, u32[]{:S(2)}) collective-permute-start(f32[256,128]{1,0:T(8,128)S(1)} %get-tuple-element.129), channel_id=1, source_target_pairs={{0,64},{1,65},{2,66},{3,67},{4,68},{5,69},{6,70},{7,71},{8,72},{9,... | collective-permute-start | bytes 393224 | tf_op jit(solution)/shard_map/cond/branch_0_fun/ppermute | solution.py:352
  20.8 4.6 %collective-permute-start.1 = (f32[256,128]{1,0:T(8,128)S(1)}, f32[256,128]{1,0:T(8,128)S(1)}, u32[]{:S(2)}, u32[]{:S(2)}) collective-permute-start(f32[256,128]{1,0:T(8,128)S(1)} %get-tuple-element.130), channel_id=1, source_target_pairs={{0,128},{1,129},{2,130},{3,131},{4,132},{5,133},{6,134},{7,135},{8... | collective-permute-start | bytes 393224 | tf_op jit(solution)/shard_map/cond/branch_0_fun/ppermute | solution.py:352
  25.4 1.3 collective-permute-start
  26.8 2.0 %collective-permute-done.1 = f32[256,128]{1,0:T(8,128)S(1)} collective-permute-done((f32[256,128]{1,0:T(8,128)S(1)}, f32[256,128]{1,0:T(8,128)S(1)}, u32[]{:S(2)}, u32[]{:S(2)}) %collective-permute-start.1) | collective-permute-done | bytes 131104 | tf_op jit(solution)/shard_map/cond/branch_0_fun/ppermute | solution.py:352
  28.8 0.1 collective-permute-done
  28.9 0.7 select_select_fusion
  29.6 0.9 copy.7
  30.5 1.9 %collective-permute-start.53 = (f32[256,128]{1,0:T(8,128)S(1)}, f32[256,128]{1,0:T(8,128)S(1)}, u32[]{:S(2)}, u32[]{:S(2)}) collective-permute-start(f32[256,128]{1,0:T(8,128)S(1)} %get-tuple-element.125.piece_ref), channel_id=1, source_target_pairs={{0,0},{1,32},{2,64},{3,96},{4,128},{5,160},{6,192},{7,224},{8,8},{... | collective-permute-start | bytes 393224 | tf_op jit(solution)/shard_map/ppermute | solution.py:328
  32.4 0.1 stack.27.info
  32.5 0.6 pick.1
  33.1 0.4 collective-permute-start.54
  33.5 1.0 collective-permute-done.54
  34.5 1.3 collective-permute-start.57
  35.8 2.5 %collective-permute-start.56 = (f32[32,512]{1,0:T(8,128)S(1)}, f32[32,512]{1,0:T(8,128)S(1)}, u32[]{:S(2)}, u32[]{:S(2)}) collective-permute-start(f32[32,512]{1,0:T(8,128)S(1)} %dynamic-slice_select_fusion), channel_id=1, source_target_pairs={{0,16},{1,17},{2,18},{3,19},{4,20},{5,21},{6,22},{7,23},{8,24},{9,... | collective-permute-start | bytes 196616 | tf_op jit(solution)/shard_map/ppermute | solution.py:328
  38.3 0.2 collective-permute-start.55
  38.5 2.8 %collective-permute-done.56 = f32[32,512]{1,0:T(8,128)S(1)} collective-permute-done((f32[32,512]{1,0:T(8,128)S(1)}, f32[32,512]{1,0:T(8,128)S(1)}, u32[]{:S(2)}, u32[]{:S(2)}) %collective-permute-start.56) | collective-permute-done | bytes 65568 | tf_op jit(solution)/shard_map/ppermute | solution.py:328
  41.3 1.4 %collective-permute-done.55 = f32[32,512]{1,0:T(8,128)S(1)} collective-permute-done((f32[32,512]{1,0:T(8,128)S(1)}, f32[32,512]{1,0:T(8,128)S(1)}, u32[]{:S(2)}, u32[]{:S(2)}) %collective-permute-start.55) | collective-permute-done | bytes 65568 | tf_op jit(solution)/shard_map/ppermute | solution.py:328
  42.8 4.0 %collective-permute-start.60 = (f32[32,512]{1,0:T(8,128)S(1)}, f32[32,512]{1,0:T(8,128)S(1)}, u32[]{:S(2)}, u32[]{:S(2)}) collective-permute-start(f32[32,512]{1,0:T(8,128)S(1)} %select_select_fusion.9), channel_id=1, source_target_pairs={{0,2},{1,3},{2,0},{3,1},{4,6},{5,7},{6,4},{7,5},{8,10},{9,11},{10,... | collective-permute-start | bytes 196616 | tf_op jit(solution)/shard_map/ppermute | solution.py:328
  46.8 5.7 %collective-permute-start.59 = (f32[32,512]{1,0:T(8,128)S(1)}, f32[32,512]{1,0:T(8,128)S(1)}, u32[]{:S(2)}, u32[]{:S(2)}) collective-permute-start(f32[32,512]{1,0:T(8,128)S(1)} %select_select_fusion.9), channel_id=1, source_target_pairs={{0,4},{1,5},{2,6},{3,7},{4,0},{5,1},{6,2},{7,3},{8,12},{9,13},{10,... | collective-permute-start | bytes 196616 | tf_op jit(solution)/shard_map/ppermute | solution.py:328
  52.5 0.2 collective-permute-start.58
  52.7 2.1 %collective-permute-done.59 = f32[32,512]{1,0:T(8,128)S(1)} collective-permute-done((f32[32,512]{1,0:T(8,128)S(1)}, f32[32,512]{1,0:T(8,128)S(1)}, u32[]{:S(2)}, u32[]{:S(2)}) %collective-permute-start.59) | collective-permute-done | bytes 65568 | tf_op jit(solution)/shard_map/ppermute | solution.py:328
  54.8 2.8 %collective-permute-done.58 = f32[32,512]{1,0:T(8,128)S(1)} collective-permute-done((f32[32,512]{1,0:T(8,128)S(1)}, f32[32,512]{1,0:T(8,128)S(1)}, u32[]{:S(2)}, u32[]{:S(2)}) %collective-permute-start.58) | collective-permute-done | bytes 65568 | tf_op jit(solution)/shard_map/ppermute | solution.py:328
  57.6 0.6 copy-done
  58.3 0.0 all-gather.3.cloned.1.call-update
  58.3 2.4 %collective-permute-start.61 = (f32[1,32,512]{2,1,0:T(8,128)S(1)}, f32[1,32,512]{2,1,0:T(8,128)S(1)}, u32[]{:S(2)}, u32[]{:S(2)}) collective-permute-start(f32[1,32,512]{2,1,0:T(8,128)S(1)} %bitcast.32), channel_id=1, source_target_pairs={{0,128},{1,129},{2,130},{3,131},{4,132},{5,133},{6,134},{7,135},{8... | collective-permute-start | bytes 196616 | tf_op jit(solution)/shard_map/ppermute | solution.py:328
  60.6 4.7 %collective-permute-done.61 = f32[1,32,512]{2,1,0:T(8,128)S(1)} collective-permute-done((f32[1,32,512]{2,1,0:T(8,128)S(1)}, f32[1,32,512]{2,1,0:T(8,128)S(1)}, u32[]{:S(2)}, u32[]{:S(2)}) %collective-permute-start.61) | collective-permute-done | bytes 65568 | tf_op jit(solution)/shard_map/ppermute | solution.py:328
  65.4 3.0 %collective-permute-start.62 = (f32[2,32,512]{2,1,0:T(8,128)S(1)}, f32[2,32,512]{2,1,0:T(8,128)S(1)}, u32[]{:S(2)}, u32[]{:S(2)}) collective-permute-start(f32[2,32,512]{2,1,0:T(8,128)S(1)} %pad_maximum_fusion.3), channel_id=1, source_target_pairs={{0,64},{1,65},{2,66},{3,67},{4,68},{5,69},{6,70},{7,71},{8,72},{9,... | collective-permute-start | bytes 393224 | tf_op jit(solution)/shard_map/ppermute | solution.py:328
  68.4 2.4 %collective-permute-done.62 = f32[2,32,512]{2,1,0:T(8,128)S(1)} collective-permute-done((f32[2,32,512]{2,1,0:T(8,128)S(1)}, f32[2,32,512]{2,1,0:T(8,128)S(1)}, u32[]{:S(2)}, u32[]{:S(2)}) %collective-permute-start.62) | collective-permute-done | bytes 131104 | tf_op jit(solution)/shard_map/ppermute | solution.py:328
  70.8 0.1 collective-permute-start.63
  70.9 2.6 %collective-permute-start.52 = (f32[1,256,128]{2,1,0:T(8,128)S(1)}, f32[1,256,128]{2,1,0:T(8,128)S(1)}, u32[]{:S(2)}, u32[]{:S(2)}) collective-permute-start(f32[1,256,128]{2,1,0:T(8,128)S(1)} %bitcast.30), channel_id=1, source_target_pairs={{0,128},{1,129},{2,130},{3,131},{4,132},{5,133},{6,134},{7,135},{8... | collective-permute-start | bytes 393224 | tf_op jit(solution)/shard_map/ppermute | solution.py:328
  73.5 6.3 %collective-permute-done.52 = f32[1,256,128]{2,1,0:T(8,128)S(1)} collective-permute-done((f32[1,256,128]{2,1,0:T(8,128)S(1)}, f32[1,256,128]{2,1,0:T(8,128)S(1)}, u32[]{:S(2)}, u32[]{:S(2)}) %collective-permute-start.52) | collective-permute-done | bytes 131104 | tf_op jit(solution)/shard_map/ppermute | solution.py:328
  79.9 6.6 %collective-permute-start.64 = (f32[8,32,512]{2,1,0:T(8,128)S(1)}, f32[8,32,512]{2,1,0:T(8,128)S(1)}, u32[]{:S(2)}, u32[]{:S(2)}) collective-permute-start(f32[8,32,512]{2,1,0:T(8,128)S(1)} %pad_maximum_fusion.own_ref), channel_id=1, source_target_pairs={{0,1},{1,0},{2,3},{3,2},{4,5},{5,4},{6,7},{7,6},{8,9},{9,8},{10,11... | collective-permute-start | bytes 1572872 | tf_op jit(solution)/shard_map/ppermute | solution.py:328
  86.5 3.4 %collective-permute-start.65 = (f32[2,256,128]{2,1,0:T(8,128)S(1)}, f32[2,256,128]{2,1,0:T(8,128)S(1)}, u32[]{:S(2)}, u32[]{:S(2)}) collective-permute-start(f32[2,256,128]{2,1,0:T(8,128)S(1)} %pad_maximum_fusion.1), channel_id=1, source_target_pairs={{0,64},{1,65},{2,66},{3,67},{4,68},{5,69},{6,70},{7,71},{8,72},{9,... | collective-permute-start | bytes 786440 | tf_op jit(solution)/shard_map/ppermute | solution.py:328
  90.0 12.2 %first.1 = (f32[256,256]{1,0:T(8,128)S(1)}, f32[256,256]{1,0:T(8,128)S(1)}, f32[256,256]{1,0:T(8,128)S(1)}) custom-call(s32[7]{0:T(128)S(1)} %stack.27.info, f32[8,32,512]{2,1,0:T(8,128)S(1)} %pad_maximum_fusion.own_ref, f32[8,32,512]{2,1,0:T(8,128)S(1)} %collective-permute-done.64.twin_ref), custom_call_target="tpu_custom_call" | custom-call | flops 100000000 | bytes 40000000 | tf_op jit(solution)/shard_map/first/pallas_call | solution.py:225
  102.2 2.4 %collective-permute-start.66 = (f32[4,256,128]{2,1,0:T(8,128)S(1)}, f32[4,256,128]{2,1,0:T(8,128)S(1)}, u32[]{:S(2)}, u32[]{:S(2)}) collective-permute-start(f32[4,256,128]{2,1,0:T(8,128)S(1)} %constant_dynamic-update-slice_fusion.near_ref), channel_id=1, source_target_pairs={{0,32},{1,33},{2,34},{3,35},{4,36},{5,37},{6,38},{7,39},{8,40},{9,... | collective-permute-start | bytes 1572872 | tf_op jit(solution)/shard_map/ppermute | solution.py:328
  104.6 11.1 %second.1 = (f32[256,256]{1,0:T(8,128)S(1)}, f32[256,256]{1,0:T(8,128)S(1)}) custom-call(f32[256,256]{1,0:T(8,128)S(1)} %get-tuple-element.110.w_ref, f32[256,256]{1,0:T(8,128)S(1)} %get-tuple-element.111.rest_ref), custom_call_target="tpu_custom_call" | custom-call | flops 100000000 | bytes 40000000 | tf_op jit(solution)/shard_map/second/pallas_call | solution.py:229
  115.8 0.9 collective-permute-done.66.far_ref
  116.6 2.2 %cross.1 = (bf16[1536,512]{1,0:T(8,128)(2,1)S(1)}, bf16[1536,512]{1,0:T(8,128)(2,1)S(1)}) custom-call(s32[7]{0:T(128)S(1)} %stack.27.info, f32[256,256]{1,0:T(8,128)S(1)} %get-tuple-element.106.first_ref, f32[256,256]{1,0:T(8,128)S(1)} %get-tuple-element.112.second_ref, f32[256,256]{1,0:T(8,128)S(1)} %get-tuple-element.113.corner_ref, ...), custom_call_target="tpu_custom_call" | custom-call | tf_op jit(solution)/shard_map/cross/pallas_call | solution.py:254
  118.9 0.0 all-gather.3.cloned.1.call-done
  118.9 11.8 %update.1 = (f32[2,2,4,256,256]{4,3,2,1,0:T(8,128)}, f32[2,4,1024,128]{3,2,1,0:T(8,128)}) custom-call(s32[7]{0:T(128)S(1)} %stack.27.info, bf16[1536,512]{1,0:T(8,128)(2,1)S(1)} %get-tuple-element.116.w_ref, bf16[1536,512]{1,0:T(8,128)(2,1)S(1)} %get-tuple-element.117.c_ref, f32[32,256,128]{2,1,0:T(8,128)} %bitcast.29, f32[2,4,1024,128]{3,2,1,0:T(8,128)} %bitcast.28), custom_call_target="tpu_custom_call" | custom-call | tf_op jit(solution)/shard_map/update/pallas_call | solution.py:289
  (29 shorter events, 0.3 us)
Async XLA Ops:
  7.2 111.7 %all-gather.3.cloned.1.call-start = ((), (), s32[]{:S(2)}) async-start(), calls=%async_computation | async-start | bytes 4325376 | tf_op jit(solution)/shard_map/all_gather | solution.py:389
  13.0 19.5 %copy-start.1 = (s32[2]{0:T(128)S(1)}, s32[2]{0:T(128)}, u32[]{:S(2)}) copy-start(s32[2]{0:T(128)} %param.11) | copy-start | bytes 28
  13.0 12.4 %collective-permute-start.5 = (f32[256,128]{1,0:T(8,128)S(1)}, f32[256,128]{1,0:T(8,128)S(1)}, u32[]{:S(2)}, u32[]{:S(2)}) collective-permute-start(f32[256,128]{1,0:T(8,128)S(1)} %get-tuple-element.126), channel_id=1, source_target_pairs={{224,32},{225,33},{226,34},{227,35},{228,36},{229,37},{230,38},{23... | collective-permute-start | bytes 393224 | tf_op jit(solution)/shard_map/cond/branch_0_fun/ppermute | solution.py:346
  13.7 13.1 %collective-permute-start.4 = (f32[256,128]{1,0:T(8,128)S(1)}, f32[256,128]{1,0:T(8,128)S(1)}, u32[]{:S(2)}, u32[]{:S(2)}) collective-permute-start(f32[256,128]{1,0:T(8,128)S(1)} %get-tuple-element.127), channel_id=1, source_target_pairs={{224,96},{225,97},{226,98},{227,99},{228,100},{229,101},{230,102},... | collective-permute-start | bytes 393224 | tf_op jit(solution)/shard_map/cond/branch_0_fun/ppermute | solution.py:346
  14.4 12.4 %collective-permute-start.2 = (f32[256,128]{1,0:T(8,128)S(1)}, f32[256,128]{1,0:T(8,128)S(1)}, u32[]{:S(2)}, u32[]{:S(2)}) collective-permute-start(f32[256,128]{1,0:T(8,128)S(1)} %get-tuple-element.128), channel_id=1, source_target_pairs={{224,160},{225,161},{226,162},{227,163},{228,164},{229,165},{230,1... | collective-permute-start | bytes 393224 | tf_op jit(solution)/shard_map/cond/branch_0_fun/ppermute | solution.py:346
  15.1 11.7 %collective-permute-start.3 = (f32[256,128]{1,0:T(8,128)S(1)}, f32[256,128]{1,0:T(8,128)S(1)}, u32[]{:S(2)}, u32[]{:S(2)}) collective-permute-start(f32[256,128]{1,0:T(8,128)S(1)} %get-tuple-element.129), channel_id=1, source_target_pairs={{0,64},{1,65},{2,66},{3,67},{4,68},{5,69},{6,70},{7,71},{8,72},{9,... | collective-permute-start | bytes 393224 | tf_op jit(solution)/shard_map/cond/branch_0_fun/ppermute | solution.py:352
  20.8 8.0 %collective-permute-start.1 = (f32[256,128]{1,0:T(8,128)S(1)}, f32[256,128]{1,0:T(8,128)S(1)}, u32[]{:S(2)}, u32[]{:S(2)}) collective-permute-start(f32[256,128]{1,0:T(8,128)S(1)} %get-tuple-element.130), channel_id=1, source_target_pairs={{0,128},{1,129},{2,130},{3,131},{4,132},{5,133},{6,134},{7,135},{8... | collective-permute-start | bytes 393224 | tf_op jit(solution)/shard_map/cond/branch_0_fun/ppermute | solution.py:352
  25.4 3.4 %collective-permute-start = (f32[256,128]{1,0:T(8,128)S(1)}, f32[256,128]{1,0:T(8,128)S(1)}, u32[]{:S(2)}, u32[]{:S(2)}) collective-permute-start(f32[256,128]{1,0:T(8,128)S(1)} %get-tuple-element.131), channel_id=1, source_target_pairs={{0,192},{1,193},{2,194},{3,195},{4,196},{5,197},{6,198},{7,199},{8... | collective-permute-start | bytes 393224 | tf_op jit(solution)/shard_map/cond/branch_0_fun/ppermute | solution.py:352
  30.5 27.1 %collective-permute-start.53 = (f32[256,128]{1,0:T(8,128)S(1)}, f32[256,128]{1,0:T(8,128)S(1)}, u32[]{:S(2)}, u32[]{:S(2)}) collective-permute-start(f32[256,128]{1,0:T(8,128)S(1)} %get-tuple-element.125.piece_ref), channel_id=1, source_target_pairs={{0,0},{1,32},{2,64},{3,96},{4,128},{5,160},{6,192},{7,224},{8,8},{... | collective-permute-start | bytes 393224 | tf_op jit(solution)/shard_map/ppermute | solution.py:328
  33.1 1.4 %collective-permute-start.54 = (f32[64,512]{1,0:T(8,128)S(1)}, f32[64,512]{1,0:T(8,128)S(1)}, u32[]{:S(2)}, u32[]{:S(2)}) collective-permute-start(f32[64,512]{1,0:T(8,128)S(1)} %pick.1), channel_id=1, source_target_pairs={{0,1},{1,0},{2,3},{3,2},{4,5},{5,4},{6,7},{7,6},{8,9},{9,8},{10,11... | collective-permute-start | bytes 393224 | tf_op jit(solution)/shard_map/ppermute | solution.py:328
  34.5 4.0 %collective-permute-start.57 = (f32[32,512]{1,0:T(8,128)S(1)}, f32[32,512]{1,0:T(8,128)S(1)}, u32[]{:S(2)}, u32[]{:S(2)}) collective-permute-start(f32[32,512]{1,0:T(8,128)S(1)} %dynamic-slice_select_fusion), channel_id=1, source_target_pairs={{0,8},{1,9},{2,10},{3,11},{4,12},{5,13},{6,14},{7,15},{8,0},{9,1},... | collective-permute-start | bytes 196616 | tf_op jit(solution)/shard_map/ppermute | solution.py:328
  35.8 5.5 %collective-permute-start.56 = (f32[32,512]{1,0:T(8,128)S(1)}, f32[32,512]{1,0:T(8,128)S(1)}, u32[]{:S(2)}, u32[]{:S(2)}) collective-permute-start(f32[32,512]{1,0:T(8,128)S(1)} %dynamic-slice_select_fusion), channel_id=1, source_target_pairs={{0,16},{1,17},{2,18},{3,19},{4,20},{5,21},{6,22},{7,23},{8,24},{9,... | collective-permute-start | bytes 196616 | tf_op jit(solution)/shard_map/ppermute | solution.py:328
  38.3 4.5 %collective-permute-start.55 = (f32[32,512]{1,0:T(8,128)S(1)}, f32[32,512]{1,0:T(8,128)S(1)}, u32[]{:S(2)}, u32[]{:S(2)}) collective-permute-start(f32[32,512]{1,0:T(8,128)S(1)} %dynamic-slice_select_fusion), channel_id=1, source_target_pairs={{0,24},{1,25},{2,26},{3,27},{4,28},{5,29},{6,30},{7,31},{8,16},{9,... | collective-permute-start | bytes 196616 | tf_op jit(solution)/shard_map/ppermute | solution.py:328
  42.8 10.0 %collective-permute-start.60 = (f32[32,512]{1,0:T(8,128)S(1)}, f32[32,512]{1,0:T(8,128)S(1)}, u32[]{:S(2)}, u32[]{:S(2)}) collective-permute-start(f32[32,512]{1,0:T(8,128)S(1)} %select_select_fusion.9), channel_id=1, source_target_pairs={{0,2},{1,3},{2,0},{3,1},{4,6},{5,7},{6,4},{7,5},{8,10},{9,11},{10,... | collective-permute-start | bytes 196616 | tf_op jit(solution)/shard_map/ppermute | solution.py:328
  46.8 8.0 %collective-permute-start.59 = (f32[32,512]{1,0:T(8,128)S(1)}, f32[32,512]{1,0:T(8,128)S(1)}, u32[]{:S(2)}, u32[]{:S(2)}) collective-permute-start(f32[32,512]{1,0:T(8,128)S(1)} %select_select_fusion.9), channel_id=1, source_target_pairs={{0,4},{1,5},{2,6},{3,7},{4,0},{5,1},{6,2},{7,3},{8,12},{9,13},{10,... | collective-permute-start | bytes 196616 | tf_op jit(solution)/shard_map/ppermute | solution.py:328
  52.5 5.0 %collective-permute-start.58 = (f32[32,512]{1,0:T(8,128)S(1)}, f32[32,512]{1,0:T(8,128)S(1)}, u32[]{:S(2)}, u32[]{:S(2)}) collective-permute-start(f32[32,512]{1,0:T(8,128)S(1)} %select_select_fusion.9), channel_id=1, source_target_pairs={{0,6},{1,7},{2,4},{3,5},{4,2},{5,3},{6,0},{7,1},{8,14},{9,15},{10,... | collective-permute-start | bytes 196616 | tf_op jit(solution)/shard_map/ppermute | solution.py:328
  57.6 0.7 copy-start
  58.3 7.1 %collective-permute-start.61 = (f32[1,32,512]{2,1,0:T(8,128)S(1)}, f32[1,32,512]{2,1,0:T(8,128)S(1)}, u32[]{:S(2)}, u32[]{:S(2)}) collective-permute-start(f32[1,32,512]{2,1,0:T(8,128)S(1)} %bitcast.32), channel_id=1, source_target_pairs={{0,128},{1,129},{2,130},{3,131},{4,132},{5,133},{6,134},{7,135},{8... | collective-permute-start | bytes 196616 | tf_op jit(solution)/shard_map/ppermute | solution.py:328
  65.4 5.4 %collective-permute-start.62 = (f32[2,32,512]{2,1,0:T(8,128)S(1)}, f32[2,32,512]{2,1,0:T(8,128)S(1)}, u32[]{:S(2)}, u32[]{:S(2)}) collective-permute-start(f32[2,32,512]{2,1,0:T(8,128)S(1)} %pad_maximum_fusion.3), channel_id=1, source_target_pairs={{0,64},{1,65},{2,66},{3,67},{4,68},{5,69},{6,70},{7,71},{8,72},{9,... | collective-permute-start | bytes 393224 | tf_op jit(solution)/shard_map/ppermute | solution.py:328
  70.8 9.0 %collective-permute-start.63 = (f32[4,32,512]{2,1,0:T(8,128)S(1)}, f32[4,32,512]{2,1,0:T(8,128)S(1)}, u32[]{:S(2)}, u32[]{:S(2)}) collective-permute-start(f32[4,32,512]{2,1,0:T(8,128)S(1)} %pad_maximum_fusion.2), channel_id=1, source_target_pairs={{0,32},{1,33},{2,34},{3,35},{4,36},{5,37},{6,38},{7,39},{8,40},{9,... | collective-permute-start | bytes 786440 | tf_op jit(solution)/shard_map/ppermute | solution.py:328
  70.9 8.9 %collective-permute-start.52 = (f32[1,256,128]{2,1,0:T(8,128)S(1)}, f32[1,256,128]{2,1,0:T(8,128)S(1)}, u32[]{:S(2)}, u32[]{:S(2)}) collective-permute-start(f32[1,256,128]{2,1,0:T(8,128)S(1)} %bitcast.30), channel_id=1, source_target_pairs={{0,128},{1,129},{2,130},{3,131},{4,132},{5,133},{6,134},{7,135},{8... | collective-permute-start | bytes 393224 | tf_op jit(solution)/shard_map/ppermute | solution.py:328
  79.9 10.1 %collective-permute-start.64 = (f32[8,32,512]{2,1,0:T(8,128)S(1)}, f32[8,32,512]{2,1,0:T(8,128)S(1)}, u32[]{:S(2)}, u32[]{:S(2)}) collective-permute-start(f32[8,32,512]{2,1,0:T(8,128)S(1)} %pad_maximum_fusion.own_ref), channel_id=1, source_target_pairs={{0,1},{1,0},{2,3},{3,2},{4,5},{5,4},{6,7},{7,6},{8,9},{9,8},{10,11... | collective-permute-start | bytes 1572872 | tf_op jit(solution)/shard_map/ppermute | solution.py:328
  86.5 15.6 %collective-permute-start.65 = (f32[2,256,128]{2,1,0:T(8,128)S(1)}, f32[2,256,128]{2,1,0:T(8,128)S(1)}, u32[]{:S(2)}, u32[]{:S(2)}) collective-permute-start(f32[2,256,128]{2,1,0:T(8,128)S(1)} %pad_maximum_fusion.1), channel_id=1, source_target_pairs={{0,64},{1,65},{2,66},{3,67},{4,68},{5,69},{6,70},{7,71},{8,72},{9,... | collective-permute-start | bytes 786440 | tf_op jit(solution)/shard_map/ppermute | solution.py:328
  102.2 14.4 %collective-permute-start.66 = (f32[4,256,128]{2,1,0:T(8,128)S(1)}, f32[4,256,128]{2,1,0:T(8,128)S(1)}, u32[]{:S(2)}, u32[]{:S(2)}) collective-permute-start(f32[4,256,128]{2,1,0:T(8,128)S(1)} %constant_dynamic-update-slice_fusion.near_ref), channel_id=1, source_target_pairs={{0,32},{1,33},{2,34},{3,35},{4,36},{5,37},{6,38},{7,39},{8,40},{9,... | collective-permute-start | bytes 1572872 | tf_op jit(solution)/shard_map/ppermute | solution.py:328
Sparse Core Ops, SparseCore 0:
  58.4 48.2 all-gather.2

commit v5 on v4

--- a/solution.py
+++ b/solution.py
@@ -367,8 +367,6 @@
 
     moved = send(piece, lambda a, b: (b % height, (b // height) * height + a))
 
-    crossing = double(piece[None], 4)
-
     core, ypos, xpos = c & 1, (c >> 1) & 3, c >> 3
     rcore, ry, rx = root_col & 1, (root_col >> 1) & 3, root_col >> 3
     side = lax.broadcasted_iota(jnp.int32, (CHUNK, 2 * NB), 1) < NB
@@ -384,8 +382,10 @@
         return out
 
     mine = spread(mine, xpos, rx, 3, 3)
+    piece, mine = tie(piece, mine)
+    crossing = double(piece[None], 4)
     mine = spread(mine, ypos, ry, 3, 1)
-    moved, mine = tie(moved, mine)
+    moved, crossing, mine = tie(moved, crossing, mine)
     gathered = lax.all_gather(moved, "pcol", axis=0, tiled=False)
     ring = double(double(double(mine[None], 4), 2), 1)
     crossing, ring = tie(crossing, ring)

time: 138 us -> 140 us (1.014)
  waiting for transfers between devices: 26.6 us -> 32.7 us
  starting transfers between devices: 50.3 us -> 48.1 us
    ppermute x3, starting transfers between devices: 11.6 us -> 2.63 us  [run(): arrived.append((plane, lax.ppermute(part(others, q), AXES, pairs)))]
    ppermute x15, starting transfers between devices: 36.7 us -> 43.4 us  [shards(): lax.ppermute(value, AXES, [(device(a, b), device(*to(a, b))) for a, b in...]
    ppermute x15, waiting for transfers between devices: 24.4 us -> 27.9 us  [shards(): lax.ppermute(value, AXES, [(device(a, b), device(*to(a, b))) for a, b in...]
    ppermute x3, waiting for transfers between devices: 2.1 us -> 4.76 us  [run(): arrived.append((plane, lax.ppermute(part(others, q), AXES, pairs)))]
where the time goes in v5:
time: 140 us
  starting transfers between devices  48.1 us (34%)
  Pallas kernels  37.9 us (27%)
  waiting for transfers between devices  32.7 us (23%)
  between operations  16.2 us (12%)
  local copies, waits for them, and re-layouts  4.64 us (3%)
    ppermute x15, starting transfers between devices, shards(): lax.ppermute(value, AXES, [(device(a, b), device(*to(a, b))) for a, b in...  43.4 us
    ppermute x15, waiting for transfers between devices, shards(): lax.ppermute(value, AXES, [(device(a, b), device(*to(a, b))) for a, b in...  27.9 us
    pallas_call x1, Pallas kernels, first_factor(): stage(first_kernel, 'first', [SMEM, VMEM, VMEM], 3, whole)(info, own, twin)  12.2 us
    pallas_call x1, Pallas kernels, update(): pl.pallas_call(update_kernel, grid_spec=pltpu.PrefetchScalarGridSpec(num_...  11.8 us
    pallas_call x1, Pallas kernels, second_factor(): return stage(second_kernel, 'second', [VMEM, VMEM], 2, [])(carried, rest)  11.1 us
    ppermute x3, waiting for transfers between devices, run(): arrived.append((plane, lax.ppermute(part(others, q), AXES, pairs)))  4.76 us
  transfers between devices with their start and end apart: 22, of which 11 were waited for; matrix products, arithmetic and copies ran while one was open for 0% of the time, Pallas kernels for 19%

profile of v5, /device:TPU:1, one launch (start us, length us, event | category | flops | bytes accessed | tf_op | source)
XLA Modules:
  0.0 139.9 jit_solution(11433693051810370186)
XLA Ops:
  7.2 0.0 all-gather.3.cloned.1.call-start
  7.2 1.3 fusion.17
  10.5 1.4 %slice.221 = f32[1,1,256,2,1,256]{5,4,3,2,1,0:T(1,128)S(1)} slice(f32[8,1,256,2,1,256]{5,4,3,2,1,0:T(1,128)} %param.10), slice={[7:8], [0:1], [0:256], [0:2], [0:1], [0:256]} | slice | bytes 1048576 | tf_op jit(solution)/shard_map/slice | solution.py:364
  11.9 1.1 dynamic-slice_bitcast_fusion
  13.0 0.0 copy-start.1
  13.0 9.7 %conditional.1 = (f32[256,128]{1,0:T(8,128)S(1)}) conditional(s32[]{:T(128)} %clamp.3, (s32[]{:T(128)}, f32[1024,128]{1,0:T(8,128)S(1)}, f32[1024,128]{1,0:T(8,128)S(1)}) %tuple.95, (s32[]{:T(128)}, f32[1024,128]{1,0:T(8,128)S(1)}, f32[1024,128]{1,0:T(8,128)S(1)}) %tuple.99, (s32[]{:T(128)}, ...), branch_computations={%region_0.1_spmd, %region_1.2_spmd, %region_2.3_spmd, %region_3.4_... | conditional | flops 229383 | bytes 6685030 | solution.py:365
  13.0 0.7 collective-permute-start.18
  13.7 0.7 collective-permute-start.16
  14.4 0.7 collective-permute-start.15
  15.1 1.3 collective-permute-start.17
  16.4 0.7 collective-permute-start.14
  17.1 0.7 collective-permute-start.13
  17.8 4.8 %collective-permute-done.17 = f32[256,128]{1,0:T(8,128)S(1)} collective-permute-done((f32[256,128]{1,0:T(8,128)S(1)}, f32[256,128]{1,0:T(8,128)S(1)}, u32[]{:S(2)}, u32[]{:S(2)}) %collective-permute-start.17) | collective-permute-done | bytes 131104 | tf_op jit(solution)/shard_map/cond/branch_2_fun/ppermute | solution.py:352
  22.6 6.3 %collective-permute-start.52 = (f32[256,128]{1,0:T(8,128)S(1)}, f32[256,128]{1,0:T(8,128)S(1)}, u32[]{:S(2)}, u32[]{:S(2)}) collective-permute-start(f32[256,128]{1,0:T(8,128)S(1)} %get-tuple-element.187.piece_ref), channel_id=1, source_target_pairs={{0,0},{1,32},{2,64},{3,96},{4,128},{5,160},{6,192},{7,224},{8,8},{... | collective-permute-start | bytes 393224 | tf_op jit(solution)/shard_map/ppermute | solution.py:328
  29.0 0.1 stack.27.info
  29.1 0.6 pick.1
  29.6 0.1 collective-permute-start.53
  29.8 1.3 collective-permute-done.53
  31.1 1.3 collective-permute-start.56
  32.4 2.5 %collective-permute-start.55 = (f32[32,512]{1,0:T(8,128)S(1)}, f32[32,512]{1,0:T(8,128)S(1)}, u32[]{:S(2)}, u32[]{:S(2)}) collective-permute-start(f32[32,512]{1,0:T(8,128)S(1)} %dynamic-slice_select_fusion), channel_id=1, source_target_pairs={{0,16},{1,17},{2,18},{3,19},{4,20},{5,21},{6,22},{7,23},{8,24},{9,... | collective-permute-start | bytes 196616 | tf_op jit(solution)/shard_map/ppermute | solution.py:328
  34.8 0.2 collective-permute-start.54
  35.0 3.3 %collective-permute-done.55 = f32[32,512]{1,0:T(8,128)S(1)} collective-permute-done((f32[32,512]{1,0:T(8,128)S(1)}, f32[32,512]{1,0:T(8,128)S(1)}, u32[]{:S(2)}, u32[]{:S(2)}) %collective-permute-start.55) | collective-permute-done | bytes 65568 | tf_op jit(solution)/shard_map/ppermute | solution.py:328
  38.3 1.0 collective-permute-done.54
  39.3 10.1 %collective-permute-start.60 = (f32[32,512]{1,0:T(8,128)S(1)}, f32[32,512]{1,0:T(8,128)S(1)}, u32[]{:S(2)}, u32[]{:S(2)}) collective-permute-start(f32[32,512]{1,0:T(8,128)S(1)} %select_select_fusion.9), channel_id=1, source_target_pairs={{0,2},{1,3},{2,0},{3,1},{4,6},{5,7},{6,4},{7,5},{8,10},{9,11},{10,... | collective-permute-start | bytes 196616 | tf_op jit(solution)/shard_map/ppermute | solution.py:328
  49.4 4.7 %collective-permute-start.59 = (f32[32,512]{1,0:T(8,128)S(1)}, f32[32,512]{1,0:T(8,128)S(1)}, u32[]{:S(2)}, u32[]{:S(2)}) collective-permute-start(f32[32,512]{1,0:T(8,128)S(1)} %select_select_fusion.9), channel_id=1, source_target_pairs={{0,4},{1,5},{2,6},{3,7},{4,0},{5,1},{6,2},{7,3},{8,12},{9,13},{10,... | collective-permute-start | bytes 196616 | tf_op jit(solution)/shard_map/ppermute | solution.py:328
  54.2 0.2 collective-permute-start.58
  54.3 2.8 %collective-permute-start.57 = (f32[1,256,128]{2,1,0:T(8,128)S(1)}, f32[1,256,128]{2,1,0:T(8,128)S(1)}, u32[]{:S(2)}, u32[]{:S(2)}) collective-permute-start(f32[1,256,128]{2,1,0:T(8,128)S(1)} %bitcast.30), channel_id=1, source_target_pairs={{0,128},{1,129},{2,130},{3,131},{4,132},{5,133},{6,134},{7,135},{8... | collective-permute-start | bytes 393224 | tf_op jit(solution)/shard_map/ppermute | solution.py:328
  57.1 1.9 %collective-permute-done.58 = f32[32,512]{1,0:T(8,128)S(1)} collective-permute-done((f32[32,512]{1,0:T(8,128)S(1)}, f32[32,512]{1,0:T(8,128)S(1)}, u32[]{:S(2)}, u32[]{:S(2)}) %collective-permute-start.58) | collective-permute-done | bytes 65568 | tf_op jit(solution)/shard_map/ppermute | solution.py:328
  59.1 3.1 %collective-permute-done.57 = f32[1,256,128]{2,1,0:T(8,128)S(1)} collective-permute-done((f32[1,256,128]{2,1,0:T(8,128)S(1)}, f32[1,256,128]{2,1,0:T(8,128)S(1)}, u32[]{:S(2)}, u32[]{:S(2)}) %collective-permute-start.57) | collective-permute-done | bytes 131104 | tf_op jit(solution)/shard_map/ppermute | solution.py:328
  62.2 0.0 copy-start
  62.2 0.6 copy-done
  62.9 0.0 all-gather.3.cloned.1.call-update
  62.9 2.9 %collective-permute-start.61 = (f32[1,32,512]{2,1,0:T(8,128)S(1)}, f32[1,32,512]{2,1,0:T(8,128)S(1)}, u32[]{:S(2)}, u32[]{:S(2)}) collective-permute-start(f32[1,32,512]{2,1,0:T(8,128)S(1)} %bitcast.32), channel_id=1, source_target_pairs={{0,128},{1,129},{2,130},{3,131},{4,132},{5,133},{6,134},{7,135},{8... | collective-permute-start | bytes 196616 | tf_op jit(solution)/shard_map/ppermute | solution.py:328
  65.7 4.3 %collective-permute-done.61 = f32[1,32,512]{2,1,0:T(8,128)S(1)} collective-permute-done((f32[1,32,512]{2,1,0:T(8,128)S(1)}, f32[1,32,512]{2,1,0:T(8,128)S(1)}, u32[]{:S(2)}, u32[]{:S(2)}) %collective-permute-start.61) | collective-permute-done | bytes 65568 | tf_op jit(solution)/shard_map/ppermute | solution.py:328
  70.0 3.6 %collective-permute-start.62 = (f32[2,32,512]{2,1,0:T(8,128)S(1)}, f32[2,32,512]{2,1,0:T(8,128)S(1)}, u32[]{:S(2)}, u32[]{:S(2)}) collective-permute-start(f32[2,32,512]{2,1,0:T(8,128)S(1)} %pad_maximum_fusion.3), channel_id=1, source_target_pairs={{0,64},{1,65},{2,66},{3,67},{4,68},{5,69},{6,70},{7,71},{8,72},{9,... | collective-permute-start | bytes 393224 | tf_op jit(solution)/shard_map/ppermute | solution.py:328
  73.6 4.5 %collective-permute-done.62 = f32[2,32,512]{2,1,0:T(8,128)S(1)} collective-permute-done((f32[2,32,512]{2,1,0:T(8,128)S(1)}, f32[2,32,512]{2,1,0:T(8,128)S(1)}, u32[]{:S(2)}, u32[]{:S(2)}) %collective-permute-start.62) | collective-permute-done | bytes 131104 | tf_op jit(solution)/shard_map/ppermute | solution.py:328
  78.1 0.3 collective-permute-start.63
  78.4 6.7 %collective-permute-done.63 = f32[4,32,512]{2,1,0:T(8,128)S(1)} collective-permute-done((f32[4,32,512]{2,1,0:T(8,128)S(1)}, f32[4,32,512]{2,1,0:T(8,128)S(1)}, u32[]{:S(2)}, u32[]{:S(2)}) %collective-permute-start.63) | collective-permute-done | bytes 262176 | tf_op jit(solution)/shard_map/ppermute | solution.py:328
  85.1 5.4 %collective-permute-start.64 = (f32[8,32,512]{2,1,0:T(8,128)S(1)}, f32[8,32,512]{2,1,0:T(8,128)S(1)}, u32[]{:S(2)}, u32[]{:S(2)}) collective-permute-start(f32[8,32,512]{2,1,0:T(8,128)S(1)} %pad_maximum_fusion.own_ref), channel_id=1, source_target_pairs={{0,1},{1,0},{2,3},{3,2},{4,5},{5,4},{6,7},{7,6},{8,9},{9,8},{10,11... | collective-permute-start | bytes 1572872 | tf_op jit(solution)/shard_map/ppermute | solution.py:328
  90.5 2.9 %collective-permute-start.65 = (f32[2,256,128]{2,1,0:T(8,128)S(1)}, f32[2,256,128]{2,1,0:T(8,128)S(1)}, u32[]{:S(2)}, u32[]{:S(2)}) collective-permute-start(f32[2,256,128]{2,1,0:T(8,128)S(1)} %pad_maximum_fusion.1), channel_id=1, source_target_pairs={{0,64},{1,65},{2,66},{3,67},{4,68},{5,69},{6,70},{7,71},{8,72},{9,... | collective-permute-start | bytes 786440 | tf_op jit(solution)/shard_map/ppermute | solution.py:328
  93.4 12.2 %first.1 = (f32[256,256]{1,0:T(8,128)S(1)}, f32[256,256]{1,0:T(8,128)S(1)}, f32[256,256]{1,0:T(8,128)S(1)}) custom-call(s32[7]{0:T(128)S(1)} %stack.27.info, f32[8,32,512]{2,1,0:T(8,128)S(1)} %pad_maximum_fusion.own_ref, f32[8,32,512]{2,1,0:T(8,128)S(1)} %collective-permute-done.64.twin_ref), custom_call_target="tpu_custom_call" | custom-call | flops 100000000 | bytes 40000000 | tf_op jit(solution)/shard_map/first/pallas_call | solution.py:225
  105.6 0.1 collective-permute-done.65
  105.7 0.3 collective-permute-start.66
  106.1 11.1 %second.1 = (f32[256,256]{1,0:T(8,128)S(1)}, f32[256,256]{1,0:T(8,128)S(1)}) custom-call(f32[256,256]{1,0:T(8,128)S(1)} %get-tuple-element.116.w_ref, f32[256,256]{1,0:T(8,128)S(1)} %get-tuple-element.117.rest_ref), custom_call_target="tpu_custom_call" | custom-call | flops 100000000 | bytes 40000000 | tf_op jit(solution)/shard_map/second/pallas_call | solution.py:229
  117.2 1.8 %collective-permute-done.66.far_ref = f32[4,256,128]{2,1,0:T(8,128)S(1)} collective-permute-done((f32[4,256,128]{2,1,0:T(8,128)S(1)}, f32[4,256,128]{2,1,0:T(8,128)S(1)}, u32[]{:S(2)}, u32[]{:S(2)}) %collective-permute-start.66) | collective-permute-done | bytes 524320 | tf_op jit(solution)/shard_map/ppermute | solution.py:328
  119.0 2.2 %cross.1 = (bf16[1536,512]{1,0:T(8,128)(2,1)S(1)}, bf16[1536,512]{1,0:T(8,128)(2,1)S(1)}) custom-call(s32[7]{0:T(128)S(1)} %stack.27.info, f32[256,256]{1,0:T(8,128)S(1)} %get-tuple-element.112.first_ref, f32[256,256]{1,0:T(8,128)S(1)} %get-tuple-element.118.second_ref, f32[256,256]{1,0:T(8,128)S(1)} %get-tuple-element.119.corner_ref, ...), custom_call_target="tpu_custom_call" | custom-call | tf_op jit(solution)/shard_map/cross/pallas_call | solution.py:254
  121.2 0.0 all-gather.3.cloned.1.call-done
  121.2 11.8 %update.1 = (f32[2,2,4,256,256]{4,3,2,1,0:T(8,128)}, f32[2,4,1024,128]{3,2,1,0:T(8,128)}) custom-call(s32[7]{0:T(128)S(1)} %stack.27.info, bf16[1536,512]{1,0:T(8,128)(2,1)S(1)} %get-tuple-element.122.w_ref, bf16[1536,512]{1,0:T(8,128)(2,1)S(1)} %get-tuple-element.123.c_ref, f32[32,256,128]{2,1,0:T(8,128)} %bitcast.29, f32[2,4,1024,128]{3,2,1,0:T(8,128)} %bitcast.28), custom_call_target="tpu_custom_call" | custom-call | tf_op jit(solution)/shard_map/update/pallas_call | solution.py:289
  (28 shorter events, 0.3 us)
Async XLA Ops:
  7.2 114.1 %all-gather.3.cloned.1.call-start = ((), (), s32[]{:S(2)}) async-start(), calls=%async_computation | async-start | bytes 4325376 | tf_op jit(solution)/shard_map/all_gather | solution.py:389
  13.0 16.0 %copy-start.1 = (s32[2]{0:T(128)S(1)}, s32[2]{0:T(128)}, u32[]{:S(2)}) copy-start(s32[2]{0:T(128)} %param.11) | copy-start | bytes 28
  13.0 4.0 %collective-permute-start.18 = (f32[256,128]{1,0:T(8,128)S(1)}, f32[256,128]{1,0:T(8,128)S(1)}, u32[]{:S(2)}, u32[]{:S(2)}) collective-permute-start(f32[256,128]{1,0:T(8,128)S(1)} %get-tuple-element.142), channel_id=1, source_target_pairs={{224,32},{225,33},{226,34},{227,35},{228,36},{229,37},{230,38},{23... | collective-permute-start | bytes 393224 | tf_op jit(solution)/shard_map/cond/branch_2_fun/ppermute | solution.py:346
  13.7 4.1 %collective-permute-start.16 = (f32[256,128]{1,0:T(8,128)S(1)}, f32[256,128]{1,0:T(8,128)S(1)}, u32[]{:S(2)}, u32[]{:S(2)}) collective-permute-start(f32[256,128]{1,0:T(8,128)S(1)} %get-tuple-element.143), channel_id=1, source_target_pairs={{224,96},{225,97},{226,98},{227,99},{228,100},{229,101},{230,102},... | collective-permute-start | bytes 393224 | tf_op jit(solution)/shard_map/cond/branch_2_fun/ppermute | solution.py:346
  14.4 3.4 %collective-permute-start.15 = (f32[256,128]{1,0:T(8,128)S(1)}, f32[256,128]{1,0:T(8,128)S(1)}, u32[]{:S(2)}, u32[]{:S(2)}) collective-permute-start(f32[256,128]{1,0:T(8,128)S(1)} %get-tuple-element.144), channel_id=1, source_target_pairs={{224,160},{225,161},{226,162},{227,163},{228,164},{229,165},{230,1... | collective-permute-start | bytes 393224 | tf_op jit(solution)/shard_map/cond/branch_2_fun/ppermute | solution.py:346
  15.1 7.5 %collective-permute-start.17 = (f32[256,128]{1,0:T(8,128)S(1)}, f32[256,128]{1,0:T(8,128)S(1)}, u32[]{:S(2)}, u32[]{:S(2)}) collective-permute-start(f32[256,128]{1,0:T(8,128)S(1)} %get-tuple-element.145), channel_id=1, source_target_pairs={{64,0},{65,1},{66,2},{67,3},{68,4},{69,5},{70,6},{71,7},{72,8},{73... | collective-permute-start | bytes 393224 | tf_op jit(solution)/shard_map/cond/branch_2_fun/ppermute | solution.py:352
  16.4 6.2 %collective-permute-start.14 = (f32[256,128]{1,0:T(8,128)S(1)}, f32[256,128]{1,0:T(8,128)S(1)}, u32[]{:S(2)}, u32[]{:S(2)}) collective-permute-start(f32[256,128]{1,0:T(8,128)S(1)} %get-tuple-element.146), channel_id=1, source_target_pairs={{64,128},{65,129},{66,130},{67,131},{68,132},{69,133},{70,134},{71... | collective-permute-start | bytes 393224 | tf_op jit(solution)/shard_map/cond/branch_2_fun/ppermute | solution.py:352
  17.1 5.5 %collective-permute-start.13 = (f32[256,128]{1,0:T(8,128)S(1)}, f32[256,128]{1,0:T(8,128)S(1)}, u32[]{:S(2)}, u32[]{:S(2)}) collective-permute-start(f32[256,128]{1,0:T(8,128)S(1)} %get-tuple-element.147), channel_id=1, source_target_pairs={{64,192},{65,193},{66,194},{67,195},{68,196},{69,197},{70,198},{71... | collective-permute-start | bytes 393224 | tf_op jit(solution)/shard_map/cond/branch_2_fun/ppermute | solution.py:352
  22.6 39.6 %collective-permute-start.52 = (f32[256,128]{1,0:T(8,128)S(1)}, f32[256,128]{1,0:T(8,128)S(1)}, u32[]{:S(2)}, u32[]{:S(2)}) collective-permute-start(f32[256,128]{1,0:T(8,128)S(1)} %get-tuple-element.187.piece_ref), channel_id=1, source_target_pairs={{0,0},{1,32},{2,64},{3,96},{4,128},{5,160},{6,192},{7,224},{8,8},{... | collective-permute-start | bytes 393224 | tf_op jit(solution)/shard_map/ppermute | solution.py:328
  29.6 1.4 %collective-permute-start.53 = (f32[64,512]{1,0:T(8,128)S(1)}, f32[64,512]{1,0:T(8,128)S(1)}, u32[]{:S(2)}, u32[]{:S(2)}) collective-permute-start(f32[64,512]{1,0:T(8,128)S(1)} %pick.1), channel_id=1, source_target_pairs={{0,1},{1,0},{2,3},{3,2},{4,5},{5,4},{6,7},{7,6},{8,9},{9,8},{10,11... | collective-permute-start | bytes 393224 | tf_op jit(solution)/shard_map/ppermute | solution.py:328
  31.1 4.0 %collective-permute-start.56 = (f32[32,512]{1,0:T(8,128)S(1)}, f32[32,512]{1,0:T(8,128)S(1)}, u32[]{:S(2)}, u32[]{:S(2)}) collective-permute-start(f32[32,512]{1,0:T(8,128)S(1)} %dynamic-slice_select_fusion), channel_id=1, source_target_pairs={{0,8},{1,9},{2,10},{3,11},{4,12},{5,13},{6,14},{7,15},{8,0},{9,1},... | collective-permute-start | bytes 196616 | tf_op jit(solution)/shard_map/ppermute | solution.py:328
  32.4 5.9 %collective-permute-start.55 = (f32[32,512]{1,0:T(8,128)S(1)}, f32[32,512]{1,0:T(8,128)S(1)}, u32[]{:S(2)}, u32[]{:S(2)}) collective-permute-start(f32[32,512]{1,0:T(8,128)S(1)} %dynamic-slice_select_fusion), channel_id=1, source_target_pairs={{0,16},{1,17},{2,18},{3,19},{4,20},{5,21},{6,22},{7,23},{8,24},{9,... | collective-permute-start | bytes 196616 | tf_op jit(solution)/shard_map/ppermute | solution.py:328
  34.8 4.5 %collective-permute-start.54 = (f32[32,512]{1,0:T(8,128)S(1)}, f32[32,512]{1,0:T(8,128)S(1)}, u32[]{:S(2)}, u32[]{:S(2)}) collective-permute-start(f32[32,512]{1,0:T(8,128)S(1)} %dynamic-slice_select_fusion), channel_id=1, source_target_pairs={{0,24},{1,25},{2,26},{3,27},{4,28},{5,29},{6,30},{7,31},{8,16},{9,... | collective-permute-start | bytes 196616 | tf_op jit(solution)/shard_map/ppermute | solution.py:328
  39.3 17.8 %collective-permute-start.60 = (f32[32,512]{1,0:T(8,128)S(1)}, f32[32,512]{1,0:T(8,128)S(1)}, u32[]{:S(2)}, u32[]{:S(2)}) collective-permute-start(f32[32,512]{1,0:T(8,128)S(1)} %select_select_fusion.9), channel_id=1, source_target_pairs={{0,2},{1,3},{2,0},{3,1},{4,6},{5,7},{6,4},{7,5},{8,10},{9,11},{10,... | collective-permute-start | bytes 196616 | tf_op jit(solution)/shard_map/ppermute | solution.py:328
  49.4 7.7 %collective-permute-start.59 = (f32[32,512]{1,0:T(8,128)S(1)}, f32[32,512]{1,0:T(8,128)S(1)}, u32[]{:S(2)}, u32[]{:S(2)}) collective-permute-start(f32[32,512]{1,0:T(8,128)S(1)} %select_select_fusion.9), channel_id=1, source_target_pairs={{0,4},{1,5},{2,6},{3,7},{4,0},{5,1},{6,2},{7,3},{8,12},{9,13},{10,... | collective-permute-start | bytes 196616 | tf_op jit(solution)/shard_map/ppermute | solution.py:328
  54.2 4.9 %collective-permute-start.58 = (f32[32,512]{1,0:T(8,128)S(1)}, f32[32,512]{1,0:T(8,128)S(1)}, u32[]{:S(2)}, u32[]{:S(2)}) collective-permute-start(f32[32,512]{1,0:T(8,128)S(1)} %select_select_fusion.9), channel_id=1, source_target_pairs={{0,6},{1,7},{2,4},{3,5},{4,2},{5,3},{6,0},{7,1},{8,14},{9,15},{10,... | collective-permute-start | bytes 196616 | tf_op jit(solution)/shard_map/ppermute | solution.py:328
  54.3 7.8 %collective-permute-start.57 = (f32[1,256,128]{2,1,0:T(8,128)S(1)}, f32[1,256,128]{2,1,0:T(8,128)S(1)}, u32[]{:S(2)}, u32[]{:S(2)}) collective-permute-start(f32[1,256,128]{2,1,0:T(8,128)S(1)} %bitcast.30), channel_id=1, source_target_pairs={{0,128},{1,129},{2,130},{3,131},{4,132},{5,133},{6,134},{7,135},{8... | collective-permute-start | bytes 393224 | tf_op jit(solution)/shard_map/ppermute | solution.py:328
  62.2 0.7 copy-start
  62.9 7.1 %collective-permute-start.61 = (f32[1,32,512]{2,1,0:T(8,128)S(1)}, f32[1,32,512]{2,1,0:T(8,128)S(1)}, u32[]{:S(2)}, u32[]{:S(2)}) collective-permute-start(f32[1,32,512]{2,1,0:T(8,128)S(1)} %bitcast.32), channel_id=1, source_target_pairs={{0,128},{1,129},{2,130},{3,131},{4,132},{5,133},{6,134},{7,135},{8... | collective-permute-start | bytes 196616 | tf_op jit(solution)/shard_map/ppermute | solution.py:328
  70.0 8.0 %collective-permute-start.62 = (f32[2,32,512]{2,1,0:T(8,128)S(1)}, f32[2,32,512]{2,1,0:T(8,128)S(1)}, u32[]{:S(2)}, u32[]{:S(2)}) collective-permute-start(f32[2,32,512]{2,1,0:T(8,128)S(1)} %pad_maximum_fusion.3), channel_id=1, source_target_pairs={{0,64},{1,65},{2,66},{3,67},{4,68},{5,69},{6,70},{7,71},{8,72},{9,... | collective-permute-start | bytes 393224 | tf_op jit(solution)/shard_map/ppermute | solution.py:328
  78.1 7.0 %collective-permute-start.63 = (f32[4,32,512]{2,1,0:T(8,128)S(1)}, f32[4,32,512]{2,1,0:T(8,128)S(1)}, u32[]{:S(2)}, u32[]{:S(2)}) collective-permute-start(f32[4,32,512]{2,1,0:T(8,128)S(1)} %pad_maximum_fusion.2), channel_id=1, source_target_pairs={{0,32},{1,33},{2,34},{3,35},{4,36},{5,37},{6,38},{7,39},{8,40},{9,... | collective-permute-start | bytes 786440 | tf_op jit(solution)/shard_map/ppermute | solution.py:328
  85.1 8.2 %collective-permute-start.64 = (f32[8,32,512]{2,1,0:T(8,128)S(1)}, f32[8,32,512]{2,1,0:T(8,128)S(1)}, u32[]{:S(2)}, u32[]{:S(2)}) collective-permute-start(f32[8,32,512]{2,1,0:T(8,128)S(1)} %pad_maximum_fusion.own_ref), channel_id=1, source_target_pairs={{0,1},{1,0},{2,3},{3,2},{4,5},{5,4},{6,7},{7,6},{8,9},{9,8},{10,11... | collective-permute-start | bytes 1572872 | tf_op jit(solution)/shard_map/ppermute | solution.py:328
  90.5 15.2 %collective-permute-start.65 = (f32[2,256,128]{2,1,0:T(8,128)S(1)}, f32[2,256,128]{2,1,0:T(8,128)S(1)}, u32[]{:S(2)}, u32[]{:S(2)}) collective-permute-start(f32[2,256,128]{2,1,0:T(8,128)S(1)} %pad_maximum_fusion.1), channel_id=1, source_target_pairs={{0,64},{1,65},{2,66},{3,67},{4,68},{5,69},{6,70},{7,71},{8,72},{9,... | collective-permute-start | bytes 786440 | tf_op jit(solution)/shard_map/ppermute | solution.py:328
  105.7 13.2 %collective-permute-start.66 = (f32[4,256,128]{2,1,0:T(8,128)S(1)}, f32[4,256,128]{2,1,0:T(8,128)S(1)}, u32[]{:S(2)}, u32[]{:S(2)}) collective-permute-start(f32[4,256,128]{2,1,0:T(8,128)S(1)} %constant_dynamic-update-slice_fusion.near_ref), channel_id=1, source_target_pairs={{0,32},{1,33},{2,34},{3,35},{4,36},{5,37},{6,38},{7,39},{8,40},{9,... | collective-permute-start | bytes 1572872 | tf_op jit(solution)/shard_map/ppermute | solution.py:328
Sparse Core Ops, SparseCore 0:
  63.0 52.3 all-gather.2

commit v6 on v5

--- a/solution.py
+++ b/solution.py
@@ -200,19 +200,25 @@
     w_ref[...] = dot3(below, inverse)
 
 
-def second_kernel(w_ref, rest_ref, m_ref, corner_ref, s_ref, z_ref):
+def second_kernel(info, first_ref, carried_ref, rest_ref, w_ref, t_ref, x_ref, m_ref, s_ref, z_ref):
     s_ref[...] = rest_ref[...]
     factor_inverse(s_ref, z_ref, m_ref)
-    corner_ref[...] = -product(m_ref[...], w_ref[...])
+    t_ref[:NB, :NB] = first_ref[...].T
+    t_ref[:NB, NB:] = (-product(m_ref[...], carried_ref[...])).T
+    t_ref[NB:, :NB] = jnp.zeros((NB, NB), jnp.float32)
+    t_ref[NB:, NB:] = m_ref[...].T
+    for plane in range(PLANES):
+        start = pl.multiple_of(place_of(info, plane) * CHUNK, CHUNK)
+        x_ref[plane * CHUNK : (plane + 1) * CHUNK, :] = t_ref[pl.ds(start, CHUNK), :]
+    w_ref[...] = stack(split(x_ref[...]))
 
 
 def stage(kernel, name, inputs, outputs, scratch):
-    square = lambda: jax.ShapeDtypeStruct((NB, NB), jnp.float32)
     return pl.pallas_call(
         kernel,
-        out_shape=[square() for _ in range(outputs)],
+        out_shape=outputs,
         in_specs=inputs,
-        out_specs=[VMEM] * outputs,
+        out_specs=[VMEM] * len(outputs),
         scratch_shapes=scratch + [pltpu.VMEM((NB, NB), jnp.float32)] * 2,
         compiler_params=PARAMS,
         cost_estimate=pl.CostEstimate(flops=10**8, transcendentals=0, bytes_accessed=4 * 10**7),
@@ -222,24 +228,19 @@
 
 def first_factor(info, own, twin):
     whole = [pltpu.VMEM((2 * NB, 2 * NB), jnp.float32)]
-    return stage(first_kernel, "first", [SMEM, VMEM, VMEM], 3, whole)(info, own, twin)
-
-
-def second_factor(carried, rest):
-    return stage(second_kernel, "second", [VMEM, VMEM], 2, [])(carried, rest)
-
-
-def cross_kernel(info, first_ref, second_ref, corner_ref, near_ref, far_ref, w_ref, c_ref, t_ref, x_ref):
-    t_ref[:NB, :NB] = first_ref[...].T
-    t_ref[:NB, NB:] = corner_ref[...].T
-    t_ref[NB:, :NB] = jnp.zeros((NB, NB), jnp.float32)
-    t_ref[NB:, NB:] = second_ref[...].T
-    for plane in range(PLANES):
-        start = pl.multiple_of(place_of(info, plane) * CHUNK, CHUNK)
-        x_ref[plane * CHUNK : (plane + 1) * CHUNK, :] = t_ref[pl.ds(start, CHUNK), :]
-    weights = split(x_ref[...])
-    w_ref[...] = stack(weights)
-    high, low = weights[0].T, weights[1].T
+    outputs = [jax.ShapeDtypeStruct((NB, NB), jnp.float32)] * 3
+    return stage(first_kernel, "first", [SMEM, VMEM, VMEM], outputs, whole)(info, own, twin)
+
+
+def second_factor(info, first, carried, rest):
+    scratch = [pltpu.VMEM((2 * NB, 2 * NB), jnp.float32)] * 2 + [pltpu.VMEM((NB, NB), jnp.float32)]
+    outputs = [jax.ShapeDtypeStruct((6 * NB, 2 * NB), jnp.bfloat16)]
+    return stage(second_kernel, "second", [SMEM, VMEM, VMEM, VMEM], outputs, scratch)(info, first, carried, rest)[0]
+
+
+def cross_kernel(info, w_ref, near_ref, far_ref, c_ref, x_ref):
+    n = 2 * NB
+    high, low = w_ref[:n].T, w_ref[n : 2 * n].T
     for slot in range(PLANES):
         ref = (near_ref, far_ref)[slot // 4].at[slot % 4]
         start = pl.multiple_of((info[ROW] ^ MASKS[slot]) * CHUNK, CHUNK)
@@ -249,17 +250,17 @@
     c_ref[...] = stack(split(jnp.dot(rows, stack(split(x_ref[...])), preferred_element_type=jnp.float32)))
 
 
-def cross(info, first, second, corner, near, far):
+def cross(info, weights, near, far):
     n = 2 * NB
     return pl.pallas_call(
         cross_kernel,
-        out_shape=[jax.ShapeDtypeStruct((3 * n, n), jnp.bfloat16)] * 2,
-        in_specs=[SMEM] + [VMEM] * 5,
-        out_specs=[VMEM] * 2,
-        scratch_shapes=[pltpu.VMEM((n, n), jnp.float32)] * 2,
+        out_shape=jax.ShapeDtypeStruct((3 * n, n), jnp.bfloat16),
+        in_specs=[SMEM] + [VMEM] * 3,
+        out_specs=VMEM,
+        scratch_shapes=[pltpu.VMEM((n, n), jnp.float32)],
         compiler_params=PARAMS,
         name="cross",
-    )(info, first, second, corner, near, far)
+    )(info, weights, near, far)
 
 
 def update_kernel(info, w_ref, c_ref, g_ref, a_ref, panels_ref, t_ref):
@@ -394,8 +395,8 @@
     crossing, facing, carried, rest = tie(crossing, facing, carried, rest)
     crossing = jnp.concatenate([crossing, facing], axis=0)
     beyond = send(crossing, lambda a, b: (a ^ 1, b))
-    second, corner = second_factor(carried, rest)
-    factors = cross(info, first, second, corner, crossing, beyond)
+    weights = second_factor(info, first, carried, rest)
+    factors = weights, cross(info, weights, crossing, beyond)
     panels, trailing = update(info, factors, gathered, flat)
     return panels.reshape(2, br, 1, NB, NB), trailing.reshape(kernel.shape)
 

time: 140 us -> 138 us (0.986)
  no operation moved by 1% of the time
where the time goes in v6:
time: 138 us; the launch traced here: 139 us
  starting transfers between devices  48.1 us (35%)
  Pallas kernels  38.2 us (28%)
  waiting for transfers between devices  31.8 us (23%)
  between operations  16.2 us (12%)
  local copies, waits for them, and re-layouts  4.64 us (3%)
    ppermute x15, starting transfers between devices, shards(): lax.ppermute(value, AXES, [(device(a, b), device(*to(a, b))) for a, b in...  43.4 us
    ppermute x15, waiting for transfers between devices, shards(): lax.ppermute(value, AXES, [(device(a, b), device(*to(a, b))) for a, b in...  27 us
    pallas_call x1, Pallas kernels, first_factor(): stage(first_kernel, 'first', [SMEM, VMEM, VMEM], outputs, whole)  12.2 us
    pallas_call x1, Pallas kernels, second_factor(): stage(second_kernel, 'second', [SMEM, VMEM, VMEM, VMEM], outputs, scratch)  12 us
    pallas_call x1, Pallas kernels, update(): pl.pallas_call(update_kernel, grid_spec=pltpu.PrefetchScalarGridSpec(num_...  11.8 us
    ppermute x3, waiting for transfers between devices, run(): arrived.append((plane, lax.ppermute(part(others, q), AXES, pairs)))  4.76 us
  transfers between devices with their start and end apart: 22, of which 11 were waited for; matrix products, arithmetic and copies ran while one was open for 0% of the time, Pallas kernels for 19%

profile of v6, /device:TPU:1, one launch (start us, length us, event | category | flops | bytes accessed | tf_op | source)
XLA Modules:
  0.0 139.3 jit_solution(5855014910721457699)
XLA Ops:
  7.2 0.0 all-gather.3.cloned.1.call-start
  7.2 1.3 fusion.17
  10.4 1.4 %slice.221 = f32[1,1,256,2,1,256]{5,4,3,2,1,0:T(1,128)S(1)} slice(f32[8,1,256,2,1,256]{5,4,3,2,1,0:T(1,128)} %param.10), slice={[7:8], [0:1], [0:256], [0:2], [0:1], [0:256]} | slice | bytes 1048576 | tf_op jit(solution)/shard_map/slice | solution.py:365
  11.8 1.1 dynamic-slice_bitcast_fusion
  12.9 0.0 copy-start.1
  12.9 9.7 %conditional.1 = (f32[256,128]{1,0:T(8,128)S(1)}) conditional(s32[]{:T(128)} %clamp.3, (s32[]{:T(128)}, f32[1024,128]{1,0:T(8,128)S(1)}, f32[1024,128]{1,0:T(8,128)S(1)}) %tuple.95, (s32[]{:T(128)}, f32[1024,128]{1,0:T(8,128)S(1)}, f32[1024,128]{1,0:T(8,128)S(1)}) %tuple.99, (s32[]{:T(128)}, ...), branch_computations={%region_0.1_spmd, %region_1.2_spmd, %region_2.3_spmd, %region_3.4_... | conditional | flops 229383 | bytes 6685030 | solution.py:366
  13.0 0.7 collective-permute-start.18
  13.7 0.7 collective-permute-start.16
  14.4 0.7 collective-permute-start.15
  15.1 1.3 collective-permute-start.17
  16.4 0.7 collective-permute-start.14
  17.1 0.7 collective-permute-start.13
  17.8 4.8 %collective-permute-done.17 = f32[256,128]{1,0:T(8,128)S(1)} collective-permute-done((f32[256,128]{1,0:T(8,128)S(1)}, f32[256,128]{1,0:T(8,128)S(1)}, u32[]{:S(2)}, u32[]{:S(2)}) %collective-permute-start.17) | collective-permute-done | bytes 131104 | tf_op jit(solution)/shard_map/cond/branch_2_fun/ppermute | solution.py:353
  22.6 6.3 %collective-permute-start.52 = (f32[256,128]{1,0:T(8,128)S(1)}, f32[256,128]{1,0:T(8,128)S(1)}, u32[]{:S(2)}, u32[]{:S(2)}) collective-permute-start(f32[256,128]{1,0:T(8,128)S(1)} %get-tuple-element.179.piece_ref), channel_id=1, source_target_pairs={{0,0},{1,32},{2,64},{3,96},{4,128},{5,160},{6,192},{7,224},{8,8},{... | collective-permute-start | bytes 393224 | tf_op jit(solution)/shard_map/ppermute | solution.py:329
  29.0 0.1 stack.27.info
  29.0 0.6 pick.1
  29.6 0.1 collective-permute-start.53
  29.8 1.3 collective-permute-done.53
  31.1 1.3 collective-permute-start.56
  32.3 2.5 %collective-permute-start.55 = (f32[32,512]{1,0:T(8,128)S(1)}, f32[32,512]{1,0:T(8,128)S(1)}, u32[]{:S(2)}, u32[]{:S(2)}) collective-permute-start(f32[32,512]{1,0:T(8,128)S(1)} %dynamic-slice_select_fusion), channel_id=1, source_target_pairs={{0,16},{1,17},{2,18},{3,19},{4,20},{5,21},{6,22},{7,23},{8,24},{9,... | collective-permute-start | bytes 196616 | tf_op jit(solution)/shard_map/ppermute | solution.py:329
  34.8 0.2 collective-permute-start.54
  35.0 3.3 %collective-permute-done.55 = f32[32,512]{1,0:T(8,128)S(1)} collective-permute-done((f32[32,512]{1,0:T(8,128)S(1)}, f32[32,512]{1,0:T(8,128)S(1)}, u32[]{:S(2)}, u32[]{:S(2)}) %collective-permute-start.55) | collective-permute-done | bytes 65568 | tf_op jit(solution)/shard_map/ppermute | solution.py:329
  38.3 1.0 collective-permute-done.54
  39.3 10.1 %collective-permute-start.60 = (f32[32,512]{1,0:T(8,128)S(1)}, f32[32,512]{1,0:T(8,128)S(1)}, u32[]{:S(2)}, u32[]{:S(2)}) collective-permute-start(f32[32,512]{1,0:T(8,128)S(1)} %select_select_fusion.9), channel_id=1, source_target_pairs={{0,2},{1,3},{2,0},{3,1},{4,6},{5,7},{6,4},{7,5},{8,10},{9,11},{10,... | collective-permute-start | bytes 196616 | tf_op jit(solution)/shard_map/ppermute | solution.py:329
  49.4 4.7 %collective-permute-start.59 = (f32[32,512]{1,0:T(8,128)S(1)}, f32[32,512]{1,0:T(8,128)S(1)}, u32[]{:S(2)}, u32[]{:S(2)}) collective-permute-start(f32[32,512]{1,0:T(8,128)S(1)} %select_select_fusion.9), channel_id=1, source_target_pairs={{0,4},{1,5},{2,6},{3,7},{4,0},{5,1},{6,2},{7,3},{8,12},{9,13},{10,... | collective-permute-start | bytes 196616 | tf_op jit(solution)/shard_map/ppermute | solution.py:329
  54.1 0.2 collective-permute-start.58
  54.3 2.8 %collective-permute-start.57 = (f32[1,256,128]{2,1,0:T(8,128)S(1)}, f32[1,256,128]{2,1,0:T(8,128)S(1)}, u32[]{:S(2)}, u32[]{:S(2)}) collective-permute-start(f32[1,256,128]{2,1,0:T(8,128)S(1)} %bitcast.30), channel_id=1, source_target_pairs={{0,128},{1,129},{2,130},{3,131},{4,132},{5,133},{6,134},{7,135},{8... | collective-permute-start | bytes 393224 | tf_op jit(solution)/shard_map/ppermute | solution.py:329
  57.1 1.9 %collective-permute-done.58 = f32[32,512]{1,0:T(8,128)S(1)} collective-permute-done((f32[32,512]{1,0:T(8,128)S(1)}, f32[32,512]{1,0:T(8,128)S(1)}, u32[]{:S(2)}, u32[]{:S(2)}) %collective-permute-start.58) | collective-permute-done | bytes 65568 | tf_op jit(solution)/shard_map/ppermute | solution.py:329
  59.0 3.1 %collective-permute-done.57 = f32[1,256,128]{2,1,0:T(8,128)S(1)} collective-permute-done((f32[1,256,128]{2,1,0:T(8,128)S(1)}, f32[1,256,128]{2,1,0:T(8,128)S(1)}, u32[]{:S(2)}, u32[]{:S(2)}) %collective-permute-start.57) | collective-permute-done | bytes 131104 | tf_op jit(solution)/shard_map/ppermute | solution.py:329
  62.2 0.0 copy-start
  62.2 0.6 copy-done
  62.8 0.0 all-gather.3.cloned.1.call-update
  62.9 2.9 %collective-permute-start.61 = (f32[1,32,512]{2,1,0:T(8,128)S(1)}, f32[1,32,512]{2,1,0:T(8,128)S(1)}, u32[]{:S(2)}, u32[]{:S(2)}) collective-permute-start(f32[1,32,512]{2,1,0:T(8,128)S(1)} %bitcast.32), channel_id=1, source_target_pairs={{0,128},{1,129},{2,130},{3,131},{4,132},{5,133},{6,134},{7,135},{8... | collective-permute-start | bytes 196616 | tf_op jit(solution)/shard_map/ppermute | solution.py:329
  65.7 4.3 %collective-permute-done.61 = f32[1,32,512]{2,1,0:T(8,128)S(1)} collective-permute-done((f32[1,32,512]{2,1,0:T(8,128)S(1)}, f32[1,32,512]{2,1,0:T(8,128)S(1)}, u32[]{:S(2)}, u32[]{:S(2)}) %collective-permute-start.61) | collective-permute-done | bytes 65568 | tf_op jit(solution)/shard_map/ppermute | solution.py:329
  70.0 3.6 %collective-permute-start.62 = (f32[2,32,512]{2,1,0:T(8,128)S(1)}, f32[2,32,512]{2,1,0:T(8,128)S(1)}, u32[]{:S(2)}, u32[]{:S(2)}) collective-permute-start(f32[2,32,512]{2,1,0:T(8,128)S(1)} %pad_maximum_fusion.3), channel_id=1, source_target_pairs={{0,64},{1,65},{2,66},{3,67},{4,68},{5,69},{6,70},{7,71},{8,72},{9,... | collective-permute-start | bytes 393224 | tf_op jit(solution)/shard_map/ppermute | solution.py:329
  73.6 4.5 %collective-permute-done.62 = f32[2,32,512]{2,1,0:T(8,128)S(1)} collective-permute-done((f32[2,32,512]{2,1,0:T(8,128)S(1)}, f32[2,32,512]{2,1,0:T(8,128)S(1)}, u32[]{:S(2)}, u32[]{:S(2)}) %collective-permute-start.62) | collective-permute-done | bytes 131104 | tf_op jit(solution)/shard_map/ppermute | solution.py:329
  78.0 0.3 collective-permute-start.63
  78.3 6.7 %collective-permute-done.63 = f32[4,32,512]{2,1,0:T(8,128)S(1)} collective-permute-done((f32[4,32,512]{2,1,0:T(8,128)S(1)}, f32[4,32,512]{2,1,0:T(8,128)S(1)}, u32[]{:S(2)}, u32[]{:S(2)}) %collective-permute-start.63) | collective-permute-done | bytes 262176 | tf_op jit(solution)/shard_map/ppermute | solution.py:329
  85.1 5.4 %collective-permute-start.64 = (f32[8,32,512]{2,1,0:T(8,128)S(1)}, f32[8,32,512]{2,1,0:T(8,128)S(1)}, u32[]{:S(2)}, u32[]{:S(2)}) collective-permute-start(f32[8,32,512]{2,1,0:T(8,128)S(1)} %pad_maximum_fusion.own_ref), channel_id=1, source_target_pairs={{0,1},{1,0},{2,3},{3,2},{4,5},{5,4},{6,7},{7,6},{8,9},{9,8},{10,11... | collective-permute-start | bytes 1572872 | tf_op jit(solution)/shard_map/ppermute | solution.py:329
  90.5 2.9 %collective-permute-start.65 = (f32[2,256,128]{2,1,0:T(8,128)S(1)}, f32[2,256,128]{2,1,0:T(8,128)S(1)}, u32[]{:S(2)}, u32[]{:S(2)}) collective-permute-start(f32[2,256,128]{2,1,0:T(8,128)S(1)} %pad_maximum_fusion.1), channel_id=1, source_target_pairs={{0,64},{1,65},{2,66},{3,67},{4,68},{5,69},{6,70},{7,71},{8,72},{9,... | collective-permute-start | bytes 786440 | tf_op jit(solution)/shard_map/ppermute | solution.py:329
  93.4 12.2 %first.1 = (f32[256,256]{1,0:T(8,128)S(1)}, f32[256,256]{1,0:T(8,128)S(1)}, f32[256,256]{1,0:T(8,128)S(1)}) custom-call(s32[7]{0:T(128)S(1)} %stack.27.info, f32[8,32,512]{2,1,0:T(8,128)S(1)} %pad_maximum_fusion.own_ref, f32[8,32,512]{2,1,0:T(8,128)S(1)} %collective-permute-done.64.twin_ref), custom_call_target="tpu_custom_call" | custom-call | flops 100000000 | bytes 40000000 | tf_op jit(solution)/shard_map/first/pallas_call | solution.py:232
  105.6 0.1 collective-permute-done.65
  105.7 0.3 collective-permute-start.66
  106.0 12.0 %second.1.w_ref = bf16[1536,512]{1,0:T(8,128)(2,1)S(1)} custom-call(s32[7]{0:T(128)S(1)} %stack.27.info, f32[256,256]{1,0:T(8,128)S(1)} %get-tuple-element.108.first_ref, f32[256,256]{1,0:T(8,128)S(1)} %get-tuple-element.112.carried_ref, f32[256,256]{1,0:T(8,128)S(1)} %get-tuple-element.113.rest_ref), custom_call_target="tpu_custom_call" | custom-call | flops 100000000 | bytes 40000000 | tf_op jit(solution)/shard_map/second/pallas_call | solution.py:238
  118.1 0.9 collective-permute-done.66.far_ref
  119.0 1.6 %cross.1.c_ref = bf16[1536,512]{1,0:T(8,128)(2,1)S(1)} custom-call(s32[7]{0:T(128)S(1)} %stack.27.info, bf16[1536,512]{1,0:T(8,128)(2,1)S(1)} %second.1.w_ref, f32[4,256,128]{2,1,0:T(8,128)S(1)} %constant_dynamic-update-slice_fusion.near_ref, f32[4,256,128]{2,1,0:T(8,128)S(1)} %collective-permute-done.66.far_ref), custom_call_target="tpu_custom_call" | custom-call | tf_op jit(solution)/shard_map/cross/pallas_call | solution.py:255
  120.6 0.0 all-gather.3.cloned.1.call-done
  120.6 11.8 %update.1 = (f32[2,2,4,256,256]{4,3,2,1,0:T(8,128)}, f32[2,4,1024,128]{3,2,1,0:T(8,128)}) custom-call(s32[7]{0:T(128)S(1)} %stack.27.info, bf16[1536,512]{1,0:T(8,128)(2,1)S(1)} %second.1.w_ref, bf16[1536,512]{1,0:T(8,128)(2,1)S(1)} %cross.1.c_ref, f32[32,256,128]{2,1,0:T(8,128)} %bitcast.29, f32[2,4,1024,128]{3,2,1,0:T(8,128)} %bitcast.28), custom_call_target="tpu_custom_call" | custom-call | tf_op jit(solution)/shard_map/update/pallas_call | solution.py:290
  (28 shorter events, 0.3 us)
Async XLA Ops:
  7.2 113.4 %all-gather.3.cloned.1.call-start = ((), (), s32[]{:S(2)}) async-start(), calls=%async_computation | async-start | bytes 4325376 | tf_op jit(solution)/shard_map/all_gather | solution.py:390
  12.9 16.0 %copy-start.1 = (s32[2]{0:T(128)S(1)}, s32[2]{0:T(128)}, u32[]{:S(2)}) copy-start(s32[2]{0:T(128)} %param.11) | copy-start | bytes 28
  13.0 4.0 %collective-permute-start.18 = (f32[256,128]{1,0:T(8,128)S(1)}, f32[256,128]{1,0:T(8,128)S(1)}, u32[]{:S(2)}, u32[]{:S(2)}) collective-permute-start(f32[256,128]{1,0:T(8,128)S(1)} %get-tuple-element.134), channel_id=1, source_target_pairs={{224,32},{225,33},{226,34},{227,35},{228,36},{229,37},{230,38},{23... | collective-permute-start | bytes 393224 | tf_op jit(solution)/shard_map/cond/branch_2_fun/ppermute | solution.py:347
  13.7 4.1 %collective-permute-start.16 = (f32[256,128]{1,0:T(8,128)S(1)}, f32[256,128]{1,0:T(8,128)S(1)}, u32[]{:S(2)}, u32[]{:S(2)}) collective-permute-start(f32[256,128]{1,0:T(8,128)S(1)} %get-tuple-element.135), channel_id=1, source_target_pairs={{224,96},{225,97},{226,98},{227,99},{228,100},{229,101},{230,102},... | collective-permute-start | bytes 393224 | tf_op jit(solution)/shard_map/cond/branch_2_fun/ppermute | solution.py:347
  14.4 3.4 %collective-permute-start.15 = (f32[256,128]{1,0:T(8,128)S(1)}, f32[256,128]{1,0:T(8,128)S(1)}, u32[]{:S(2)}, u32[]{:S(2)}) collective-permute-start(f32[256,128]{1,0:T(8,128)S(1)} %get-tuple-element.136), channel_id=1, source_target_pairs={{224,160},{225,161},{226,162},{227,163},{228,164},{229,165},{230,1... | collective-permute-start | bytes 393224 | tf_op jit(solution)/shard_map/cond/branch_2_fun/ppermute | solution.py:347
  15.1 7.5 %collective-permute-start.17 = (f32[256,128]{1,0:T(8,128)S(1)}, f32[256,128]{1,0:T(8,128)S(1)}, u32[]{:S(2)}, u32[]{:S(2)}) collective-permute-start(f32[256,128]{1,0:T(8,128)S(1)} %get-tuple-element.137), channel_id=1, source_target_pairs={{64,0},{65,1},{66,2},{67,3},{68,4},{69,5},{70,6},{71,7},{72,8},{73... | collective-permute-start | bytes 393224 | tf_op jit(solution)/shard_map/cond/branch_2_fun/ppermute | solution.py:353
  16.4 6.2 %collective-permute-start.14 = (f32[256,128]{1,0:T(8,128)S(1)}, f32[256,128]{1,0:T(8,128)S(1)}, u32[]{:S(2)}, u32[]{:S(2)}) collective-permute-start(f32[256,128]{1,0:T(8,128)S(1)} %get-tuple-element.138), channel_id=1, source_target_pairs={{64,128},{65,129},{66,130},{67,131},{68,132},{69,133},{70,134},{71... | collective-permute-start | bytes 393224 | tf_op jit(solution)/shard_map/cond/branch_2_fun/ppermute | solution.py:353
  17.1 5.5 %collective-permute-start.13 = (f32[256,128]{1,0:T(8,128)S(1)}, f32[256,128]{1,0:T(8,128)S(1)}, u32[]{:S(2)}, u32[]{:S(2)}) collective-permute-start(f32[256,128]{1,0:T(8,128)S(1)} %get-tuple-element.139), channel_id=1, source_target_pairs={{64,192},{65,193},{66,194},{67,195},{68,196},{69,197},{70,198},{71... | collective-permute-start | bytes 393224 | tf_op jit(solution)/shard_map/cond/branch_2_fun/ppermute | solution.py:353
  22.6 39.6 %collective-permute-start.52 = (f32[256,128]{1,0:T(8,128)S(1)}, f32[256,128]{1,0:T(8,128)S(1)}, u32[]{:S(2)}, u32[]{:S(2)}) collective-permute-start(f32[256,128]{1,0:T(8,128)S(1)} %get-tuple-element.179.piece_ref), channel_id=1, source_target_pairs={{0,0},{1,32},{2,64},{3,96},{4,128},{5,160},{6,192},{7,224},{8,8},{... | collective-permute-start | bytes 393224 | tf_op jit(solution)/shard_map/ppermute | solution.py:329
  29.6 1.4 %collective-permute-start.53 = (f32[64,512]{1,0:T(8,128)S(1)}, f32[64,512]{1,0:T(8,128)S(1)}, u32[]{:S(2)}, u32[]{:S(2)}) collective-permute-start(f32[64,512]{1,0:T(8,128)S(1)} %pick.1), channel_id=1, source_target_pairs={{0,1},{1,0},{2,3},{3,2},{4,5},{5,4},{6,7},{7,6},{8,9},{9,8},{10,11... | collective-permute-start | bytes 393224 | tf_op jit(solution)/shard_map/ppermute | solution.py:329
  31.1 4.0 %collective-permute-start.56 = (f32[32,512]{1,0:T(8,128)S(1)}, f32[32,512]{1,0:T(8,128)S(1)}, u32[]{:S(2)}, u32[]{:S(2)}) collective-permute-start(f32[32,512]{1,0:T(8,128)S(1)} %dynamic-slice_select_fusion), channel_id=1, source_target_pairs={{0,8},{1,9},{2,10},{3,11},{4,12},{5,13},{6,14},{7,15},{8,0},{9,1},... | collective-permute-start | bytes 196616 | tf_op jit(solution)/shard_map/ppermute | solution.py:329
  32.3 5.9 %collective-permute-start.55 = (f32[32,512]{1,0:T(8,128)S(1)}, f32[32,512]{1,0:T(8,128)S(1)}, u32[]{:S(2)}, u32[]{:S(2)}) collective-permute-start(f32[32,512]{1,0:T(8,128)S(1)} %dynamic-slice_select_fusion), channel_id=1, source_target_pairs={{0,16},{1,17},{2,18},{3,19},{4,20},{5,21},{6,22},{7,23},{8,24},{9,... | collective-permute-start | bytes 196616 | tf_op jit(solution)/shard_map/ppermute | solution.py:329
  34.8 4.5 %collective-permute-start.54 = (f32[32,512]{1,0:T(8,128)S(1)}, f32[32,512]{1,0:T(8,128)S(1)}, u32[]{:S(2)}, u32[]{:S(2)}) collective-permute-start(f32[32,512]{1,0:T(8,128)S(1)} %dynamic-slice_select_fusion), channel_id=1, source_target_pairs={{0,24},{1,25},{2,26},{3,27},{4,28},{5,29},{6,30},{7,31},{8,16},{9,... | collective-permute-start | bytes 196616 | tf_op jit(solution)/shard_map/ppermute | solution.py:329
  39.3 17.8 %collective-permute-start.60 = (f32[32,512]{1,0:T(8,128)S(1)}, f32[32,512]{1,0:T(8,128)S(1)}, u32[]{:S(2)}, u32[]{:S(2)}) collective-permute-start(f32[32,512]{1,0:T(8,128)S(1)} %select_select_fusion.9), channel_id=1, source_target_pairs={{0,2},{1,3},{2,0},{3,1},{4,6},{5,7},{6,4},{7,5},{8,10},{9,11},{10,... | collective-permute-start | bytes 196616 | tf_op jit(solution)/shard_map/ppermute | solution.py:329
  49.4 7.7 %collective-permute-start.59 = (f32[32,512]{1,0:T(8,128)S(1)}, f32[32,512]{1,0:T(8,128)S(1)}, u32[]{:S(2)}, u32[]{:S(2)}) collective-permute-start(f32[32,512]{1,0:T(8,128)S(1)} %select_select_fusion.9), channel_id=1, source_target_pairs={{0,4},{1,5},{2,6},{3,7},{4,0},{5,1},{6,2},{7,3},{8,12},{9,13},{10,... | collective-permute-start | bytes 196616 | tf_op jit(solution)/shard_map/ppermute | solution.py:329
  54.1 4.9 %collective-permute-start.58 = (f32[32,512]{1,0:T(8,128)S(1)}, f32[32,512]{1,0:T(8,128)S(1)}, u32[]{:S(2)}, u32[]{:S(2)}) collective-permute-start(f32[32,512]{1,0:T(8,128)S(1)} %select_select_fusion.9), channel_id=1, source_target_pairs={{0,6},{1,7},{2,4},{3,5},{4,2},{5,3},{6,0},{7,1},{8,14},{9,15},{10,... | collective-permute-start | bytes 196616 | tf_op jit(solution)/shard_map/ppermute | solution.py:329
  54.3 7.8 %collective-permute-start.57 = (f32[1,256,128]{2,1,0:T(8,128)S(1)}, f32[1,256,128]{2,1,0:T(8,128)S(1)}, u32[]{:S(2)}, u32[]{:S(2)}) collective-permute-start(f32[1,256,128]{2,1,0:T(8,128)S(1)} %bitcast.30), channel_id=1, source_target_pairs={{0,128},{1,129},{2,130},{3,131},{4,132},{5,133},{6,134},{7,135},{8... | collective-permute-start | bytes 393224 | tf_op jit(solution)/shard_map/ppermute | solution.py:329
  62.2 0.7 copy-start
  62.9 7.1 %collective-permute-start.61 = (f32[1,32,512]{2,1,0:T(8,128)S(1)}, f32[1,32,512]{2,1,0:T(8,128)S(1)}, u32[]{:S(2)}, u32[]{:S(2)}) collective-permute-start(f32[1,32,512]{2,1,0:T(8,128)S(1)} %bitcast.32), channel_id=1, source_target_pairs={{0,128},{1,129},{2,130},{3,131},{4,132},{5,133},{6,134},{7,135},{8... | collective-permute-start | bytes 196616 | tf_op jit(solution)/shard_map/ppermute | solution.py:329
  70.0 8.0 %collective-permute-start.62 = (f32[2,32,512]{2,1,0:T(8,128)S(1)}, f32[2,32,512]{2,1,0:T(8,128)S(1)}, u32[]{:S(2)}, u32[]{:S(2)}) collective-permute-start(f32[2,32,512]{2,1,0:T(8,128)S(1)} %pad_maximum_fusion.3), channel_id=1, source_target_pairs={{0,64},{1,65},{2,66},{3,67},{4,68},{5,69},{6,70},{7,71},{8,72},{9,... | collective-permute-start | bytes 393224 | tf_op jit(solution)/shard_map/ppermute | solution.py:329
  78.0 7.0 %collective-permute-start.63 = (f32[4,32,512]{2,1,0:T(8,128)S(1)}, f32[4,32,512]{2,1,0:T(8,128)S(1)}, u32[]{:S(2)}, u32[]{:S(2)}) collective-permute-start(f32[4,32,512]{2,1,0:T(8,128)S(1)} %pad_maximum_fusion.2), channel_id=1, source_target_pairs={{0,32},{1,33},{2,34},{3,35},{4,36},{5,37},{6,38},{7,39},{8,40},{9,... | collective-permute-start | bytes 786440 | tf_op jit(solution)/shard_map/ppermute | solution.py:329
  85.1 8.2 %collective-permute-start.64 = (f32[8,32,512]{2,1,0:T(8,128)S(1)}, f32[8,32,512]{2,1,0:T(8,128)S(1)}, u32[]{:S(2)}, u32[]{:S(2)}) collective-permute-start(f32[8,32,512]{2,1,0:T(8,128)S(1)} %pad_maximum_fusion.own_ref), channel_id=1, source_target_pairs={{0,1},{1,0},{2,3},{3,2},{4,5},{5,4},{6,7},{7,6},{8,9},{9,8},{10,11... | collective-permute-start | bytes 1572872 | tf_op jit(solution)/shard_map/ppermute | solution.py:329
  90.5 15.2 %collective-permute-start.65 = (f32[2,256,128]{2,1,0:T(8,128)S(1)}, f32[2,256,128]{2,1,0:T(8,128)S(1)}, u32[]{:S(2)}, u32[]{:S(2)}) collective-permute-start(f32[2,256,128]{2,1,0:T(8,128)S(1)} %pad_maximum_fusion.1), channel_id=1, source_target_pairs={{0,64},{1,65},{2,66},{3,67},{4,68},{5,69},{6,70},{7,71},{8,72},{9,... | collective-permute-start | bytes 786440 | tf_op jit(solution)/shard_map/ppermute | solution.py:329
  105.7 13.2 %collective-permute-start.66 = (f32[4,256,128]{2,1,0:T(8,128)S(1)}, f32[4,256,128]{2,1,0:T(8,128)S(1)}, u32[]{:S(2)}, u32[]{:S(2)}) collective-permute-start(f32[4,256,128]{2,1,0:T(8,128)S(1)} %constant_dynamic-update-slice_fusion.near_ref), channel_id=1, source_target_pairs={{0,32},{1,33},{2,34},{3,35},{4,36},{5,37},{6,38},{7,39},{8,40},{9,... | collective-permute-start | bytes 1572872 | tf_op jit(solution)/shard_map/ppermute | solution.py:329
Sparse Core Ops, SparseCore 0:
  63.0 52.2 all-gather.2
